TPU v7x, 256 devices: a whole 4x4x8 slice. The times are simulated.
256 devices in a mesh: expert: 64 (over y, z, core), dp: 4 (over x).
Axes of the slice: x: 4, y: 4, z: 8, core: 2. Of those that a mesh axis runs over, the one named last changes fastest.
Arguments:
- tokens_in: bfloat16 [65536, 1024], P(('expert', 'dp')), may hold values from -6 to 6
- out_grad: bfloat16 [65536, 1024], P(('expert', 'dp')), may hold values from -4 to 4
- gates: bfloat16 [65536], P(('expert', 'dp')), may hold values from 0.19921875 to 1
- expert_ids: int32 [65536], P(('expert', 'dp')), may hold values from 0 to 31, as said below
- slot_ids: int32 [65536], P(('expert', 'dp')), may hold values from 0 to 8
- w_up: bfloat16 [64, 1024, 1024], P('expert'), may hold values from -0.1875 to 0.1875
- w_down: bfloat16 [64, 1024, 1024], P('expert'), may hold values from -0.125 to 0.125
Outputs:
- in_grad: bfloat16 [65536, 1024], P(('expert', 'dp'))
- gate_grad: bfloat16 [65536], P(('expert', 'dp'))
- up_grad: bfloat16 [64, 1024, 1024], P('expert', 'dp')
- down_grad: bfloat16 [64, 1024, 1024], P('expert', 'dp')
Inputs may be any that keep to these rules, and one draw needn't show every extreme that they name: `expert_ids`: the tokens of one device (aligned blocks of 256) take distinct pairs of expert and slot; no expert receives more than 9 tokens of one device, and one expert receives exactly 9 from every device.
All inputs are finite; a program needn't handle non-finite values.
Results may differ from a plain program's by a relative error of at most 0.015.
Values may be sent and summed in bfloat16 or wider, within the bound.
No kernel may reach another device: no remote copies, remote signals or barrier semaphores. Data moves between devices by JAX's collectives and lax.ppermute only.
A program may use at most 64 MiB of HBM per device.

v0:
```python
import jax
import jax.numpy as jnp
from jax import lax
from jax.sharding import PartitionSpec as P


def gelu_parts(hidden):
    cdf = 0.5 * (1.0 + lax.erf(hidden * 0.7071067811865476))
    pdf = jnp.exp(-0.5 * hidden * hidden) * 0.3989422804014327
    return (hidden * cdf, cdf + hidden * pdf)


def packed(values, place, total):
    return jnp.zeros((total,) + values.shape[1:], values.dtype).at[place].set(values)


def on_device(tokens_in, out_grad, gates, expert_ids, slot_ids, w_up, w_down):
    devices_e = lax.axis_size("expert")
    rows = tokens_in.shape[0]
    width = tokens_in.shape[1]
    groups = devices_e // 2
    capacity = 9 * rows // (8 * groups)
    total = groups * capacity
    place = expert_ids * capacity + slot_ids
    up_w = w_up[0]
    down_w = w_down[0]
    gate_pack = packed(gates, place, total)
    gate_twice = jnp.broadcast_to(
        gate_pack.reshape(groups, 1, capacity), (groups, 2, capacity)
    ).reshape(devices_e * capacity)

    def doubled(values):
        return jnp.broadcast_to(
            values.reshape(groups, 1, capacity, width), (groups, 2, capacity, width)
        ).reshape(devices_e * capacity, width)

    x_slots, g_slots, gate_slots = (
        lax.all_to_all(
            doubled(packed(tokens_in, place, total)),
            "expert",
            split_axis=0,
            concat_axis=0,
            tiled=True,
        ),
        lax.all_to_all(
            doubled(packed(out_grad, place, total)),
            "expert",
            split_axis=0,
            concat_axis=0,
            tiled=True,
        ),
        lax.all_to_all(gate_twice, "expert", split_axis=0, concat_axis=0, tiled=True),
    )
    hidden = jnp.dot(x_slots, up_w, preferred_element_type=jnp.float32)
    value, slope = gelu_parts(hidden)
    expert_act = value.astype(jnp.bfloat16)
    expert_d_slots = (gate_slots.astype(jnp.float32)[:, None] * g_slots.astype(jnp.float32)).astype(
        jnp.bfloat16
    )
    out_part = jnp.dot(expert_act, down_w, preferred_element_type=jnp.float32).astype(jnp.bfloat16)
    gate_part = jnp.sum(g_slots.astype(jnp.float32) * out_part.astype(jnp.float32), axis=-1).astype(
        jnp.bfloat16
    )
    d_act = lax.dot_general(
        expert_d_slots, down_w, (((1,), (1,)), ((), ())), preferred_element_type=jnp.float32
    )
    expert_d_hidden = (d_act * slope).astype(jnp.bfloat16)
    d_part = lax.dot_general(
        expert_d_hidden, up_w, (((1,), (1,)), ((), ())), preferred_element_type=jnp.float32
    ).astype(jnp.bfloat16)
    act, d_slots, d_hidden, d_part, gate_part = (
        expert_act,
        expert_d_slots,
        expert_d_hidden,
        d_part,
        gate_part,
    )
    back_rows, back_gate = (
        lax.all_to_all(d_part, "expert", split_axis=0, concat_axis=0, tiled=True),
        lax.all_to_all(gate_part, "expert", split_axis=0, concat_axis=0, tiled=True),
    )
    row_sum = jnp.sum(
        back_rows.reshape(groups, 2, capacity, width).astype(jnp.float32), axis=1
    ).astype(jnp.bfloat16)
    gate_sum = jnp.sum(back_gate.reshape(groups, 2, capacity).astype(jnp.float32), axis=1).astype(
        jnp.bfloat16
    )
    in_grad = row_sum.reshape(total, width)[place]
    gate_grad = gate_sum.reshape(total)[place]
    piece = x_slots
    up_grad = lax.psum_scatter(
        lax.dot_general(
            piece, d_hidden, (((0,), (0,)), ((), ())), preferred_element_type=jnp.float32
        ).astype(jnp.bfloat16),
        "dp",
        scatter_dimension=0,
        tiled=True,
    )
    piece = act
    down_grad = lax.psum_scatter(
        lax.dot_general(
            piece, d_slots, (((0,), (0,)), ((), ())), preferred_element_type=jnp.float32
        ).astype(jnp.bfloat16),
        "dp",
        scatter_dimension=0,
        tiled=True,
    )
    return (in_grad, gate_grad, up_grad[None], down_grad[None])


def solution(mesh):
    return jax.shard_map(
        on_device,
        mesh=mesh,
        in_specs=(
            P(("expert", "dp"), None),
            P(("expert", "dp"), None),
            P(("expert", "dp")),
            P(("expert", "dp")),
            P(("expert", "dp")),
            P("expert", None, None),
            P("expert", None, None),
        ),
        out_specs=(
            P(("expert", "dp"), None),
            P(("expert", "dp")),
            P("expert", "dp", None),
            P("expert", "dp", None),
        ),
        check_vma=False,
    )
```

profile of v0, /device:TPU:32, one launch (start us, length us, event | category | flops | bytes accessed | tf_op | source)
XLA Modules:
  0.0 262.6 jit_solution(2417283577721368462)
XLA Ops:
  8.0 2.3 scatter_custom_fusion
  11.1 11.8 %all-to-all-start = ((bf16[64,9,1]{1,2,0:T(2,128)(2,1)}), bf16[64,9,1]{1,2,0:T(2,128)(2,1)S(1)}, u32[]{:S(2)}, u32[]{:S(2)}) async-start(bf16[64,9,1]{1,2,0:T(2,128)(2,1)} %copy.12), calls=%async_computation | async-start | bytes 65536 | tf_op jit(solution)/shard_map/all_to_all | solution.py:52
  22.9 3.0 %scatter_custom_fusion.1 = bf16[288,1024]{1,0:T(8,128)(2,1)} fusion(s32[256]{0:T(256)S(1)} %compare_select_fusion, bf16[256,1024]{1,0:T(8,128)(2,1)} %param.8, bf16[]{:T(256)} %constant.10.clone.1), kind=kCustom, calls=%fused_computation.33 | custom fusion | bytes 590336 | tf_op jit(solution)/shard_map/scatter | solution.py:14
  27.2 4.2 %all-to-all-done = bf16[64,9,1]{1,2,0:T(2,128)(2,1)S(1)} async-done(((bf16[64,9,1]{1,2,0:T(2,128)(2,1)}), bf16[64,9,1]{1,2,0:T(2,128)(2,1)S(1)}, u32[]{:S(2)}, u32[]{:S(2)}) %all-to-all-start) | async-done | bytes 1184 | tf_op jit(solution)/shard_map/all_to_all | solution.py:52
  33.0 6.3 %all-to-all-start.1 = ((bf16[64,9,1024]{2,1,0:T(8,128)(2,1)}), bf16[64,9,1024]{2,1,0:T(8,128)(2,1)}, u32[]{:S(2)}, u32[]{:S(2)}) async-start(bf16[64,9,1024]{2,1,0:T(8,128)(2,1)} %bitcast.37), calls=%async_computation.1 | async-start | bytes 4194304 | tf_op jit(solution)/shard_map/all_to_all | solution.py:45
  39.3 3.0 %scatter_custom_fusion.2 = bf16[288,1024]{1,0:T(8,128)(2,1)} fusion(s32[256]{0:T(256)S(1)} %compare_select_fusion, bf16[256,1024]{1,0:T(8,128)(2,1)} %param.7, bf16[]{:T(256)} %constant.10.clone.1), kind=kCustom, calls=%fused_computation.31 | custom fusion | bytes 590336 | tf_op jit(solution)/shard_map/scatter | solution.py:14
  43.6 45.4 %all-to-all-done.1 = bf16[64,9,1024]{2,1,0:T(8,128)(2,1)} async-done(((bf16[64,9,1024]{2,1,0:T(8,128)(2,1)}), bf16[64,9,1024]{2,1,0:T(8,128)(2,1)}, u32[]{:S(2)}, u32[]{:S(2)}) %all-to-all-start.1) | async-done | bytes 1179680 | tf_op jit(solution)/shard_map/all_to_all | solution.py:45
  90.6 7.6 %all-to-all-start.2 = ((bf16[64,9,1024]{2,1,0:T(8,128)(2,1)}), bf16[64,9,1024]{2,1,0:T(8,128)(2,1)}, u32[]{:S(2)}, u32[]{:S(2)}) async-start(bf16[64,9,1024]{2,1,0:T(8,128)(2,1)} %bitcast.36), calls=%async_computation.2 | async-start | bytes 4194304 | tf_op jit(solution)/shard_map/all_to_all | solution.py:38
  98.5 3.3 %multiply_convert_fusion = bf16[64,9,1024]{2,1,0:T(8,128)(2,1)} fusion(f32[64,9]{1,0:T(8,128)S(1)} %bitcast.38, bf16[64,9,1024]{2,1,0:T(8,128)(2,1)} %all-to-all-done.1), kind=kLoop, calls=%fused_computation.5 | loop fusion | flops 1769472 | bytes 2361600 | tf_op jit(solution)/shard_map/convert_element_type | solution.py:57
  101.8 2.5 convert_element_type.76
  104.4 43.5 %all-to-all-done.2 = bf16[64,9,1024]{2,1,0:T(8,128)(2,1)} async-done(((bf16[64,9,1024]{2,1,0:T(8,128)(2,1)}), bf16[64,9,1024]{2,1,0:T(8,128)(2,1)}, u32[]{:S(2)}, u32[]{:S(2)}) %all-to-all-start.2) | async-done | bytes 1179680 | tf_op jit(solution)/shard_map/all_to_all | solution.py:38
  147.9 3.6 %all_to_all.36 = bf16[576,1024]{1,0:T(8,128)(2,1)} reshape(bf16[64,9,1024]{2,1,0:T(8,128)(2,1)} %all-to-all-done.2) | data formatting | bytes 2359296 | tf_op jit(solution)/shard_map/all_to_all | solution.py:38
  151.5 4.1 %multiply_convert_fusion.2 = (bf16[576,1024]{1,0:T(8,128)(2,1)}, f32[576,1024]{1,0:T(8,128)S(1)}) fusion(bf16[576,1024]{1,0:T(8,128)(2,1)} %all_to_all.36, bf16[1,1024,1024]{2,1,0:T(8,128)(2,1)S(1)} %copy-done), kind=kOutput, calls=%fused_computation.15 | convolution fusion | flops 1210908672 | bytes 6815744 | tf_op jit(solution)/shard_map/dot_general | solution.py:54
  158.8 3.2 %convolution_convert_fusion.1 = bf16[1024,1024]{1,0:T(8,128)(2,1)} fusion(bf16[576,1024]{1,0:T(8,128)(2,1)S(1)} %copy-done.1, bf16[576,1024]{1,0:T(8,128)(2,1)S(1)} %fusion.5), kind=kOutput, calls=%fused_computation.27 | convolution fusion | flops 1209008128 | bytes 4456448 | tf_op jit(solution)/shard_map/dot_general | solution.py:92
  162.3 3.7 %reshape.78 = f32[576,1024]{1,0:T(8,128)} reshape(bf16[64,9,1024]{2,1,0:T(8,128)(2,1)} %all-to-all-done.1) | data formatting | bytes 3538944 | tf_op jit(solution)/shard_map/convert_element_type | solution.py:57
  166.0 5.2 %convolution_convert_fusion = bf16[1024,1024]{1,0:T(8,128)(2,1)} fusion(bf16[576,1024]{1,0:T(8,128)(2,1)} %get-tuple-element.4, f32[576,1024]{1,0:T(8,128)} %reshape.78, f32[576]{0:T(1024)S(1)} %reshape.79), kind=kOutput, calls=%fused_computation.26 | convolution fusion | flops 1210187776 | bytes 5638400 | tf_op jit(solution)/shard_map/dot_general | solution.py:101
  172.6 3.8 %multiply_reduce_fusion = bf16[576]{0:T(1024)(128)(2,1)S(1)} fusion(f32[576,1024]{1,0:T(8,128)} %reshape.78, bf16[576,1024]{1,0:T(8,128)(2,1)S(1)} %copy-done.3, bf16[1,1024,1024]{2,1,0:T(8,128)(2,1)} %param.13), kind=kOutput, calls=%fused_computation.14 | convolution fusion | flops 1210318336 | bytes 5637248 | tf_op jit(solution)/shard_map/dot_general | solution.py:60
  177.2 7.3 %all-to-all-start.4 = ((bf16[64,9,1]{1,2,0:T(2,128)(2,1)}), bf16[64,9,1]{1,2,0:T(2,128)(2,1)S(1)}, u32[]{:S(2)}, u32[]{:S(2)}) async-start(bf16[64,9,1]{1,2,0:T(2,128)(2,1)} %convert_element_type.94), calls=%async_computation.4 | async-start | bytes 65536 | tf_op jit(solution)/shard_map/all_to_all | solution.py:80
  184.5 2.7 %fusion.17 = bf16[576,1024]{1,0:T(8,128)(2,1)S(1)} fusion(bf16[576,1024]{1,0:T(8,128)(2,1)} %copy-done.4, bf16[1,1024,1024]{2,1,0:T(8,128)(2,1)S(1)} %copy-done), kind=kOutput, calls=%fused_computation.29 | convolution fusion | flops 1208549376 | bytes 4456448 | tf_op jit(solution)/shard_map/dot_general | solution.py:68
  188.8 4.2 %all-to-all-done.4 = bf16[64,9,1]{1,2,0:T(2,128)(2,1)S(1)} async-done(((bf16[64,9,1]{1,2,0:T(2,128)(2,1)}), bf16[64,9,1]{1,2,0:T(2,128)(2,1)S(1)}, u32[]{:S(2)}, u32[]{:S(2)}) %all-to-all-start.4) | async-done | bytes 1184 | tf_op jit(solution)/shard_map/all_to_all | solution.py:80
  193.0 6.3 %all-to-all-start.3 = ((bf16[64,9,1024]{2,1,0:T(8,128)(2,1)}), bf16[64,9,1024]{2,1,0:T(8,128)(2,1)}, u32[]{:S(2)}, u32[]{:S(2)}) async-start(bf16[64,9,1024]{2,1,0:T(8,128)(2,1)} %all_to_all.37), calls=%async_computation.3 | async-start | bytes 4194304 | tf_op jit(solution)/shard_map/all_to_all | solution.py:79
  199.5 2.4 gather_fusion.1
  202.0 47.0 %all-to-all-done.3 = bf16[64,9,1024]{2,1,0:T(8,128)(2,1)} async-done(((bf16[64,9,1024]{2,1,0:T(8,128)(2,1)}), bf16[64,9,1024]{2,1,0:T(8,128)(2,1)}, u32[]{:S(2)}, u32[]{:S(2)}) %all-to-all-start.3) | async-done | bytes 1179680 | tf_op jit(solution)/shard_map/all_to_all | solution.py:79
  249.0 3.4 %bitcast_reduce_fusion = bf16[32,9,1024]{2,1,0:T(8,128)(2,1)} fusion(bf16[64,9,1024]{2,1,0:T(8,128)(2,1)} %all-to-all-done.3), kind=kLoop, calls=%fused_computation.17 | loop fusion | flops 294912 | bytes 1769472 | tf_op jit(solution)/shard_map/reduce_sum | solution.py:82
  (36 shorter events, 18.6 us)
Async XLA Ops:
  7.2 144.3 %copy-start = (bf16[1,1024,1024]{2,1,0:T(8,128)(2,1)S(1)}, bf16[1,1024,1024]{2,1,0:T(8,128)(2,1)}, u32[]{:S(2)}) copy-start(bf16[1,1024,1024]{2,1,0:T(8,128)(2,1)} %param.12) | copy-start | bytes 6291460
  11.1 20.2 %all-to-all-start = ((bf16[64,9,1]{1,2,0:T(2,128)(2,1)}), bf16[64,9,1]{1,2,0:T(2,128)(2,1)S(1)}, u32[]{:S(2)}, u32[]{:S(2)}) async-start(bf16[64,9,1]{1,2,0:T(2,128)(2,1)} %copy.12), calls=%async_computation | async-start | bytes 65536 | tf_op jit(solution)/shard_map/all_to_all | solution.py:52
  33.0 56.0 %all-to-all-start.1 = ((bf16[64,9,1024]{2,1,0:T(8,128)(2,1)}), bf16[64,9,1024]{2,1,0:T(8,128)(2,1)}, u32[]{:S(2)}, u32[]{:S(2)}) async-start(bf16[64,9,1024]{2,1,0:T(8,128)(2,1)} %bitcast.37), calls=%async_computation.1 | async-start | bytes 4194304 | tf_op jit(solution)/shard_map/all_to_all | solution.py:45
  90.6 57.3 %all-to-all-start.2 = ((bf16[64,9,1024]{2,1,0:T(8,128)(2,1)}), bf16[64,9,1024]{2,1,0:T(8,128)(2,1)}, u32[]{:S(2)}, u32[]{:S(2)}) async-start(bf16[64,9,1024]{2,1,0:T(8,128)(2,1)} %bitcast.36), calls=%async_computation.2 | async-start | bytes 4194304 | tf_op jit(solution)/shard_map/all_to_all | solution.py:38
  98.2 157.6 %reduce-scatter.3.cloned.1.call-start = ((), (), s32[]{:S(2)}) async-start(), calls=%async_computation.7 | async-start | bytes 2621440 | tf_op jit(solution)/shard_map/reduce_scatter | solution.py:91
  151.5 4.1 %copy-start.2 = (bf16[1,1024,1024]{2,1,0:T(8,128)(2,1)S(1)}, bf16[1,1024,1024]{2,1,0:T(8,128)(2,1)}, u32[]{:S(2)}) copy-start(bf16[1,1024,1024]{2,1,0:T(8,128)(2,1)} %param.13) | copy-start | bytes 6291460
  155.6 3.2 %copy-start.1 = (bf16[576,1024]{1,0:T(8,128)(2,1)S(1)}, bf16[576,1024]{1,0:T(8,128)(2,1)}, u32[]{:S(2)}) copy-start(bf16[576,1024]{1,0:T(8,128)(2,1)} %all_to_all.36) | copy-start | bytes 3538948
  157.7 1.0 copy-start.4
  162.0 93.8 %reduce-scatter.5.cloned.1.call-start = ((), (), s32[]{:S(2)}) async-start(), calls=%async_computation.8 | async-start | bytes 2621440 | tf_op jit(solution)/shard_map/reduce_scatter | solution.py:100
  171.2 1.4 copy-start.3
  177.2 15.8 %all-to-all-start.4 = ((bf16[64,9,1]{1,2,0:T(2,128)(2,1)}), bf16[64,9,1]{1,2,0:T(2,128)(2,1)S(1)}, u32[]{:S(2)}, u32[]{:S(2)}) async-start(bf16[64,9,1]{1,2,0:T(2,128)(2,1)} %convert_element_type.94), calls=%async_computation.4 | async-start | bytes 65536 | tf_op jit(solution)/shard_map/all_to_all | solution.py:80
  193.0 56.0 %all-to-all-start.3 = ((bf16[64,9,1024]{2,1,0:T(8,128)(2,1)}), bf16[64,9,1024]{2,1,0:T(8,128)(2,1)}, u32[]{:S(2)}, u32[]{:S(2)}) async-start(bf16[64,9,1024]{2,1,0:T(8,128)(2,1)} %all_to_all.37), calls=%async_computation.3 | async-start | bytes 4194304 | tf_op jit(solution)/shard_map/all_to_all | solution.py:79
Sparse Core Ops, SparseCore 0:
  162.1 30.2 reduce-scatter.2
  195.7 31.9 reduce-scatter.4
where the time goes:
time: 267 us; the launch traced here: 263 us
  waiting for transfers between devices  144 us (54%)
  starting transfers between devices  39.6 us (15%)
  local copies, waits for them, and re-layouts  35.6 us (13%)
  matrix products  21.2 us (8%)
  between operations  14.2 us (5%)
  other arithmetic  7.77 us (3%)
    all_to_all x1, waiting for transfers between devices, on_device(): lax.all_to_all(d_part, 'expert', split_axis=0, concat_axis=0, tiled=True)  47 us
    all_to_all x1, waiting for transfers between devices, on_device(): lax.all_to_all(doubled(packed(out_grad, place, total)), 'expert', split_a...  45.4 us
    all_to_all x1, waiting for transfers between devices, on_device(): lax.all_to_all(doubled(packed(tokens_in, place, total)), 'expert', split_...  43.5 us
    all_to_all x1, starting transfers between devices, on_device(): lax.all_to_all(gate_twice, 'expert', split_axis=0, concat_axis=0, tiled=T...  11.8 us
    scatter x3, local copies, waits for them, and re-layouts, packed(): jnp.zeros((total,) + values.shape[1:], values.dtype).at[place].set(values)  8.26 us
    all_to_all x1, starting transfers between devices, on_device(): lax.all_to_all(doubled(packed(tokens_in, place, total)), 'expert', split_...  7.6 us
    all_to_all x1, starting transfers between devices, on_device(): lax.all_to_all(gate_part, 'expert', split_axis=0, concat_axis=0, tiled=True)  7.28 us
    all_to_all x1, starting transfers between devices, on_device(): lax.all_to_all(d_part, 'expert', split_axis=0, concat_axis=0, tiled=True)  6.34 us
  transfers between devices with their start and end apart: 7, of which 5 were waited for; matrix products, arithmetic and copies ran while one was open for 15% of the time, Pallas kernels for 0%

commit v1 on v0

v1 whole, which is shorter than its diff:
```python
import functools

import jax
import jax.numpy as jnp
from jax import lax
from jax.experimental import pallas as pl
from jax.experimental.pallas import tpu as pltpu
from jax.sharding import Mesh, PartitionSpec as P

BF = jnp.bfloat16
F32 = jnp.float32
VMEM = 56 * 1024 * 1024
LANES = 128


def matmul(a, b, contract):
    return lax.dot_general(a, b, (contract, ((), ())), preferred_element_type=F32)


def slot_row(expert, slot, groups):
    return jnp.where(slot < 8, expert * 8 + slot, 8 * groups + expert)


def to_tiles(get, out_ref, base, groups, turn):
    for j in range(8):
        part = get(0, 8 * groups, j)
        out_ref[:, base + j] = part.reshape(groups, 8, LANES).astype(BF)
        turn[:, j, :] = get(8 * groups, 9 * groups, j)
    out_ref[:, base + 8] = turn[...].astype(BF)


def from_tiles(ref, base, dst_ref, row, groups, turn):
    turn[...] = ref[:, base + 8].astype(F32)
    for j in range(8):
        cols = slice(LANES * j, LANES * (j + 1))
        part = ref[:, base + j].astype(F32).reshape(8 * groups, LANES)
        dst_ref[row : row + 8 * groups, cols] = part.astype(BF)
        dst_ref[row + 8 * groups : row + 9 * groups, cols] = turn[:, j, :].astype(BF)


def pack_kernel(x_ref, g_ref, gate_ref, expert_ref, slot_ref, out_ref, full, turn):
    groups = out_ref.shape[0]
    count = x_ref.shape[0]
    place = slot_row(expert_ref[...], slot_ref[...], groups)
    rows = lax.broadcasted_iota(jnp.int32, (9 * groups, count), 0)
    hit = rows == place
    gate = gate_ref[...].astype(F32)
    for side, (ref, scale) in enumerate(((x_ref, 1.0), (g_ref, gate))):
        pick = jnp.where(hit, scale, 0.0).astype(BF)
        full[...] = matmul(pick, ref[...], ((1,), (0,)))
        to_tiles(
            lambda a, b, j: full[a:b, LANES * j : LANES * (j + 1)],
            out_ref,
            9 * side,
            groups,
            turn,
        )


def weight_parts(lhs_ref, rhs, me, fwd1, bwd1, fwd2, bwd2, own):
    half = own.shape[0] // 2
    size = 2 * half

    def chunk(step):
        at = pl.multiple_of(lax.rem(me + step, 4) * size, size)
        return matmul(lhs_ref[:, pl.ds(at, size)], rhs, ((0,), (0,))).astype(BF)

    far = chunk(2)
    fwd1[:half] = far[:half]
    bwd1[half:] = far[half:]
    right = chunk(1)
    fwd1[half:] = right[half:]
    fwd2[...] = right[:half]
    left = chunk(3)
    bwd1[:half] = left[:half]
    bwd2[...] = left[half:]
    own[...] = chunk(0)


def expert_kernel(
    mine_ref, other_ref, up_ref, down_ref, xs, dh, gate, fwd1, bwd1, fwd2, bwd2, own, ds, act, hid, dact, turn
):
    groups = mine_ref.shape[0]
    rows = 9 * groups
    for part, ref in enumerate((mine_ref, other_ref)):
        from_tiles(ref, 0, xs, part * rows, groups, turn)
        from_tiles(ref, 9, ds, part * rows, groups, turn)
    hid[...] = matmul(xs[...], up_ref[0], ((1,), (0,)))
    dact[...] = matmul(ds[...], down_ref[0], ((1,), (1,)))
    step = 32

    def block(i, carry):
        at = pl.ds(pl.multiple_of(i * step, step), step)
        v = hid[at, :]
        d = dact[at, :]
        cdf = 0.5 * (1.0 + lax.erf(v * 0.7071067811865476))
        pdf = jnp.exp(-0.5 * v * v) * 0.3989422804014327
        a = (v * cdf).astype(BF)
        act[at, :] = a
        dh[at, :] = (d * (cdf + v * pdf)).astype(BF)
        total = jnp.sum(a.astype(F32) * d, axis=1, keepdims=True)
        gate[at, :] = jnp.broadcast_to(total, (step, LANES))
        return carry

    lax.fori_loop(0, 2 * rows // step, block, 0)
    weight_parts(act, ds[...], lax.axis_index("dp"), fwd1, bwd1, fwd2, bwd2, own)


def up_kernel(xs, dh, fwd1, bwd1, fwd2, bwd2, own):
    weight_parts(xs, dh[...], lax.axis_index("dp"), fwd1, bwd1, fwd2, bwd2, own)


def input_kernel(dh, gate, up_ref, mine_ref, other_ref, full, turn):
    groups = mine_ref.shape[0]
    rows = 9 * groups
    full[...] = matmul(dh[...], up_ref[0], ((1,), (1,)))
    lane = lax.broadcasted_iota(jnp.int32, (groups, 8, LANES), 2)
    for part, ref in enumerate((mine_ref, other_ref)):
        at = part * rows
        to_tiles(
            lambda a, b, j: full[at + a : at + b, LANES * j : LANES * (j + 1)], ref, 0, groups, turn
        )
        last = gate[at + 8 * groups : at + rows, :]
        for j in range(8):
            turn[:, j, :] = last
        first = gate[at : at + 8 * groups, :].reshape(groups, 8, LANES)
        ref[:, 9] = jnp.where(lane < 64, first, turn[...]).astype(BF)


def unpack_kernel(back_ref, gate_ref, expert_ref, slot_ref, out_ref, gate_out_ref, rowbuf, turn):
    groups = back_ref.shape[0]
    count = out_ref.shape[0]
    from_tiles(back_ref, 0, rowbuf, 0, groups, turn)
    expert, slot = expert_ref[...], slot_ref[...]
    rows = lax.broadcasted_iota(jnp.int32, (9 * groups, count), 0)
    pick = jnp.where(rows == slot_row(expert, slot, groups), 1.0, 0.0).astype(BF)
    out_ref[...] = matmul(pick, rowbuf[...], ((0,), (0,))).astype(BF)
    gates = back_ref[:, 9].astype(F32).reshape(8 * groups, LANES).astype(BF)
    rows = lax.broadcasted_iota(jnp.int32, (8 * groups, count), 0)
    low = jnp.where(rows == slot_row(expert, slot, groups), 1.0, 0.0).astype(BF)
    high = jnp.where((rows == expert * 8) & (slot == 8), 1.0, 0.0).astype(BF)
    low = matmul(gates, low, ((0,), (0,)))
    high = matmul(gates, high, ((0,), (0,)))
    total = low[0:1, :] + high[64:65, :]
    gate_out_ref[...] = (total / gate_ref[...].astype(F32)).astype(BF)


def call(kernel, out, scratch, *args):
    whole = pl.BlockSpec(memory_space=pltpu.VMEM)
    return pl.pallas_call(
        kernel,
        out_shape=out,
        in_specs=[whole] * len(args),
        out_specs=jax.tree.map(lambda _: whole, out),
        scratch_shapes=scratch,
        compiler_params=pltpu.CompilerParams(vmem_limit_bytes=VMEM),
    )(*args)


def shape(*dims, dtype=BF):
    return jax.ShapeDtypeStruct(dims, dtype)


def scattered(parts):
    fwd1, bwd1, fwd2, bwd2, own = parts
    half = fwd2.shape[0]
    ahead = [(i, (i + 1) % 4) for i in range(4)]
    behind = [(i, (i + 3) % 4) for i in range(4)]
    left = lax.ppermute(fwd1, "dp", ahead)
    right = lax.ppermute(bwd1, "dp", behind)
    fwd2 = (fwd2.astype(F32) + left[:half].astype(F32)).astype(BF)
    bwd2 = (bwd2.astype(F32) + right[half:].astype(F32)).astype(BF)
    left2 = lax.ppermute(fwd2, "dp", ahead)
    right2 = lax.ppermute(bwd2, "dp", behind)
    wide = own.astype(F32)
    low = wide[:half] + right[:half].astype(F32) + left2.astype(F32)
    high = wide[half:] + left[half:].astype(F32) + right2.astype(F32)
    return jnp.concatenate([low, high], axis=0).astype(BF)


def on_device(tokens_in, out_grad, gates, expert_ids, slot_ids, w_up, w_down):
    groups = lax.axis_size("chip")
    count, width = tokens_in.shape
    hidden = w_up.shape[2]
    rows = 9 * groups
    expert_ids = expert_ids.reshape(1, count)
    slot_ids = slot_ids.reshape(1, count)
    gates = gates.reshape(1, count)
    turn = pltpu.VMEM((groups, 8, LANES), F32)
    swap = [(0, 1), (1, 0)]
    sent = call(
        pack_kernel,
        shape(groups, 18, 8, LANES),
        [pltpu.VMEM((rows, width), F32), turn],
        tokens_in,
        out_grad,
        gates,
        expert_ids,
        slot_ids,
    )
    mine = lax.all_to_all(sent, "chip", split_axis=0, concat_axis=0, tiled=True)
    other = lax.ppermute(mine, "core", swap)

    def parts(length, columns):
        quarter = length // 4
        return (
            shape(quarter, columns),
            shape(quarter, columns),
            shape(quarter // 2, columns),
            shape(quarter // 2, columns),
            shape(quarter, columns),
        )

    xs, dh, gate, *down = call(
        expert_kernel,
        (shape(2 * rows, width), shape(2 * rows, hidden), shape(2 * rows, LANES, dtype=F32))
        + parts(hidden, width),
        [
            pltpu.VMEM((2 * rows, width), BF),
            pltpu.VMEM((2 * rows, hidden), BF),
            pltpu.VMEM((2 * rows, hidden), F32),
            pltpu.VMEM((2 * rows, hidden), F32),
            turn,
        ],
        mine,
        other,
        w_up,
        w_down,
    )
    up = call(up_kernel, parts(width, hidden), [], xs, dh)
    keep, give = call(
        input_kernel,
        (shape(groups, 10, 8, LANES), shape(groups, 10, 8, LANES)),
        [pltpu.VMEM((2 * rows, width), F32), turn],
        dh,
        gate,
        w_up,
    )
    got = lax.ppermute(give, "core", swap)
    both = (keep.astype(F32) + got.astype(F32)).astype(BF)
    back = lax.all_to_all(both, "chip", split_axis=0, concat_axis=0, tiled=True)
    down_grad = scattered(down)
    up_grad = scattered(up)
    in_grad, gate_grad = call(
        unpack_kernel,
        (shape(count, width), shape(1, count)),
        [pltpu.VMEM((rows, width), BF), turn],
        back,
        gates,
        expert_ids,
        slot_ids,
    )
    return (in_grad, gate_grad.reshape(count), up_grad[None], down_grad[None])


def solution(mesh):
    chips = mesh.devices.reshape(mesh.shape["expert"] // 2, 2, mesh.shape["dp"])
    finer = Mesh(chips, ("chip", "core", "dp"))
    tokens = ("chip", "core", "dp")
    pieces = ("chip", "core")
    return jax.shard_map(
        on_device,
        mesh=finer,
        in_specs=(
            P(tokens, None),
            P(tokens, None),
            P(tokens),
            P(tokens),
            P(tokens),
            P(pieces, None, None),
            P(pieces, None, None),
        ),
        out_specs=(
            P(tokens, None),
            P(tokens),
            P(pieces, "dp", None),
            P(pieces, "dp", None),
        ),
        check_vma=False,
    )
```

time: 267 us -> 114 us (0.43); the launches traced: 263 us -> 114 us
  waiting for transfers between devices: 144 us -> 13.8 us
  blocking collectives: 0 us -> 43.5 us
  local copies, waits for them, and re-layouts: 35.6 us -> 3.11 us
  Pallas kernels: 0 us -> 24.9 us
  starting transfers between devices: 39.6 us -> 16.2 us
  matrix products: 21.2 us -> 0 us
  between operations: 14.2 us -> 0.73 us
  other arithmetic: 7.77 us -> 11.5 us
    all_to_all x5 -> x1, waiting for transfers between devices: 144 us -> 3.47 us  [on_device(): back = lax.all_to_all(both, 'chip', split_axis=0, concat_axis=0, tiled=True)]
    all_to_all x0 -> x1, blocking collectives: none -> 43.5 us  [on_device(): mine = lax.all_to_all(sent, 'chip', split_axis=0, concat_axis=0, tiled=True)]
    all_to_all x5 -> x1, starting transfers between devices: 39.3 us -> 4.75 us  [on_device(): back = lax.all_to_all(both, 'chip', split_axis=0, concat_axis=0, tiled=True)]
    pallas_call x0 -> x5, Pallas kernels: none -> 24.9 us  [call(): pl.pallas_call(kernel, out_shape=out, in_specs=[whole] * len(args), out_s...]
    dot_general x6 -> x0, matrix products: 21.2 us -> none  [the longest x1 5.23 us: on_device(): lax.dot_general(piece, d_slots, (((0,), (0,)), ((), ())), preferred_eleme...]
    ppermute x0 -> x10, starting transfers between devices: none -> 11.4 us  [the longest x2 5.8 us: scattered(): right2 = lax.ppermute(bwd2, 'dp', behind)]
    ppermute x0 -> x10, waiting for transfers between devices: none -> 10.3 us  [the longest x2 5.45 us: scattered(): left2 = lax.ppermute(fwd2, 'dp', ahead)]
    scatter x3 -> x0, local copies, waits for them, and re-layouts: 8.26 us -> none  [packed(): jnp.zeros((total,) + values.shape[1:], values.dtype).at[place].set(values)]
  transfers between devices with their start and end apart: 7 -> 11, of which waited for: 5 -> 6; matrix products, arithmetic and copies ran while one was open for 15% -> 9% of each run, Pallas kernels for 0% -> 8%
where the time goes in v1:
time: 114 us
  blocking collectives  43.5 us (38%)
  Pallas kernels  24.9 us (22%)
  starting transfers between devices  16.2 us (14%)
  waiting for transfers between devices  13.8 us (12%)
  other arithmetic  11.5 us (10%)
  local copies, waits for them, and re-layouts  3.11 us (3%)
    all_to_all x1, blocking collectives, on_device(): mine = lax.all_to_all(sent, 'chip', split_axis=0, concat_axis=0, tiled=True)  43.5 us
    pallas_call x5, Pallas kernels, call(): pl.pallas_call(kernel, out_shape=out, in_specs=[whole] * len(args), out_s...  24.9 us
    ppermute x2, starting transfers between devices, scattered(): right2 = lax.ppermute(bwd2, 'dp', behind)  5.8 us
    ppermute x2, waiting for transfers between devices, scattered(): left2 = lax.ppermute(fwd2, 'dp', ahead)  5.45 us
    all_to_all x1, starting transfers between devices, on_device(): back = lax.all_to_all(both, 'chip', split_axis=0, concat_axis=0, tiled=True)  4.75 us
    concatenate x4, other arithmetic, scattered(): return jnp.concatenate([low, high], axis=0).astype(BF)  4.19 us
    all_to_all x1, waiting for transfers between devices, on_device(): back = lax.all_to_all(both, 'chip', split_axis=0, concat_axis=0, tiled=True)  3.47 us
    ppermute x2, starting transfers between devices, scattered(): right = lax.ppermute(bwd1, 'dp', behind)  3.3 us
  transfers between devices with their start and end apart: 11, of which 6 were waited for; matrix products, arithmetic and copies ran while one was open for 9% of the time, Pallas kernels for 8%

profile of v1, /device:TPU:32, one launch (start us, length us, event | category | flops | bytes accessed | tf_op | source)
XLA Modules:
  0.0 113.6 jit_solution(14221320517278635920)
XLA Ops:
  0.6 1.2 %reshape.82.gate_ref = bf16[1,256]{1,0:T(2,128)(2,1)} reshape(bf16[256]{0:T(256)(128)(2,1)} %param.9) | data formatting | bytes 1024 | tf_op jit(solution)/shard_map/reshape | solution.py:188
  1.8 2.8 %shard_map.102 = bf16[32,18,8,128]{3,2,1,0:T(8,128)(2,1)} custom-call(bf16[256,1024]{1,0:T(8,128)(2,1)} %x_ref.1, bf16[256,1024]{1,0:T(8,128)(2,1)} %g_ref.1, bf16[1,256]{1,0:T(2,128)(2,1)} %reshape.82.gate_ref, s32[1,256]{1,0:T(1,128)} %bitcast.10, s32[1,256]{1,0:T(1,128)} %bitcast.12), custom_call_target="tpu_custom_call" | custom-call | tf_op jit(solution)/shard_map/pallas_call | solution.py:150
  4.6 43.5 %all_to_all.10.mine_ref = bf16[32,18,8,128]{3,2,1,0:T(8,128)(2,1)S(1)} all-to-all(bf16[32,18,8,128]{3,2,1,0:T(8,128)(2,1)} %shard_map.102), channel_id=1, replica_groups=mesh['chip'=32,'core'=2,'dp'=4] {'chip'}, dimensions={0} | all-to-all | bytes 2359296 | tf_op jit(solution)/shard_map/all_to_all | solution.py:201
  48.1 2.8 %collective-permute-done.other_ref = bf16[32,18,8,128]{3,2,1,0:T(8,128)(2,1)S(1)} collective-permute-done((bf16[32,18,8,128]{3,2,1,0:T(8,128)(2,1)S(1)}, bf16[32,18,8,128]{3,2,1,0:T(8,128)(2,1)S(1)}, u32[]{:S(2)}, u32[]{:S(2)}) %collective-permute-start) | collective-permute-done | bytes 1179680 | tf_op jit(solution)/shard_map/ppermute | solution.py:202
  52.0 10.6 %shard_map.103 = (bf16[576,1024]{1,0:T(8,128)(2,1)}, bf16[576,1024]{1,0:T(8,128)(2,1)}, f32[576,128]{1,0:T(8,128)}, bf16[256,1024]{1,0:T(8,128)(2,1)}, bf16[256,...) custom-call(bf16[32,18,8,128]{3,2,1,0:T(8,128)(2,1)} %copy-done, ...), custom_call_target="tpu_custom_call" | custom-call | tf_op jit(solution)/shard_map/pallas_call | solution.py:150
  62.6 1.5 %collective-permute-start.7 = (bf16[256,1024]{1,0:T(8,128)(2,1)}, bf16[256,1024]{1,0:T(8,128)(2,1)S(1)}, u32[]{:S(2)}, u32[]{:S(2)}) collective-permute-start(bf16[256,1024]{1,0:T(8,128)(2,1)} %get-tuple-element.36), channel_id=1, source_target_pairs={{0,1},{1,2},{2,3},{3,0},{4,5},{5,6},{6,7},{7,4},{8,9},{9,10},{10,1... | collective-permute-start | bytes 1572872 | tf_op jit(solution)/shard_map/ppermute | solution.py:169
  64.1 1.7 %collective-permute-start.6 = (bf16[256,1024]{1,0:T(8,128)(2,1)}, bf16[256,1024]{1,0:T(8,128)(2,1)S(1)}, u32[]{:S(2)}, u32[]{:S(2)}) collective-permute-start(bf16[256,1024]{1,0:T(8,128)(2,1)} %get-tuple-element.34), channel_id=1, source_target_pairs={{0,3},{1,0},{2,1},{3,2},{4,7},{5,4},{6,5},{7,6},{8,11},{9,8},{10,9... | collective-permute-start | bytes 1572872 | tf_op jit(solution)/shard_map/ppermute | solution.py:170
  65.9 4.7 %shard_map.104 = (bf16[32,10,8,128]{3,2,1,0:T(8,128)(2,1)}, bf16[32,10,8,128]{3,2,1,0:T(8,128)(2,1)}) custom-call(bf16[576,1024]{1,0:T(8,128)(2,1)} %get-tuple-element.21.dh, f32[576,128]{1,0:T(8,128)} %get-tuple-element.22.gate, bf16[1,1024,1024]{2,1,0:T(8,128)(2,1)} %up_ref.3), custom_call_target="tpu_custom_call" | custom-call | tf_op jit(solution)/shard_map/pallas_call | solution.py:150
  70.7 4.3 %shard_map.106 = (bf16[256,1024]{1,0:T(8,128)(2,1)}, bf16[256,1024]{1,0:T(8,128)(2,1)}, bf16[128,1024]{1,0:T(8,128)(2,1)}, bf16[128,1024]{1,0:T(8,128)(2,1)}, bf16[256,1024]{1,0:T(8,128)(2,1)}) custom-call(bf16[576,1024]{1,0:T(8,128)(2,1)} %get-tuple-element.27.xs, bf16[576,1024]{1,0:T(8,128)(2,1)} %get-tuple-element.21.dh), custom_call_target="tpu_custom_call" | custom-call | tf_op jit(solution)/shard_map/pallas_call | solution.py:150
  75.0 1.6 %collective-permute-start.2 = (bf16[256,1024]{1,0:T(8,128)(2,1)}, bf16[256,1024]{1,0:T(8,128)(2,1)}, u32[]{:S(2)}, u32[]{:S(2)}) collective-permute-start(bf16[256,1024]{1,0:T(8,128)(2,1)} %get-tuple-element.29), channel_id=1, source_target_pairs={{0,3},{1,0},{2,1},{3,2},{4,7},{5,4},{6,5},{7,6},{8,11},{9,8},{10,9... | collective-permute-start | bytes 1572872 | tf_op jit(solution)/shard_map/ppermute | solution.py:170
  77.0 1.2 %convert_element_type.94 = f32[256,1024]{1,0:T(8,128)S(1)} convert(bf16[256,1024]{1,0:T(8,128)(2,1)} %get-tuple-element.28) | non-fusion elementwise | flops 262144 | bytes 1572864 | tf_op jit(solution)/shard_map/convert_element_type | solution.py:175
  80.2 3.0 %collective-permute-start.9 = (bf16[128,1024]{1,0:T(8,128)(2,1)}, bf16[128,1024]{1,0:T(8,128)(2,1)}, u32[]{:S(2)}, u32[]{:S(2)}) collective-permute-start(bf16[128,1024]{1,0:T(8,128)(2,1)} %add_convert_fusion.1), channel_id=1, source_target_pairs={{0,3},{1,0},{2,1},{3,2},{4,7},{5,4},{6,5},{7,6},{8,11},{9,8},{10,9... | collective-permute-start | bytes 786440 | tf_op jit(solution)/shard_map/ppermute | solution.py:174
  83.1 1.0 add_convert_fusion
  84.2 4.7 %all-to-all-start.1 = ((bf16[32,10,8,128]{3,2,1,0:T(8,128)(2,1)}), bf16[32,10,8,128]{3,2,1,0:T(8,128)(2,1)S(1)}, u32[]{:S(2)}, u32[]{:S(2)}) async-start(bf16[32,10,8,128]{3,2,1,0:T(8,128)(2,1)} %add_convert_fusion), calls=%async_computation.1 | async-start | bytes 1310720 | tf_op jit(solution)/shard_map/all_to_all | solution.py:241
  88.9 1.1 collective-permute-done.2
  90.0 1.1 add_convert_fusion.3
  91.1 2.8 %collective-permute-start.5 = (bf16[128,1024]{1,0:T(8,128)(2,1)S(1)}, bf16[128,1024]{1,0:T(8,128)(2,1)S(1)}, u32[]{:S(2)}, u32[]{:S(2)}) collective-permute-start(bf16[128,1024]{1,0:T(8,128)(2,1)S(1)} %add_convert_fusion.3), channel_id=1, source_target_pairs={{0,3},{1,0},{2,1},{3,2},{4,7},{5,4},{6,5},{7,6},{8,11},{9,8},{10,9... | collective-permute-start | bytes 786440 | tf_op jit(solution)/shard_map/ppermute | solution.py:174
  95.1 2.7 %collective-permute-done.8 = bf16[128,1024]{1,0:T(8,128)(2,1)} collective-permute-done((bf16[128,1024]{1,0:T(8,128)(2,1)}, bf16[128,1024]{1,0:T(8,128)(2,1)}, u32[]{:S(2)}, u32[]{:S(2)}) %collective-permute-start.8) | collective-permute-done | bytes 262176 | tf_op jit(solution)/shard_map/ppermute | solution.py:173
  97.7 1.3 %fusion.10 = (bf16[1,128,1024]{2,1,0:T(8,128)(2,1)S(1)}, bf16[1,128,1024]{2,1,0:T(8,128)(2,1)S(1)}) fusion(bf16[128,1024]{1,0:T(8,128)(2,1)} %collective-permute-done.8, f32[256,1024]{1,0:T(8,128)S(1)} %convert_element_type.105, bf16[256,1024]{1,0:T(8,128)(2,1)S(1)} %copy-done.5, bf16[128,1024]{1,0:T(8,128)(2,1)} %collective-permute-done.9, ...), kind=kLoop, calls=%fused_computation.21 | loop fusion | flops 1310720 | bytes 2621440 | tf_op jit(solution)/shard_map/concatenate | solution.py:178
  100.8 2.8 %collective-permute-done.4 = bf16[128,1024]{1,0:T(8,128)(2,1)S(1)} collective-permute-done((bf16[128,1024]{1,0:T(8,128)(2,1)S(1)}, bf16[128,1024]{1,0:T(8,128)(2,1)S(1)}, u32[]{:S(2)}, u32[]{:S(2)}) %collective-permute-start.4) | collective-permute-done | bytes 262176 | tf_op jit(solution)/shard_map/ppermute | solution.py:173
  103.5 1.3 %fusion.8 = (bf16[1,128,1024]{2,1,0:T(8,128)(2,1)S(1)}, bf16[1,128,1024]{2,1,0:T(8,128)(2,1)S(1)}) fusion(bf16[128,1024]{1,0:T(8,128)(2,1)S(1)} %collective-permute-done.4, f32[256,1024]{1,0:T(8,128)S(1)} %convert_element_type.94, bf16[256,1024]{1,0:T(8,128)(2,1)} %collective-permute-done.2, bf16[128,1024]{1,0:T(8,128)(2,1)S(1)} %collective-permute-done.5, ...), kind=kLoop, calls=%fused_computation.19 | loop fusion | flops 1310720 | bytes 2621440 | tf_op jit(solution)/shard_map/concatenate | solution.py:178
  105.6 3.5 %all-to-all-done.1.back_ref = bf16[32,10,8,128]{3,2,1,0:T(8,128)(2,1)S(1)} async-done(((bf16[32,10,8,128]{3,2,1,0:T(8,128)(2,1)}), bf16[32,10,8,128]{3,2,1,0:T(8,128)(2,1)S(1)}, u32[]{:S(2)}, u32[]{:S(2)}) %all-to-all-start.1) | async-done | bytes 655392 | tf_op jit(solution)/shard_map/all_to_all | solution.py:241
  110.0 2.4 %shard_map.105 = (bf16[256,1024]{1,0:T(8,128)(2,1)}, bf16[1,256]{1,0:T(2,128)(2,1)}) custom-call(bf16[32,10,8,128]{3,2,1,0:T(8,128)(2,1)} %copy-done.1, bf16[1,256]{1,0:T(2,128)(2,1)} %reshape.82.gate_ref, s32[1,256]{1,0:T(1,128)} %bitcast.11, s32[1,256]{1,0:T(1,128)} %bitcast.13), custom_call_target="tpu_custom_call" | custom-call | tf_op jit(solution)/shard_map/pallas_call | solution.py:150
  112.4 1.2 %reduce = bf16[256]{0:T(256)(128)(2,1)} reduce(bf16[1,256]{1,0:T(2,128)(2,1)} %get-tuple-element.26, bf16[]{:T(256)} %constant.2), dimensions={0}, to_apply=%get-tuple-element.26.reduce_sub_computation | reduce | bytes 1026 | tf_op jit(solution)/shard_map/pallas_call | solution.py:150
  (37 shorter events, 8.1 us)
Async XLA Ops:
  48.1 2.9 %copy-start = (bf16[32,18,8,128]{3,2,1,0:T(8,128)(2,1)}, bf16[32,18,8,128]{3,2,1,0:T(8,128)(2,1)S(1)}, u32[]{:S(2)}) copy-start(bf16[32,18,8,128]{3,2,1,0:T(8,128)(2,1)S(1)} %all_to_all.10.mine_ref) | copy-start | bytes 3538948
  48.1 2.8 %collective-permute-start = (bf16[32,18,8,128]{3,2,1,0:T(8,128)(2,1)S(1)}, bf16[32,18,8,128]{3,2,1,0:T(8,128)(2,1)S(1)}, u32[]{:S(2)}, u32[]{:S(2)}) collective-permute-start(bf16[32,18,8,128]{3,2,1,0:T(8,128)(2,1)S(1)} %all_to_all.10.mine_ref), channel_id=1, source_target_pairs={{0,4},{4,0},{1,5},{5,1},{2,6},{6,2},{3,7},{7,3},{8,12},{12,8},{9,1... | collective-permute-start | bytes 3538952 | tf_op jit(solution)/shard_map/ppermute | solution.py:202
  51.0 1.0 copy-start.2
  62.6 15.6 %collective-permute-start.7 = (bf16[256,1024]{1,0:T(8,128)(2,1)}, bf16[256,1024]{1,0:T(8,128)(2,1)S(1)}, u32[]{:S(2)}, u32[]{:S(2)}) collective-permute-start(bf16[256,1024]{1,0:T(8,128)(2,1)} %get-tuple-element.36), channel_id=1, source_target_pairs={{0,1},{1,2},{2,3},{3,0},{4,5},{5,6},{6,7},{7,4},{8,9},{9,10},{10,1... | collective-permute-start | bytes 1572872 | tf_op jit(solution)/shard_map/ppermute | solution.py:169
  64.1 15.2 %collective-permute-start.6 = (bf16[256,1024]{1,0:T(8,128)(2,1)}, bf16[256,1024]{1,0:T(8,128)(2,1)S(1)}, u32[]{:S(2)}, u32[]{:S(2)}) collective-permute-start(bf16[256,1024]{1,0:T(8,128)(2,1)} %get-tuple-element.34), channel_id=1, source_target_pairs={{0,3},{1,0},{2,1},{3,2},{4,7},{5,4},{6,5},{7,6},{8,11},{9,8},{10,9... | collective-permute-start | bytes 1572872 | tf_op jit(solution)/shard_map/ppermute | solution.py:170
  65.9 4.7 %copy-start.6 = (bf16[256,1024]{1,0:T(8,128)(2,1)S(1)}, bf16[256,1024]{1,0:T(8,128)(2,1)}, u32[]{:S(2)}) copy-start(bf16[256,1024]{1,0:T(8,128)(2,1)} %get-tuple-element.33) | copy-start | bytes 1572868
  70.6 12.6 %collective-permute-start.1 = (bf16[32,10,8,128]{3,2,1,0:T(8,128)(2,1)}, bf16[32,10,8,128]{3,2,1,0:T(8,128)(2,1)S(1)}, u32[]{:S(2)}, u32[]{:S(2)}) collective-permute-start(bf16[32,10,8,128]{3,2,1,0:T(8,128)(2,1)} %get-tuple-element.24), channel_id=1, source_target_pairs={{0,4},{4,0},{1,5},{5,1},{2,6},{6,2},{3,7},{7,3},{8,12},{12,8},{9,1... | collective-permute-start | bytes 1966088 | tf_op jit(solution)/shard_map/ppermute | solution.py:239
  75.0 3.3 %copy-start.9 = (bf16[128,1024]{1,0:T(8,128)(2,1)S(1)}, bf16[128,1024]{1,0:T(8,128)(2,1)}, u32[]{:S(2)}) copy-start(bf16[128,1024]{1,0:T(8,128)(2,1)} %get-tuple-element.35) | copy-start | bytes 786436
  75.0 4.3 %copy-start.8 = (bf16[128,1024]{1,0:T(8,128)(2,1)S(1)}, bf16[128,1024]{1,0:T(8,128)(2,1)}, u32[]{:S(2)}) copy-start(bf16[128,1024]{1,0:T(8,128)(2,1)} %get-tuple-element.37) | copy-start | bytes 786436
  75.0 15.0 %collective-permute-start.2 = (bf16[256,1024]{1,0:T(8,128)(2,1)}, bf16[256,1024]{1,0:T(8,128)(2,1)}, u32[]{:S(2)}, u32[]{:S(2)}) collective-permute-start(bf16[256,1024]{1,0:T(8,128)(2,1)} %get-tuple-element.29), channel_id=1, source_target_pairs={{0,3},{1,0},{2,1},{3,2},{4,7},{5,4},{6,5},{7,6},{8,11},{9,8},{10,9... | collective-permute-start | bytes 1572872 | tf_op jit(solution)/shard_map/ppermute | solution.py:170
  76.5 17.4 %collective-permute-start.3 = (bf16[256,1024]{1,0:T(8,128)(2,1)}, bf16[256,1024]{1,0:T(8,128)(2,1)}, u32[]{:S(2)}, u32[]{:S(2)}) collective-permute-start(bf16[256,1024]{1,0:T(8,128)(2,1)} %get-tuple-element.31), channel_id=1, source_target_pairs={{0,1},{1,2},{2,3},{3,0},{4,5},{5,6},{6,7},{7,4},{8,9},{9,10},{10,1... | collective-permute-start | bytes 1572872 | tf_op jit(solution)/shard_map/ppermute | solution.py:169
  77.0 6.1 %copy-start.3 = (bf16[32,10,8,128]{3,2,1,0:T(8,128)(2,1)S(1)}, bf16[32,10,8,128]{3,2,1,0:T(8,128)(2,1)}, u32[]{:S(2)}) copy-start(bf16[32,10,8,128]{3,2,1,0:T(8,128)(2,1)} %get-tuple-element.23) | copy-start | bytes 1966084
  79.0 18.7 %collective-permute-start.8 = (bf16[128,1024]{1,0:T(8,128)(2,1)}, bf16[128,1024]{1,0:T(8,128)(2,1)}, u32[]{:S(2)}, u32[]{:S(2)}) collective-permute-start(bf16[128,1024]{1,0:T(8,128)(2,1)} %add_convert_fusion.2), channel_id=1, source_target_pairs={{0,1},{1,2},{2,3},{3,0},{4,5},{5,6},{6,7},{7,4},{8,9},{9,10},{10,1... | collective-permute-start | bytes 786440 | tf_op jit(solution)/shard_map/ppermute | solution.py:173
  79.3 4.9 %copy-start.4 = (bf16[256,1024]{1,0:T(8,128)(2,1)}, bf16[256,1024]{1,0:T(8,128)(2,1)S(1)}, u32[]{:S(2)}) copy-start(bf16[256,1024]{1,0:T(8,128)(2,1)S(1)} %collective-permute-done.6) | copy-start | bytes 1572868
  80.2 17.6 %collective-permute-start.9 = (bf16[128,1024]{1,0:T(8,128)(2,1)}, bf16[128,1024]{1,0:T(8,128)(2,1)}, u32[]{:S(2)}, u32[]{:S(2)}) collective-permute-start(bf16[128,1024]{1,0:T(8,128)(2,1)} %add_convert_fusion.1), channel_id=1, source_target_pairs={{0,3},{1,0},{2,1},{3,2},{4,7},{5,4},{6,5},{7,6},{8,11},{9,8},{10,9... | collective-permute-start | bytes 786440 | tf_op jit(solution)/shard_map/ppermute | solution.py:174
  84.2 9.8 %copy-start.7 = (bf16[128,1024]{1,0:T(8,128)(2,1)S(1)}, bf16[128,1024]{1,0:T(8,128)(2,1)}, u32[]{:S(2)}) copy-start(bf16[128,1024]{1,0:T(8,128)(2,1)} %get-tuple-element.30) | copy-start | bytes 786436
  84.2 24.9 %all-to-all-start.1 = ((bf16[32,10,8,128]{3,2,1,0:T(8,128)(2,1)}), bf16[32,10,8,128]{3,2,1,0:T(8,128)(2,1)S(1)}, u32[]{:S(2)}, u32[]{:S(2)}) async-start(bf16[32,10,8,128]{3,2,1,0:T(8,128)(2,1)} %add_convert_fusion), calls=%async_computation.1 | async-start | bytes 1310720 | tf_op jit(solution)/shard_map/all_to_all | solution.py:241
  88.9 8.8 %copy-start.5 = (bf16[256,1024]{1,0:T(8,128)(2,1)S(1)}, bf16[256,1024]{1,0:T(8,128)(2,1)}, u32[]{:S(2)}) copy-start(bf16[256,1024]{1,0:T(8,128)(2,1)} %copy-done.4) | copy-start | bytes 1572868
  91.1 9.6 %collective-permute-start.5 = (bf16[128,1024]{1,0:T(8,128)(2,1)S(1)}, bf16[128,1024]{1,0:T(8,128)(2,1)S(1)}, u32[]{:S(2)}, u32[]{:S(2)}) collective-permute-start(bf16[128,1024]{1,0:T(8,128)(2,1)S(1)} %add_convert_fusion.3), channel_id=1, source_target_pairs={{0,3},{1,0},{2,1},{3,2},{4,7},{5,4},{6,5},{7,6},{8,11},{9,8},{10,9... | collective-permute-start | bytes 786440 | tf_op jit(solution)/shard_map/ppermute | solution.py:174
  95.0 8.6 %collective-permute-start.4 = (bf16[128,1024]{1,0:T(8,128)(2,1)S(1)}, bf16[128,1024]{1,0:T(8,128)(2,1)S(1)}, u32[]{:S(2)}, u32[]{:S(2)}) collective-permute-start(bf16[128,1024]{1,0:T(8,128)(2,1)S(1)} %add_convert_fusion.4), channel_id=1, source_target_pairs={{0,1},{1,2},{2,3},{3,0},{4,5},{5,6},{6,7},{7,4},{8,9},{9,10},{10,1... | collective-permute-start | bytes 786440 | tf_op jit(solution)/shard_map/ppermute | solution.py:173
  109.1 0.9 copy-start.1

commit v2 on v1

v2 whole, which is shorter than its diff:
```python
import functools

import jax
import jax.numpy as jnp
from jax import lax
from jax.experimental import pallas as pl
from jax.experimental.pallas import tpu as pltpu
from jax.sharding import Mesh, PartitionSpec as P

BF = jnp.bfloat16
F32 = jnp.float32
VMEM = 56 * 1024 * 1024
LANES = 128


def matmul(a, b, contract):
    return lax.dot_general(a, b, (contract, ((), ())), preferred_element_type=F32)


def slot_row(expert, slot, groups):
    return jnp.where(slot < 8, expert * 8 + slot, 8 * groups + expert)


def to_tiles(full, row, out_ref, groups, turn):
    last = row + 8 * groups
    for j in range(8):
        cols = slice(LANES * j, LANES * (j + 1))
        out_ref[:, j] = full[row:last, cols].reshape(groups, 8, LANES).astype(BF)
        turn[:, j, :] = full[last : last + groups, cols]
    out_ref[:, 8] = turn[...].astype(BF)


def from_tiles(ref, dst_ref, row, groups, turn):
    last = row + 8 * groups
    turn[...] = ref[:, 8].astype(F32)
    for j in range(8):
        cols = slice(LANES * j, LANES * (j + 1))
        dst_ref[row:last, cols] = ref[:, j].astype(F32).reshape(8 * groups, LANES).astype(BF)
        dst_ref[last : last + groups, cols] = turn[:, j, :].astype(BF)


def pack_x_kernel(x_ref, expert_ref, slot_ref, out_ref, full, turn):
    groups = out_ref.shape[0]
    place = slot_row(expert_ref[...], slot_ref[...], groups)
    hit = lax.broadcasted_iota(jnp.int32, (9 * groups, x_ref.shape[0]), 0) == place
    full[...] = matmul(jnp.where(hit, 1.0, 0.0).astype(BF), x_ref[...], ((1,), (0,)))
    to_tiles(full, 0, out_ref, groups, turn)


def pack_d_kernel(g_ref, gate_ref, expert_ref, slot_ref, out_ref, full, turn):
    groups = out_ref.shape[0]
    place = slot_row(expert_ref[...], slot_ref[...], groups)
    hit = lax.broadcasted_iota(jnp.int32, (9 * groups, g_ref.shape[0]), 0) == place
    scale = jnp.where(hit, gate_ref[...].astype(F32), 0.0).astype(BF)
    full[...] = matmul(scale, g_ref[...], ((1,), (0,)))
    to_tiles(full, 0, out_ref, groups, turn)


def weight_parts(lhs_ref, rhs, me, fwd1, bwd1, fwd2, bwd2, own):
    half = own.shape[0] // 2
    size = 2 * half

    def chunk(step):
        at = pl.multiple_of(lax.rem(me + step, 4) * size, size)
        return matmul(lhs_ref[:, pl.ds(at, size)], rhs, ((0,), (0,))).astype(BF)

    far = chunk(2)
    fwd1[:half] = far[:half]
    bwd1[half:] = far[half:]
    right = chunk(1)
    fwd1[half:] = right[half:]
    fwd2[...] = right[:half]
    left = chunk(3)
    bwd1[:half] = left[:half]
    bwd2[...] = left[half:]
    own[...] = chunk(0)


def hidden_kernel(mine_ref, other_ref, up_ref, xs, act, slope, hid, turn):
    groups = mine_ref.shape[0]
    rows = 9 * groups
    from_tiles(mine_ref, xs, 0, groups, turn)
    from_tiles(other_ref, xs, rows, groups, turn)
    hid[...] = matmul(xs[...], up_ref[0], ((1,), (0,)))
    step = 32

    def block(i, carry):
        at = pl.ds(pl.multiple_of(i * step, step), step)
        v = hid[at, :]
        cdf = 0.5 * (1.0 + lax.erf(v * 0.7071067811865476))
        pdf = jnp.exp(-0.5 * v * v) * 0.3989422804014327
        act[at, :] = (v * cdf).astype(BF)
        slope[at, :] = cdf + v * pdf
        return carry

    lax.fori_loop(0, 2 * rows // step, block, 0)


def backward(ds, down_ref, act, slope, row, dh, gate, dact):
    dact[...] = matmul(ds, down_ref[0], ((1,), (1,)))
    step = 32

    def block(i, carry):
        at = pl.ds(pl.multiple_of(i * step, step), step)
        there = pl.ds(pl.multiple_of(row + i * step, step), step)
        d = dact[at, :]
        dh[at, :] = (d * slope[there, :]).astype(BF)
        total = jnp.sum(act[there, :].astype(F32) * d, axis=1, keepdims=True)
        gate[at, :] = jnp.broadcast_to(total, (step, LANES))
        return carry

    lax.fori_loop(0, dact.shape[0] // step, block, 0)


def own_kernel(raw_ref, down_ref, act, slope, ds, dh, gate, dact, turn):
    from_tiles(raw_ref, ds, 0, raw_ref.shape[0], turn)
    backward(ds[...], down_ref, act, slope, 0, dh, gate, dact)


def down_kernel(own_ref, raw_ref, act, fwd1, bwd1, fwd2, bwd2, own, ds_other, ds, turn):
    rows = own_ref.shape[0]
    from_tiles(raw_ref, ds, rows, raw_ref.shape[0], turn)
    ds[:rows] = own_ref[...]
    ds_other[...] = ds[rows:]
    weight_parts(act, ds[...], lax.axis_index("dp"), fwd1, bwd1, fwd2, bwd2, own)


def to_part(dh, gate, up_ref, out_ref, full, turn):
    groups = out_ref.shape[0]
    full[...] = matmul(dh, up_ref[0], ((1,), (1,)))
    to_tiles(full, 0, out_ref, groups, turn)
    last = gate[8 * groups :, :]
    for j in range(8):
        turn[:, j, :] = last
    lane = lax.broadcasted_iota(jnp.int32, (groups, 8, LANES), 2)
    first = gate[: 8 * groups, :].reshape(groups, 8, LANES)
    out_ref[:, 9] = jnp.where(lane < 64, first, turn[...]).astype(BF)


def other_kernel(ds_ref, down_ref, act, slope, up_ref, dh, out_ref, gate, dact, turn):
    backward(ds_ref[...], down_ref, act, slope, ds_ref.shape[0], dh, gate, dact)
    to_part(dh[...], gate, up_ref, out_ref, dact, turn)


def part_kernel(dh, gate, up_ref, out_ref, full, turn):
    to_part(dh[...], gate, up_ref, out_ref, full, turn)


def up_kernel(xs, dh_own, dh_other, fwd1, bwd1, fwd2, bwd2, own, dh):
    rows = dh_own.shape[0]
    dh[:rows] = dh_own[...]
    dh[rows:] = dh_other[...]
    weight_parts(xs, dh[...], lax.axis_index("dp"), fwd1, bwd1, fwd2, bwd2, own)


def unpack_kernel(back_ref, gate_ref, expert_ref, slot_ref, out_ref, gate_out_ref, rowbuf, turn):
    groups = back_ref.shape[0]
    count = out_ref.shape[0]
    from_tiles(back_ref, rowbuf, 0, groups, turn)
    expert, slot = expert_ref[...], slot_ref[...]
    rows = lax.broadcasted_iota(jnp.int32, (9 * groups, count), 0)
    pick = jnp.where(rows == slot_row(expert, slot, groups), 1.0, 0.0).astype(BF)
    out_ref[...] = matmul(pick, rowbuf[...], ((0,), (0,))).astype(BF)
    gates = back_ref[:, 9].astype(F32).reshape(8 * groups, LANES).astype(BF)
    rows = lax.broadcasted_iota(jnp.int32, (8 * groups, count), 0)
    low = jnp.where(rows == slot_row(expert, slot, groups), 1.0, 0.0).astype(BF)
    high = jnp.where((rows == expert * 8) & (slot == 8), 1.0, 0.0).astype(BF)
    low = matmul(gates, low, ((0,), (0,)))
    high = matmul(gates, high, ((0,), (0,)))
    total = low[0:1, :] + high[64:65, :]
    gate_out_ref[...] = (total / gate_ref[...].astype(F32)).astype(BF)


def call(kernel, out, scratch, *args):
    whole = pl.BlockSpec(memory_space=pltpu.VMEM)
    return pl.pallas_call(
        kernel,
        out_shape=out,
        in_specs=[whole] * len(args),
        out_specs=jax.tree.map(lambda _: whole, out),
        scratch_shapes=scratch,
        compiler_params=pltpu.CompilerParams(vmem_limit_bytes=VMEM),
    )(*args)


def after(value, earlier):
    return lax.optimization_barrier((value, earlier))[0]


def shape(*dims, dtype=BF):
    return jax.ShapeDtypeStruct(dims, dtype)


def scattered(parts):
    fwd1, bwd1, fwd2, bwd2, own = parts
    half = fwd2.shape[0]
    ahead = [(i, (i + 1) % 4) for i in range(4)]
    behind = [(i, (i + 3) % 4) for i in range(4)]
    left = lax.ppermute(fwd1, "dp", ahead)
    right = lax.ppermute(bwd1, "dp", behind)
    fwd2 = (fwd2.astype(F32) + left[:half].astype(F32)).astype(BF)
    bwd2 = (bwd2.astype(F32) + right[half:].astype(F32)).astype(BF)
    left2 = lax.ppermute(fwd2, "dp", ahead)
    right2 = lax.ppermute(bwd2, "dp", behind)
    wide = own.astype(F32)
    low = wide[:half] + right[:half].astype(F32) + left2.astype(F32)
    high = wide[half:] + left[half:].astype(F32) + right2.astype(F32)
    return jnp.concatenate([low, high], axis=0).astype(BF)


def on_device(tokens_in, out_grad, gates, expert_ids, slot_ids, w_up, w_down):
    groups = lax.axis_size("chip")
    count, width = tokens_in.shape
    hidden = w_up.shape[2]
    rows = 9 * groups
    expert_ids = expert_ids.reshape(1, count)
    slot_ids = slot_ids.reshape(1, count)
    gates = gates.reshape(1, count)
    turn = pltpu.VMEM((groups, 8, LANES), F32)
    swap = [(0, 1), (1, 0)]
    blocks = shape(groups, 9, 8, LANES)
    full = pltpu.VMEM((rows, width), F32)

    def exchange(values):
        return lax.all_to_all(values, "chip", split_axis=0, concat_axis=0, tiled=True)

    def parts(length, columns):
        quarter = length // 4
        return (
            shape(quarter, columns),
            shape(quarter, columns),
            shape(quarter // 2, columns),
            shape(quarter // 2, columns),
            shape(quarter, columns),
        )

    x_mine = exchange(call(pack_x_kernel, blocks, [full, turn], tokens_in, expert_ids, slot_ids))
    d_sent = call(pack_d_kernel, blocks, [full, turn], out_grad, gates, expert_ids, slot_ids)
    x_other = lax.ppermute(x_mine, "core", swap)
    d_mine = exchange(d_sent)
    xs, act, slope = call(
        hidden_kernel,
        (shape(2 * rows, width), shape(2 * rows, hidden), shape(2 * rows, hidden, dtype=F32)),
        [pltpu.VMEM((2 * rows, hidden), F32), turn],
        x_mine,
        x_other,
        w_up,
    )
    d_mine = after(d_mine, act)
    d_other = lax.ppermute(d_mine, "core", swap)
    half = (shape(rows, hidden), shape(rows, LANES, dtype=F32))
    back = pltpu.VMEM((rows, hidden), F32)
    ds_own, dh_own, gate_own = call(
        own_kernel, (shape(rows, width),) + half, [back, turn], d_mine, w_down, act, slope
    )
    *down, ds_other = call(
        down_kernel,
        parts(hidden, width) + (shape(rows, width),),
        [pltpu.VMEM((2 * rows, width), BF), turn],
        ds_own,
        d_other,
        act,
    )
    returned = shape(groups, 10, 8, LANES)
    dh_other, give = call(
        other_kernel,
        (shape(rows, hidden), returned),
        [pltpu.VMEM((rows, LANES), F32), back, turn],
        ds_other,
        w_down,
        act,
        slope,
        w_up,
    )
    got = lax.ppermute(give, "core", swap)
    keep = call(part_kernel, returned, [full, turn], dh_own, gate_own, w_up)
    both = (keep.astype(F32) + got.astype(F32)).astype(BF)
    back = exchange(both)
    xs = after(xs, both)
    up = call(
        up_kernel, parts(width, hidden), [pltpu.VMEM((2 * rows, hidden), BF)], xs, dh_own, dh_other
    )
    down_grad = scattered(down)
    up_grad = scattered(up)
    in_grad, gate_grad = call(
        unpack_kernel,
        (shape(count, width), shape(1, count)),
        [pltpu.VMEM((rows, width), BF), turn],
        back,
        gates,
        expert_ids,
        slot_ids,
    )
    return (in_grad, gate_grad.reshape(count), up_grad[None], down_grad[None])


def solution(mesh):
    chips = mesh.devices.reshape(mesh.shape["expert"] // 2, 2, mesh.shape["dp"])
    finer = Mesh(chips, ("chip", "core", "dp"))
    tokens = ("chip", "core", "dp")
    pieces = ("chip", "core")
    return jax.shard_map(
        on_device,
        mesh=finer,
        in_specs=(
            P(tokens, None),
            P(tokens, None),
            P(tokens),
            P(tokens),
            P(tokens),
            P(pieces, None, None),
            P(pieces, None, None),
        ),
        out_specs=(
            P(tokens, None),
            P(tokens),
            P(pieces, "dp", None),
            P(pieces, "dp", None),
        ),
        check_vma=False,
    )
```

time: 114 us -> 128 us (1.12)
  blocking collectives: 43.5 us -> 0 us
  waiting for transfers between devices: 13.8 us -> 38.3 us
  starting transfers between devices: 16.2 us -> 34 us
  Pallas kernels: 24.9 us -> 38.6 us
    all_to_all x1 -> x0, blocking collectives: 43.5 us -> none  [on_device(): mine = lax.all_to_all(sent, 'chip', split_axis=0, concat_axis=0, tiled=True)]
    all_to_all x1 -> x3, waiting for transfers between devices: 3.47 us -> 26 us  [exchange(): lax.all_to_all(values, 'chip', split_axis=0, concat_axis=0, tiled=True)]
    all_to_all x1 -> x3, starting transfers between devices: 4.75 us -> 21.2 us  [exchange(): lax.all_to_all(values, 'chip', split_axis=0, concat_axis=0, tiled=True)]
    pallas_call x5 -> x9, Pallas kernels: 24.9 us -> 38.6 us  [call(): pl.pallas_call(kernel, out_shape=out, in_specs=[whole] * len(args), out_s...]
    ppermute x2, waiting for transfers between devices: 0.01 us -> 3.1 us  [scattered(): left = lax.ppermute(fwd1, 'dp', ahead)]
    ppermute x2, starting transfers between devices: 3.3 us -> 6.07 us  [scattered(): right = lax.ppermute(bwd1, 'dp', behind)]
    ppermute x2, starting transfers between devices: 1.96 us -> 0.09 us  [scattered(): left = lax.ppermute(fwd1, 'dp', ahead)]
    ppermute x2, waiting for transfers between devices: 5.45 us -> 7.2 us  [scattered(): left2 = lax.ppermute(fwd2, 'dp', ahead)]
  transfers between devices with their start and end apart: 11 -> 14, of which waited for: 6 -> 8; matrix products, arithmetic and copies ran while one was open for 9% -> 8% of each run, Pallas kernels for 8% -> 18%
where the time goes in v2:
time: 128 us; the launch traced here: 127 us
  Pallas kernels  38.6 us (30%)
  waiting for transfers between devices  38.3 us (30%)
  starting transfers between devices  34 us (27%)
  other arithmetic  11.3 us (9%)
  local copies, waits for them, and re-layouts  3.9 us (3%)
    pallas_call x9, Pallas kernels, call(): pl.pallas_call(kernel, out_shape=out, in_specs=[whole] * len(args), out_s...  38.6 us
    all_to_all x3, waiting for transfers between devices, exchange(): lax.all_to_all(values, 'chip', split_axis=0, concat_axis=0, tiled=True)  26 us
    all_to_all x3, starting transfers between devices, exchange(): lax.all_to_all(values, 'chip', split_axis=0, concat_axis=0, tiled=True)  21.2 us
    ppermute x2, waiting for transfers between devices, scattered(): left2 = lax.ppermute(fwd2, 'dp', ahead)  7.2 us
    ppermute x2, starting transfers between devices, scattered(): right2 = lax.ppermute(bwd2, 'dp', behind)  6.52 us
    ppermute x2, starting transfers between devices, scattered(): right = lax.ppermute(bwd1, 'dp', behind)  6.07 us
    concatenate x4, other arithmetic, scattered(): return jnp.concatenate([low, high], axis=0).astype(BF)  4.03 us
    unnamed x26, local copies, waits for them, and re-layouts  3.37 us
  transfers between devices with their start and end apart: 14, of which 8 were waited for; matrix products, arithmetic and copies ran while one was open for 8% of the time, Pallas kernels for 18%

profile of v2, /device:TPU:32, one launch (start us, length us, event | category | flops | bytes accessed | tf_op | source)
XLA Modules:
  0.0 126.9 jit_solution(7322988162559775479)
XLA Ops:
  0.6 2.2 %shard_map.103 = bf16[32,9,8,128]{3,2,1,0:T(8,128)(2,1)} custom-call(bf16[256,1024]{1,0:T(8,128)(2,1)} %x_ref.1, s32[1,256]{1,0:T(1,128)} %bitcast.10, s32[1,256]{1,0:T(1,128)} %bitcast.13), custom_call_target="tpu_custom_call" | custom-call | tf_op jit(solution)/shard_map/pallas_call | solution.py:176
  2.9 11.4 %all-to-all-start.1 = ((bf16[32,9,8,128]{3,2,1,0:T(8,128)(2,1)}), bf16[32,9,8,128]{3,2,1,0:T(8,128)(2,1)S(1)}, u32[]{:S(2)}, u32[]{:S(2)}) async-start(bf16[32,9,8,128]{3,2,1,0:T(8,128)(2,1)} %shard_map.103), calls=%async_computation.1 | async-start | bytes 1179648 | tf_op jit(solution)/shard_map/all_to_all | solution.py:225
  14.8 2.3 %shard_map.102 = bf16[32,9,8,128]{3,2,1,0:T(8,128)(2,1)} custom-call(bf16[256,1024]{1,0:T(8,128)(2,1)} %g_ref.1, bf16[1,256]{1,0:T(2,128)(2,1)} %reshape.82.gate_ref, s32[1,256]{1,0:T(1,128)} %bitcast.11, s32[1,256]{1,0:T(1,128)} %bitcast.14), custom_call_target="tpu_custom_call" | custom-call | tf_op jit(solution)/shard_map/pallas_call | solution.py:176
  17.0 16.2 %all-to-all-done.1.mine_ref = bf16[32,9,8,128]{3,2,1,0:T(8,128)(2,1)S(1)} async-done(((bf16[32,9,8,128]{3,2,1,0:T(8,128)(2,1)}), bf16[32,9,8,128]{3,2,1,0:T(8,128)(2,1)S(1)}, u32[]{:S(2)}, u32[]{:S(2)}) %all-to-all-start.1) | async-done | bytes 589856 | tf_op jit(solution)/shard_map/all_to_all | solution.py:225
  33.3 4.9 %all-to-all-start = ((bf16[32,9,8,128]{3,2,1,0:T(8,128)(2,1)}), bf16[32,9,8,128]{3,2,1,0:T(8,128)(2,1)S(1)}, u32[]{:S(2)}, u32[]{:S(2)}) async-start(bf16[32,9,8,128]{3,2,1,0:T(8,128)(2,1)} %shard_map.102), calls=%async_computation | async-start | bytes 1179648 | tf_op jit(solution)/shard_map/all_to_all | solution.py:225
  38.2 2.0 %collective-permute-done.other_ref = bf16[32,9,8,128]{3,2,1,0:T(8,128)(2,1)S(1)} collective-permute-done((bf16[32,9,8,128]{3,2,1,0:T(8,128)(2,1)S(1)}, bf16[32,9,8,128]{3,2,1,0:T(8,128)(2,1)S(1)}, u32[]{:S(2)}, u32[]{:S(2)}) %collective-permute-start) | collective-permute-done | bytes 589856 | tf_op jit(solution)/shard_map/ppermute | solution.py:239
  41.1 6.7 %shard_map.104 = (bf16[576,1024]{1,0:T(8,128)(2,1)}, bf16[576,1024]{1,0:T(8,128)(2,1)}, f32[576,1024]{1,0:T(8,128)}) custom-call(bf16[32,9,8,128]{3,2,1,0:T(8,128)(2,1)} %copy-done.2, bf16[32,9,8,128]{3,2,1,0:T(8,128)(2,1)} %copy-done.3, bf16[1,1024,1024]{2,1,0:T(8,128)(2,1)} %up_ref.5), custom_call_target="tpu_custom_call" | custom-call | tf_op jit(solution)/shard_map/pallas_call | solution.py:176
  47.8 8.6 %all-to-all-done.raw_ref = bf16[32,9,8,128]{3,2,1,0:T(8,128)(2,1)S(1)} async-done(((bf16[32,9,8,128]{3,2,1,0:T(8,128)(2,1)}), bf16[32,9,8,128]{3,2,1,0:T(8,128)(2,1)S(1)}, u32[]{:S(2)}, u32[]{:S(2)}) %all-to-all-start) | async-done | bytes 589856 | tf_op jit(solution)/shard_map/all_to_all | solution.py:225
  57.2 5.6 %shard_map.105 = (bf16[288,1024]{1,0:T(8,128)(2,1)}, bf16[288,1024]{1,0:T(8,128)(2,1)}, f32[288,128]{1,0:T(8,128)}) custom-call(bf16[32,9,8,128]{3,2,1,0:T(8,128)(2,1)} %copy-done.1, bf16[1,1024,1024]{2,1,0:T(8,128)(2,1)} %down_ref.3, bf16[576,1024]{1,0:T(8,128)(2,1)} %get-tuple-element.27.act, f32[576,1024]{1,0:T(8,128)} %get-tuple-element.29.slope), custom_call_target="tpu_custom_call" | custom-call | tf_op jit(solution)/shard_map/pallas_call | solution.py:176
  63.6 4.3 %shard_map.107 = (bf16[256,1024]{1,0:T(8,128)(2,1)}, bf16[256,1024]{1,0:T(8,128)(2,1)}, bf16[128,1024]{1,0:T(8,128)(2,1)}, bf16[128,1024]{1,0:T(8,128)(2,1)}, bf...) custom-call(bf16[288,1024]{1,0:T(8,128)(2,1)} %get-tuple-element.32.own_ref, bf16[32,9,8,128]{3,2,1,0:T(8,128)(2,1)} %copy-done.4, ...), custom_call_target="tpu_custom_call" | custom-call | tf_op jit(solution)/shard_map/pallas_call | solution.py:176
  67.9 7.0 %shard_map.108 = (bf16[288,1024]{1,0:T(8,128)(2,1)}, bf16[32,10,8,128]{3,2,1,0:T(8,128)(2,1)}) custom-call(bf16[288,1024]{1,0:T(8,128)(2,1)} %get-tuple-element.33.ds_ref, bf16[1,1024,1024]{2,1,0:T(8,128)(2,1)} %down_ref.3, bf16[576,1024]{1,0:T(8,128)(2,1)} %get-tuple-element.27.act, f32[576,1024]{1,0:T(8,128)} %get-tuple-element.29.slope, ...), custom_call_target="tpu_custom_call" | custom-call | tf_op jit(solution)/shard_map/pallas_call | solution.py:176
  74.9 2.8 %collective-permute-start.7 = (bf16[256,1024]{1,0:T(8,128)(2,1)S(1)}, bf16[256,1024]{1,0:T(8,128)(2,1)S(1)}, u32[]{:S(2)}, u32[]{:S(2)}) collective-permute-start(bf16[256,1024]{1,0:T(8,128)(2,1)S(1)} %copy-done.11), channel_id=1, source_target_pairs={{0,3},{1,0},{2,1},{3,2},{4,7},{5,4},{6,5},{7,6},{8,11},{9,8},{10,9... | collective-permute-start | bytes 1572872 | tf_op jit(solution)/shard_map/ppermute | solution.py:200
  77.8 3.7 %shard_map.106 = bf16[32,10,8,128]{3,2,1,0:T(8,128)(2,1)} custom-call(bf16[288,1024]{1,0:T(8,128)(2,1)} %get-tuple-element.30.dh.dh_own, f32[288,128]{1,0:T(8,128)} %get-tuple-element.31.gate, bf16[1,1024,1024]{2,1,0:T(8,128)(2,1)} %up_ref.5), custom_call_target="tpu_custom_call" | custom-call | tf_op jit(solution)/shard_map/pallas_call | solution.py:176
  81.5 2.1 %add_convert_fusion = bf16[32,10,8,128]{3,2,1,0:T(8,128)(2,1)} fusion(bf16[32,10,8,128]{3,2,1,0:T(8,128)(2,1)S(1)} %collective-permute-done.2, bf16[32,10,8,128]{3,2,1,0:T(8,128)(2,1)} %shard_map.106), kind=kLoop, calls=%fused_computation | loop fusion | flops 1310720 | bytes 1966080 | tf_op jit(solution)/shard_map/convert_element_type | solution.py:277
  83.6 4.3 %shard_map.110 = (bf16[256,1024]{1,0:T(8,128)(2,1)}, bf16[256,1024]{1,0:T(8,128)(2,1)}, bf16[128,1024]{1,0:T(8,128)(2,1)}, bf16[128,1024]{1,0:T(8,128)(2,1)}, bf16[256,1024]{1,0:T(8,128)(2,1)}) custom-call(bf16[576,1024]{1,0:T(8,128)(2,1)} %get-tuple-element.38.xs, bf16[288,1024]{1,0:T(8,128)(2,1)} %get-tuple-element.30.dh.dh_own, ...), custom_call_target="tpu_custom_call" | custom-call | tf_op jit(solution)/shard_map/pallas_call | solution.py:176
  87.9 3.2 %collective-permute-start.3 = (bf16[256,1024]{1,0:T(8,128)(2,1)}, bf16[256,1024]{1,0:T(8,128)(2,1)S(1)}, u32[]{:S(2)}, u32[]{:S(2)}) collective-permute-start(bf16[256,1024]{1,0:T(8,128)(2,1)} %get-tuple-element.41), channel_id=1, source_target_pairs={{0,3},{1,0},{2,1},{3,2},{4,7},{5,4},{6,5},{7,6},{8,11},{9,8},{10,9... | collective-permute-start | bytes 1572872 | tf_op jit(solution)/shard_map/ppermute | solution.py:200
  92.2 3.2 %collective-permute-start.10 = (bf16[128,1024]{1,0:T(8,128)(2,1)}, bf16[128,1024]{1,0:T(8,128)(2,1)S(1)}, u32[]{:S(2)}, u32[]{:S(2)}) collective-permute-start(bf16[128,1024]{1,0:T(8,128)(2,1)} %add_convert_fusion.1), channel_id=1, source_target_pairs={{0,3},{1,0},{2,1},{3,2},{4,7},{5,4},{6,5},{7,6},{8,11},{9,8},{10,9... | collective-permute-start | bytes 786440 | tf_op jit(solution)/shard_map/ppermute | solution.py:204
  95.4 2.1 %collective-permute-done.8 = bf16[256,1024]{1,0:T(8,128)(2,1)S(1)} collective-permute-done((bf16[256,1024]{1,0:T(8,128)(2,1)S(1)}, bf16[256,1024]{1,0:T(8,128)(2,1)S(1)}, u32[]{:S(2)}, u32[]{:S(2)}) %collective-permute-start.8) | collective-permute-done | bytes 524320 | tf_op jit(solution)/shard_map/ppermute | solution.py:199
  98.3 4.9 %all-to-all-start.2 = ((bf16[32,10,8,128]{3,2,1,0:T(8,128)(2,1)}), bf16[32,10,8,128]{3,2,1,0:T(8,128)(2,1)S(1)}, u32[]{:S(2)}, u32[]{:S(2)}) async-start(bf16[32,10,8,128]{3,2,1,0:T(8,128)(2,1)} %add_convert_fusion), calls=%async_computation.2 | async-start | bytes 1310720 | tf_op jit(solution)/shard_map/all_to_all | solution.py:225
  104.5 3.3 %collective-permute-start.6 = (bf16[128,1024]{1,0:T(8,128)(2,1)S(1)}, bf16[128,1024]{1,0:T(8,128)(2,1)S(1)}, u32[]{:S(2)}, u32[]{:S(2)}) collective-permute-start(bf16[128,1024]{1,0:T(8,128)(2,1)S(1)} %add_convert_fusion.3), channel_id=1, source_target_pairs={{0,3},{1,0},{2,1},{3,2},{4,7},{5,4},{6,5},{7,6},{8,11},{9,8},{10,9... | collective-permute-start | bytes 786440 | tf_op jit(solution)/shard_map/ppermute | solution.py:204
  110.0 4.5 %collective-permute-done.9 = bf16[128,1024]{1,0:T(8,128)(2,1)} collective-permute-done((bf16[128,1024]{1,0:T(8,128)(2,1)}, bf16[128,1024]{1,0:T(8,128)(2,1)}, u32[]{:S(2)}, u32[]{:S(2)}) %collective-permute-start.9) | collective-permute-done | bytes 262176 | tf_op jit(solution)/shard_map/ppermute | solution.py:203
  116.5 2.7 %collective-permute-done.5 = bf16[128,1024]{1,0:T(8,128)(2,1)S(1)} collective-permute-done((bf16[128,1024]{1,0:T(8,128)(2,1)S(1)}, bf16[128,1024]{1,0:T(8,128)(2,1)S(1)}, u32[]{:S(2)}, u32[]{:S(2)}) %collective-permute-start.5) | collective-permute-done | bytes 262176 | tf_op jit(solution)/shard_map/ppermute | solution.py:203
  123.2 2.4 %shard_map.109 = (bf16[256,1024]{1,0:T(8,128)(2,1)}, bf16[1,256]{1,0:T(2,128)(2,1)}) custom-call(bf16[32,10,8,128]{3,2,1,0:T(8,128)(2,1)} %copy-done, bf16[1,256]{1,0:T(2,128)(2,1)} %reshape.82.gate_ref, s32[1,256]{1,0:T(1,128)} %bitcast.12, s32[1,256]{1,0:T(1,128)} %bitcast.15), custom_call_target="tpu_custom_call" | custom-call | tf_op jit(solution)/shard_map/pallas_call | solution.py:176
  125.6 1.2 reduce
  (52 shorter events, 14.3 us)
Async XLA Ops:
  0.6 13.6 %copy-start.12 = (bf16[256]{0:T(256)(128)(2,1)S(1)}, bf16[256]{0:T(256)(128)(2,1)}, u32[]{:S(2)}) copy-start(bf16[256]{0:T(256)(128)(2,1)} %param.9) | copy-start | bytes 1540
  2.9 30.4 %all-to-all-start.1 = ((bf16[32,9,8,128]{3,2,1,0:T(8,128)(2,1)}), bf16[32,9,8,128]{3,2,1,0:T(8,128)(2,1)S(1)}, u32[]{:S(2)}, u32[]{:S(2)}) async-start(bf16[32,9,8,128]{3,2,1,0:T(8,128)(2,1)} %shard_map.103), calls=%async_computation.1 | async-start | bytes 1179648 | tf_op jit(solution)/shard_map/all_to_all | solution.py:225
  33.3 7.0 %copy-start.2 = (bf16[32,9,8,128]{3,2,1,0:T(8,128)(2,1)}, bf16[32,9,8,128]{3,2,1,0:T(8,128)(2,1)S(1)}, u32[]{:S(2)}) copy-start(bf16[32,9,8,128]{3,2,1,0:T(8,128)(2,1)S(1)} %all-to-all-done.1.mine_ref) | copy-start | bytes 1769476
  33.3 23.1 %all-to-all-start = ((bf16[32,9,8,128]{3,2,1,0:T(8,128)(2,1)}), bf16[32,9,8,128]{3,2,1,0:T(8,128)(2,1)S(1)}, u32[]{:S(2)}, u32[]{:S(2)}) async-start(bf16[32,9,8,128]{3,2,1,0:T(8,128)(2,1)} %shard_map.102), calls=%async_computation | async-start | bytes 1179648 | tf_op jit(solution)/shard_map/all_to_all | solution.py:225
  38.1 2.1 %collective-permute-start = (bf16[32,9,8,128]{3,2,1,0:T(8,128)(2,1)S(1)}, bf16[32,9,8,128]{3,2,1,0:T(8,128)(2,1)S(1)}, u32[]{:S(2)}, u32[]{:S(2)}) collective-permute-start(bf16[32,9,8,128]{3,2,1,0:T(8,128)(2,1)S(1)} %all-to-all-done.1.mine_ref), channel_id=1, source_target_pairs={{0,4},{4,0},{1,5},{5,1},{2,6},{6,2},{3,7},{7,3},{8,12},{12,8},{9,1... | collective-permute-start | bytes 1769480 | tf_op jit(solution)/shard_map/ppermute | solution.py:239
  56.4 6.4 %collective-permute-start.1 = (bf16[32,9,8,128]{3,2,1,0:T(8,128)(2,1)S(1)}, bf16[32,9,8,128]{3,2,1,0:T(8,128)(2,1)S(1)}, u32[]{:S(2)}, u32[]{:S(2)}) collective-permute-start(bf16[32,9,8,128]{3,2,1,0:T(8,128)(2,1)S(1)} %all-to-all-done.raw_ref), channel_id=1, source_target_pairs={{0,4},{4,0},{1,5},{5,1},{2,6},{6,2},{3,7},{7,3},{8,12},{12,8},{9,1... | collective-permute-start | bytes 1769480 | tf_op jit(solution)/shard_map/ppermute | solution.py:250
  67.9 7.0 %copy-start.11 = (bf16[256,1024]{1,0:T(8,128)(2,1)S(1)}, bf16[256,1024]{1,0:T(8,128)(2,1)}, u32[]{:S(2)}) copy-start(bf16[256,1024]{1,0:T(8,128)(2,1)} %get-tuple-element.46) | copy-start | bytes 1572868
  74.9 6.6 %collective-permute-start.2 = (bf16[32,10,8,128]{3,2,1,0:T(8,128)(2,1)}, bf16[32,10,8,128]{3,2,1,0:T(8,128)(2,1)S(1)}, u32[]{:S(2)}, u32[]{:S(2)}) collective-permute-start(bf16[32,10,8,128]{3,2,1,0:T(8,128)(2,1)} %get-tuple-element.34), channel_id=1, source_target_pairs={{0,4},{4,0},{1,5},{5,1},{2,6},{6,2},{3,7},{7,3},{8,12},{12,8},{9,1... | collective-permute-start | bytes 1966088 | tf_op jit(solution)/shard_map/ppermute | solution.py:275
  74.9 16.4 %collective-permute-start.7 = (bf16[256,1024]{1,0:T(8,128)(2,1)S(1)}, bf16[256,1024]{1,0:T(8,128)(2,1)S(1)}, u32[]{:S(2)}, u32[]{:S(2)}) collective-permute-start(bf16[256,1024]{1,0:T(8,128)(2,1)S(1)} %copy-done.11), channel_id=1, source_target_pairs={{0,3},{1,0},{2,1},{3,2},{4,7},{5,4},{6,5},{7,6},{8,11},{9,8},{10,9... | collective-permute-start | bytes 1572872 | tf_op jit(solution)/shard_map/ppermute | solution.py:200
  77.8 3.7 %copy-start.10 = (bf16[256,1024]{1,0:T(8,128)(2,1)S(1)}, bf16[256,1024]{1,0:T(8,128)(2,1)}, u32[]{:S(2)}) copy-start(bf16[256,1024]{1,0:T(8,128)(2,1)} %get-tuple-element.48) | copy-start | bytes 1572868
  81.5 16.0 %collective-permute-start.8 = (bf16[256,1024]{1,0:T(8,128)(2,1)S(1)}, bf16[256,1024]{1,0:T(8,128)(2,1)S(1)}, u32[]{:S(2)}, u32[]{:S(2)}) collective-permute-start(bf16[256,1024]{1,0:T(8,128)(2,1)S(1)} %copy-done.10), channel_id=1, source_target_pairs={{0,1},{1,2},{2,3},{3,0},{4,5},{5,6},{6,7},{7,4},{8,9},{9,10},{10,1... | collective-permute-start | bytes 1572872 | tf_op jit(solution)/shard_map/ppermute | solution.py:199
  83.6 7.6 %copy-start.5 = (bf16[256,1024]{1,0:T(8,128)(2,1)S(1)}, bf16[256,1024]{1,0:T(8,128)(2,1)}, u32[]{:S(2)}) copy-start(bf16[256,1024]{1,0:T(8,128)(2,1)} %get-tuple-element.45) | copy-start | bytes 1572868
  87.9 3.5 %copy-start.7 = (bf16[128,1024]{1,0:T(8,128)(2,1)S(1)}, bf16[128,1024]{1,0:T(8,128)(2,1)}, u32[]{:S(2)}) copy-start(bf16[128,1024]{1,0:T(8,128)(2,1)} %get-tuple-element.49) | copy-start | bytes 786436
  87.9 9.6 %copy-start.6 = (bf16[128,1024]{1,0:T(8,128)(2,1)S(1)}, bf16[128,1024]{1,0:T(8,128)(2,1)}, u32[]{:S(2)}) copy-start(bf16[128,1024]{1,0:T(8,128)(2,1)} %get-tuple-element.47) | copy-start | bytes 786436
  87.9 16.5 %collective-permute-start.3 = (bf16[256,1024]{1,0:T(8,128)(2,1)}, bf16[256,1024]{1,0:T(8,128)(2,1)S(1)}, u32[]{:S(2)}, u32[]{:S(2)}) collective-permute-start(bf16[256,1024]{1,0:T(8,128)(2,1)} %get-tuple-element.41), channel_id=1, source_target_pairs={{0,3},{1,0},{2,1},{3,2},{4,7},{5,4},{6,5},{7,6},{8,11},{9,8},{10,9... | collective-permute-start | bytes 1572872 | tf_op jit(solution)/shard_map/ppermute | solution.py:200
  91.3 17.5 %collective-permute-start.4 = (bf16[256,1024]{1,0:T(8,128)(2,1)}, bf16[256,1024]{1,0:T(8,128)(2,1)}, u32[]{:S(2)}, u32[]{:S(2)}) collective-permute-start(bf16[256,1024]{1,0:T(8,128)(2,1)} %get-tuple-element.43), channel_id=1, source_target_pairs={{0,1},{1,2},{2,3},{3,0},{4,5},{5,6},{6,7},{7,4},{8,9},{9,10},{10,1... | collective-permute-start | bytes 1572872 | tf_op jit(solution)/shard_map/ppermute | solution.py:199
  92.2 17.8 %collective-permute-start.10 = (bf16[128,1024]{1,0:T(8,128)(2,1)}, bf16[128,1024]{1,0:T(8,128)(2,1)S(1)}, u32[]{:S(2)}, u32[]{:S(2)}) collective-permute-start(bf16[128,1024]{1,0:T(8,128)(2,1)} %add_convert_fusion.1), channel_id=1, source_target_pairs={{0,3},{1,0},{2,1},{3,2},{4,7},{5,4},{6,5},{7,6},{8,11},{9,8},{10,9... | collective-permute-start | bytes 786440 | tf_op jit(solution)/shard_map/ppermute | solution.py:204
  98.3 16.2 %collective-permute-start.9 = (bf16[128,1024]{1,0:T(8,128)(2,1)}, bf16[128,1024]{1,0:T(8,128)(2,1)}, u32[]{:S(2)}, u32[]{:S(2)}) collective-permute-start(bf16[128,1024]{1,0:T(8,128)(2,1)} %add_convert_fusion.2), channel_id=1, source_target_pairs={{0,1},{1,2},{2,3},{3,0},{4,5},{5,6},{6,7},{7,4},{8,9},{9,10},{10,1... | collective-permute-start | bytes 786440 | tf_op jit(solution)/shard_map/ppermute | solution.py:203
  98.3 24.1 %all-to-all-start.2 = ((bf16[32,10,8,128]{3,2,1,0:T(8,128)(2,1)}), bf16[32,10,8,128]{3,2,1,0:T(8,128)(2,1)S(1)}, u32[]{:S(2)}, u32[]{:S(2)}) async-start(bf16[32,10,8,128]{3,2,1,0:T(8,128)(2,1)} %add_convert_fusion), calls=%async_computation.2 | async-start | bytes 1310720 | tf_op jit(solution)/shard_map/all_to_all | solution.py:225
  103.2 1.2 copy-start.9
  103.2 5.6 %copy-start.8 = (bf16[128,1024]{1,0:T(8,128)(2,1)S(1)}, bf16[128,1024]{1,0:T(8,128)(2,1)}, u32[]{:S(2)}) copy-start(bf16[128,1024]{1,0:T(8,128)(2,1)} %get-tuple-element.42) | copy-start | bytes 786436
  104.5 11.9 %collective-permute-start.6 = (bf16[128,1024]{1,0:T(8,128)(2,1)S(1)}, bf16[128,1024]{1,0:T(8,128)(2,1)S(1)}, u32[]{:S(2)}, u32[]{:S(2)}) collective-permute-start(bf16[128,1024]{1,0:T(8,128)(2,1)S(1)} %add_convert_fusion.3), channel_id=1, source_target_pairs={{0,3},{1,0},{2,1},{3,2},{4,7},{5,4},{6,5},{7,6},{8,11},{9,8},{10,9... | collective-permute-start | bytes 786440 | tf_op jit(solution)/shard_map/ppermute | solution.py:204
  109.9 9.3 %collective-permute-start.5 = (bf16[128,1024]{1,0:T(8,128)(2,1)S(1)}, bf16[128,1024]{1,0:T(8,128)(2,1)S(1)}, u32[]{:S(2)}, u32[]{:S(2)}) collective-permute-start(bf16[128,1024]{1,0:T(8,128)(2,1)S(1)} %add_convert_fusion.4), channel_id=1, source_target_pairs={{0,1},{1,2},{2,3},{3,0},{4,5},{5,6},{6,7},{7,4},{8,9},{9,10},{10,1... | collective-permute-start | bytes 786440 | tf_op jit(solution)/shard_map/ppermute | solution.py:203
  122.4 0.8 copy-start
  (3 other events, 2.5 us)

commit v3 on v1

v3 whole, which is shorter than its diff:
```python
import functools

import jax
import jax.numpy as jnp
from jax import lax
from jax.experimental import pallas as pl
from jax.experimental.pallas import tpu as pltpu
from jax.sharding import Mesh, PartitionSpec as P

BF = jnp.bfloat16
F32 = jnp.float32
VMEM = 56 * 1024 * 1024
LANES = 128


def matmul(a, b, contract):
    return lax.dot_general(a, b, (contract, ((), ())), preferred_element_type=F32)


def slot_row(expert, slot, groups):
    return jnp.where(slot < 8, expert * 8 + slot, 8 * groups + expert)


def to_tiles(full, row, out_ref, base, groups, turn):
    last = row + 8 * groups
    for j in range(8):
        cols = slice(LANES * j, LANES * (j + 1))
        out_ref[:, base + j] = full[row:last, cols].reshape(groups, 8, LANES).astype(BF)
        turn[:, j, :] = full[last : last + groups, cols]
    out_ref[:, base + 8] = turn[...].astype(BF)


def from_tiles(ref, base, dst_ref, groups, turn):
    last = 8 * groups
    turn[...] = ref[:, base + 8].astype(F32)
    for j in range(8):
        cols = slice(LANES * j, LANES * (j + 1))
        dst_ref[:last, cols] = ref[:, base + j].astype(F32).reshape(last, LANES).astype(BF)
        dst_ref[last : last + groups, cols] = turn[:, j, :].astype(BF)


def pack_kernel(x_ref, g_ref, gate_ref, expert_ref, slot_ref, out_ref, full, turn):
    groups = out_ref.shape[0]
    count = x_ref.shape[0]
    place = slot_row(expert_ref[...], slot_ref[...], groups).reshape(1, count)
    hit = lax.broadcasted_iota(jnp.int32, (9 * groups, count), 0) == place
    full[...] = matmul(jnp.where(hit, 1.0, 0.0).astype(BF), x_ref[...], ((1,), (0,)))
    to_tiles(full, 0, out_ref, 0, groups, turn)
    gate = gate_ref[...].astype(F32).reshape(1, count)
    full[...] = matmul(jnp.where(hit, gate, 0.0).astype(BF), g_ref[...], ((1,), (0,)))
    to_tiles(full, 0, out_ref, 9, groups, turn)


def turn_kernel(up_ref, down_ref, up_out, down_out):
    up_out[...] = up_ref[0].T
    down_out[...] = down_ref[0].T


def weight_parts(lhs_ref, rhs, me, fwd1, bwd1, fwd2, bwd2, own):
    half = own.shape[0] // 2
    size = 2 * half

    def chunk(step):
        at = pl.multiple_of(lax.rem(me + step, 4) * size, size)
        return matmul(lhs_ref[:, pl.ds(at, size)], rhs, ((0,), (0,))).astype(BF)

    far = chunk(2)
    fwd1[:half] = far[:half]
    bwd1[half:] = far[half:]
    right = chunk(1)
    fwd1[half:] = right[half:]
    fwd2[...] = right[:half]
    left = chunk(3)
    bwd1[:half] = left[:half]
    bwd2[...] = left[half:]
    own[...] = chunk(0)


def forward(raw_ref, up_ref, xs, ds, act, slope, hid, turn):
    groups = raw_ref.shape[0]
    from_tiles(raw_ref, 0, xs, groups, turn)
    from_tiles(raw_ref, 9, ds, groups, turn)
    hid[...] = matmul(xs[...], up_ref[0], ((1,), (0,)))
    step = 32

    def block(i, carry):
        at = pl.ds(pl.multiple_of(i * step, step), step)
        v = hid[at, :]
        cdf = 0.5 * (1.0 + lax.erf(v * 0.7071067811865476))
        pdf = jnp.exp(-0.5 * v * v) * 0.3989422804014327
        act[at, :] = (v * cdf).astype(BF)
        slope[at, :] = cdf + v * pdf
        return carry

    lax.fori_loop(0, hid.shape[0] // step, block, 0)


def expert_kernel(
    raw_ref, up_ref, up_turned, down_turned, ds_own, act_own, slope_own,
    fwd1, bwd1, fwd2, bwd2, own, xs, dh, keep, give,
    ds, act, slope, work, gate, half_ds, half_act, turn,
):
    groups = raw_ref.shape[0]
    rows = 9 * groups
    forward(raw_ref, up_ref, xs, half_ds, half_act, slope, work.at[:rows], turn)
    ds[:rows] = ds_own[...]
    ds[rows:] = half_ds[...]
    act[:rows] = act_own[...]
    act[rows:] = half_act[...]
    weight_parts(act, ds[...], lax.axis_index("dp"), fwd1, bwd1, fwd2, bwd2, own)
    work[...] = matmul(ds[...], down_turned[...], ((1,), (0,)))
    step = 32
    for half, slopes in enumerate((slope_own, slope)):

        def block(i, carry):
            here = pl.ds(pl.multiple_of(i * step, step), step)
            at = pl.ds(pl.multiple_of(half * rows + i * step, step), step)
            d = work[at, :]
            dh[at, :] = (d * slopes[here, :]).astype(BF)
            total = jnp.sum(act[at, :].astype(F32) * d, axis=1, keepdims=True)
            gate[at, :] = jnp.broadcast_to(total, (step, LANES))
            return carry

        lax.fori_loop(0, rows // step, block, 0)
    work[...] = matmul(dh[...], up_turned[...], ((1,), (0,)))
    lane = lax.broadcasted_iota(jnp.int32, (groups, 8, LANES), 2)
    for row, ref in ((0, keep), (rows, give)):
        to_tiles(work, row, ref, 0, groups, turn)
        last = gate[row + 8 * groups : row + rows, :]
        for j in range(8):
            turn[:, j, :] = last
        first = gate[row : row + 8 * groups, :].reshape(groups, 8, LANES)
        ref[:, 9] = jnp.where(lane < 64, first, turn[...]).astype(BF)


def up_kernel(xs_own, xs_other, dh, fwd1, bwd1, fwd2, bwd2, own, xs):
    rows = xs_own.shape[0]
    xs[:rows] = xs_own[...]
    xs[rows:] = xs_other[...]
    weight_parts(xs, dh[...], lax.axis_index("dp"), fwd1, bwd1, fwd2, bwd2, own)


def ring_kernel(fwd2, left, bwd2, right, fwd_out, bwd_out):
    half = fwd2.shape[0]
    fwd_out[...] = (fwd2[...].astype(F32) + left[:half].astype(F32)).astype(BF)
    bwd_out[...] = (bwd2[...].astype(F32) + right[half:].astype(F32)).astype(BF)


def final_kernel(own, left, right, left2, right2, out):
    half = left2.shape[0]
    low = own[:half].astype(F32) + right[:half].astype(F32)
    out[:half] = (low + left2[...].astype(F32)).astype(BF)
    high = own[half:].astype(F32) + left[half:].astype(F32)
    out[half:] = (high + right2[...].astype(F32)).astype(BF)


def unpack_kernel(back_ref, gate_ref, expert_ref, slot_ref, out_ref, gate_out_ref, rowbuf, turn):
    groups = back_ref.shape[0]
    count = out_ref.shape[0]
    from_tiles(back_ref, 0, rowbuf, groups, turn)
    expert = expert_ref[...].reshape(1, count)
    slot = slot_ref[...].reshape(1, count)
    rows = lax.broadcasted_iota(jnp.int32, (9 * groups, count), 0)
    pick = jnp.where(rows == slot_row(expert, slot, groups), 1.0, 0.0).astype(BF)
    out_ref[...] = matmul(pick, rowbuf[...], ((0,), (0,))).astype(BF)
    gates = back_ref[:, 9].astype(F32).reshape(8 * groups, LANES).astype(BF)
    rows = lax.broadcasted_iota(jnp.int32, (8 * groups, count), 0)
    low = jnp.where(rows == slot_row(expert, slot, groups), 1.0, 0.0).astype(BF)
    high = jnp.where((rows == expert * 8) & (slot == 8), 1.0, 0.0).astype(BF)
    low = matmul(gates, low, ((0,), (0,)))
    high = matmul(gates, high, ((0,), (0,)))
    total = low[0:1, :] + high[64:65, :]
    gate = gate_ref[...].astype(F32).reshape(1, count)
    gate_out_ref[...] = (total / gate).astype(BF).reshape(count)


def call(kernel, out, scratch, *args):
    whole = pl.BlockSpec(memory_space=pltpu.VMEM)
    return pl.pallas_call(
        kernel,
        out_shape=out,
        in_specs=[whole] * len(args),
        out_specs=jax.tree.map(lambda _: whole, out),
        scratch_shapes=scratch,
        compiler_params=pltpu.CompilerParams(vmem_limit_bytes=VMEM),
    )(*args)


def after(value, earlier):
    return lax.optimization_barrier((value, earlier))[0]


def shape(*dims, dtype=BF):
    return jax.ShapeDtypeStruct(dims, dtype)


AHEAD = [(i, (i + 1) % 4) for i in range(4)]
BEHIND = [(i, (i + 3) % 4) for i in range(4)]


def ring(fwd, bwd):
    return lax.ppermute(fwd, "dp", AHEAD), lax.ppermute(bwd, "dp", BEHIND)


def on_device(tokens_in, out_grad, gates, expert_ids, slot_ids, w_up, w_down):
    groups = lax.axis_size("chip")
    count, width = tokens_in.shape
    hidden = w_up.shape[2]
    rows = 9 * groups
    turn = pltpu.VMEM((groups, 8, LANES), F32)
    swap = [(0, 1), (1, 0)]

    def exchange(values):
        return lax.all_to_all(values, "chip", split_axis=0, concat_axis=0, tiled=True)

    def parts(length, columns):
        quarter = length // 4
        return (
            shape(quarter, columns),
            shape(quarter, columns),
            shape(quarter // 2, columns),
            shape(quarter // 2, columns),
            shape(quarter, columns),
        )

    sent = call(
        pack_kernel,
        shape(groups, 18, 8, LANES),
        [pltpu.VMEM((rows, width), F32), turn],
        tokens_in,
        out_grad,
        gates,
        expert_ids,
        slot_ids,
    )
    mine = exchange(sent)
    up_turned, down_turned = call(
        turn_kernel, (shape(hidden, width), shape(width, hidden)), [], w_up, w_down
    )
    mine, up_turned = lax.optimization_barrier((mine, up_turned))
    other = lax.ppermute(mine, "core", swap)
    half = (
        shape(rows, width),
        shape(rows, width),
        shape(rows, hidden),
        shape(rows, hidden, dtype=F32),
    )
    hid = pltpu.VMEM((rows, hidden), F32)
    xs_own, ds_own, act_own, slope_own = call(forward, half, [hid, turn], mine, w_up)
    returned = shape(groups, 10, 8, LANES)
    *down, xs_other, dh, keep, give = call(
        expert_kernel,
        parts(hidden, width) + (shape(rows, width), shape(2 * rows, hidden), returned, returned),
        [
            pltpu.VMEM((2 * rows, width), BF),
            pltpu.VMEM((2 * rows, hidden), BF),
            pltpu.VMEM((rows, hidden), F32),
            pltpu.VMEM((2 * rows, width), F32),
            pltpu.VMEM((2 * rows, LANES), F32),
            pltpu.VMEM((rows, width), BF),
            pltpu.VMEM((rows, hidden), BF),
            turn,
        ],
        other,
        w_up,
        up_turned,
        down_turned,
        ds_own,
        act_own,
        slope_own,
    )
    left_d, right_d = ring(down[0], down[1])
    got = lax.ppermute(give, "core", swap)
    both = (keep.astype(F32) + got.astype(F32)).astype(BF)
    back = exchange(both)
    pair = lambda parts: (shape(*parts[2].shape), shape(*parts[3].shape))
    down2 = call(ring_kernel, pair(down), [], down[2], left_d, down[3], right_d)
    xs_own = after(xs_own, down2)
    down2 = ring(*down2)
    up = call(
        up_kernel, parts(width, hidden), [pltpu.VMEM((2 * rows, width), BF)], xs_own, xs_other, dh
    )
    left_u, right_u = ring(up[0], up[1])
    down_grad = call(final_kernel, shape(hidden // 4, width), [], down[4], left_d, right_d, *down2)
    left_u, right_u, down_grad = lax.optimization_barrier((left_u, right_u, down_grad))
    up2 = ring(*call(ring_kernel, pair(up), [], up[2], left_u, up[3], right_u))
    in_grad, gate_grad = call(
        unpack_kernel,
        (shape(count, width), shape(count)),
        [pltpu.VMEM((rows, width), BF), turn],
        back,
        gates,
        expert_ids,
        slot_ids,
    )
    *up2, in_grad = lax.optimization_barrier((*up2, in_grad))
    up_grad = call(final_kernel, shape(width // 4, hidden), [], up[4], left_u, right_u, *up2)
    return (in_grad, gate_grad, up_grad[None], down_grad[None])


def solution(mesh):
    chips = mesh.devices.reshape(mesh.shape["expert"] // 2, 2, mesh.shape["dp"])
    finer = Mesh(chips, ("chip", "core", "dp"))
    tokens = ("chip", "core", "dp")
    pieces = ("chip", "core")
    return jax.shard_map(
        on_device,
        mesh=finer,
        in_specs=(
            P(tokens, None),
            P(tokens, None),
            P(tokens),
            P(tokens),
            P(tokens),
            P(pieces, None, None),
            P(pieces, None, None),
        ),
        out_specs=(
            P(tokens, None),
            P(tokens),
            P(pieces, "dp", None),
            P(pieces, "dp", None),
        ),
        check_vma=False,
    )
```

time: 114 us -> 130 us (1.14)
  blocking collectives: 43.5 us -> 0 us
  waiting for transfers between devices: 13.8 us -> 47.5 us
  Pallas kernels: 24.9 us -> 42.2 us
  starting transfers between devices: 16.2 us -> 29.6 us
  other arithmetic: 11.5 us -> 2.09 us
  local copies, waits for them, and re-layouts: 3.11 us -> 6.43 us
    all_to_all x1 -> x0, blocking collectives: 43.5 us -> none  [on_device(): mine = lax.all_to_all(sent, 'chip', split_axis=0, concat_axis=0, tiled=True)]
    all_to_all x1 -> x2, waiting for transfers between devices: 3.47 us -> 26.4 us  [exchange(): lax.all_to_all(values, 'chip', split_axis=0, concat_axis=0, tiled=True)]
    pallas_call x5 -> x10, Pallas kernels: 24.9 us -> 42.2 us  [call(): pl.pallas_call(kernel, out_shape=out, in_specs=[whole] * len(args), out_s...]
    ppermute x8, waiting for transfers between devices: 7.44 us -> 21.2 us  [ring(): return (lax.ppermute(fwd, 'dp', AHEAD), lax.ppermute(bwd, 'dp', BEHIND))]
    all_to_all x1 -> x2, starting transfers between devices: 4.75 us -> 16.7 us  [exchange(): lax.all_to_all(values, 'chip', split_axis=0, concat_axis=0, tiled=True)]
    convert_element_type x6 -> x0, other arithmetic: 5.07 us -> none  [the longest x2 1.95 us: scattered(): bwd2 = (bwd2.astype(F32) + right[half:].astype(F32)).astype(BF)]
    unnamed x20 -> x26, local copies, waits for them, and re-layouts: 1.91 us -> 6.43 us
    concatenate x4 -> x0, other arithmetic: 4.19 us -> none  [scattered(): return jnp.concatenate([low, high], axis=0).astype(BF)]
  transfers between devices with their start and end apart: 11 -> 12, of which waited for: 6 -> 4; matrix products, arithmetic and copies ran while one was open for 9% -> 2% of each run, Pallas kernels for 8% -> 18%
where the time goes in v3:
time: 130 us; the launch traced here: 129 us
  waiting for transfers between devices  47.5 us (37%)
  Pallas kernels  42.2 us (32%)
  starting transfers between devices  29.6 us (23%)
  local copies, waits for them, and re-layouts  6.43 us (5%)
  other arithmetic  2.09 us (2%)
    pallas_call x10, Pallas kernels, call(): pl.pallas_call(kernel, out_shape=out, in_specs=[whole] * len(args), out_s...  42.2 us
    all_to_all x2, waiting for transfers between devices, exchange(): lax.all_to_all(values, 'chip', split_axis=0, concat_axis=0, tiled=True)  26.4 us
    ppermute x8, waiting for transfers between devices, ring(): return (lax.ppermute(fwd, 'dp', AHEAD), lax.ppermute(bwd, 'dp', BEHIND))  21.2 us
    all_to_all x2, starting transfers between devices, exchange(): lax.all_to_all(values, 'chip', split_axis=0, concat_axis=0, tiled=True)  16.7 us
    ppermute x8, starting transfers between devices, ring(): return (lax.ppermute(fwd, 'dp', AHEAD), lax.ppermute(bwd, 'dp', BEHIND))  12.9 us
    unnamed x26, local copies, waits for them, and re-layouts  6.43 us
  transfers between devices with their start and end apart: 12, of which 4 were waited for; matrix products, arithmetic and copies ran while one was open for 2% of the time, Pallas kernels for 18%

profile of v3, /device:TPU:32, one launch (start us, length us, event | category | flops | bytes accessed | tf_op | source)
XLA Modules:
  0.0 128.6 jit_solution(11151690058263267510)
XLA Ops:
  0.6 2.8 %shard_map.102 = bf16[32,18,8,128]{3,2,1,0:T(8,128)(2,1)} custom-call(bf16[256,1024]{1,0:T(8,128)(2,1)} %x_ref.1, bf16[256,1024]{1,0:T(8,128)(2,1)} %g_ref.1, bf16[256]{0:T(256)(128)(2,1)} %gate_ref.3, s32[256]{0:T(256)} %expert_ref.3, s32[256]{0:T(256)} %slot_ref.3), custom_call_target="tpu_custom_call" | custom-call | tf_op jit(solution)/shard_map/pallas_call | solution.py:179
  3.5 11.4 %all-to-all-start = ((bf16[32,18,8,128]{3,2,1,0:T(8,128)(2,1)}), bf16[32,18,8,128]{3,2,1,0:T(8,128)(2,1)S(1)}, u32[]{:S(2)}, u32[]{:S(2)}) async-start(bf16[32,18,8,128]{3,2,1,0:T(8,128)(2,1)} %shard_map.102), calls=%async_computation | async-start | bytes 2359296 | tf_op jit(solution)/shard_map/all_to_all | solution.py:214
  14.8 4.8 %shard_map.103 = (bf16[1024,1024]{1,0:T(8,128)(2,1)}, bf16[1024,1024]{1,0:T(8,128)(2,1)}) custom-call(bf16[1,1024,1024]{2,1,0:T(8,128)(2,1)} %up_ref.5, bf16[1,1024,1024]{2,1,0:T(8,128)(2,1)} %down_ref.1), custom_call_target="tpu_custom_call" | custom-call | tf_op jit(solution)/shard_map/pallas_call | solution.py:179
  19.6 26.4 %all-to-all-done.raw_ref = bf16[32,18,8,128]{3,2,1,0:T(8,128)(2,1)S(1)} async-done(((bf16[32,18,8,128]{3,2,1,0:T(8,128)(2,1)}), bf16[32,18,8,128]{3,2,1,0:T(8,128)(2,1)S(1)}, u32[]{:S(2)}, u32[]{:S(2)}) %all-to-all-start) | async-done | bytes 1179680 | tf_op jit(solution)/shard_map/all_to_all | solution.py:214
  46.0 1.1 copy-done
  47.1 5.2 %shard_map.104 = (bf16[288,1024]{1,0:T(8,128)(2,1)}, bf16[288,1024]{1,0:T(8,128)(2,1)}, bf16[288,1024]{1,0:T(8,128)(2,1)}, f32[288,1024]{1,0:T(8,128)}) custom-call(bf16[32,18,8,128]{3,2,1,0:T(8,128)(2,1)} %copy-done, bf16[1,1024,1024]{2,1,0:T(8,128)(2,1)} %up_ref.5), custom_call_target="tpu_custom_call" | custom-call | tf_op jit(solution)/shard_map/pallas_call | solution.py:179
  53.3 13.2 %shard_map.105 = (bf16[256,1024]{1,0:T(8,128)(2,1)}, bf16[256,1024]{1,0:T(8,128)(2,1)}, bf16[128,1024]{1,0:T(8,128)(2,1)}, bf16[128,1024]{1,0:T(8,128)(2,1)}, bf...) custom-call(bf16[32,18,8,128]{3,2,1,0:T(8,128)(2,1)} %copy-done.6, ...), custom_call_target="tpu_custom_call" | custom-call | tf_op jit(solution)/shard_map/pallas_call | solution.py:179
  66.4 1.5 %collective-permute-start.1 = (bf16[256,1024]{1,0:T(8,128)(2,1)}, bf16[256,1024]{1,0:T(8,128)(2,1)S(1)}, u32[]{:S(2)}, u32[]{:S(2)}) collective-permute-start(bf16[256,1024]{1,0:T(8,128)(2,1)} %get-tuple-element.48), channel_id=1, source_target_pairs={{0,1},{1,2},{2,3},{3,0},{4,5},{5,6},{6,7},{7,4},{8,9},{9,10},{10,1... | collective-permute-start | bytes 1572872 | tf_op jit(solution)/shard_map/ppermute | solution.py:202
  67.9 1.7 %collective-permute-start.2 = (bf16[256,1024]{1,0:T(8,128)(2,1)}, bf16[256,1024]{1,0:T(8,128)(2,1)S(1)}, u32[]{:S(2)}, u32[]{:S(2)}) collective-permute-start(bf16[256,1024]{1,0:T(8,128)(2,1)} %get-tuple-element.50), channel_id=1, source_target_pairs={{0,3},{1,0},{2,1},{3,2},{4,7},{5,4},{6,5},{7,6},{8,11},{9,8},{10,9... | collective-permute-start | bytes 1572872 | tf_op jit(solution)/shard_map/ppermute | solution.py:202
  69.7 2.1 %add_convert_fusion = bf16[32,10,8,128]{3,2,1,0:T(8,128)(2,1)} fusion(bf16[32,10,8,128]{3,2,1,0:T(8,128)(2,1)S(1)} %collective-permute-done.9, bf16[32,10,8,128]{3,2,1,0:T(8,128)(2,1)} %get-tuple-element.65), kind=kLoop, calls=%fused_computation | loop fusion | flops 1310720 | bytes 1966080 | tf_op jit(solution)/shard_map/convert_element_type | solution.py:274
  71.8 5.3 %all-to-all-start.1 = ((bf16[32,10,8,128]{3,2,1,0:T(8,128)(2,1)}), bf16[32,10,8,128]{3,2,1,0:T(8,128)(2,1)S(1)}, u32[]{:S(2)}, u32[]{:S(2)}) async-start(bf16[32,10,8,128]{3,2,1,0:T(8,128)(2,1)} %add_convert_fusion), calls=%async_computation.1 | async-start | bytes 1310720 | tf_op jit(solution)/shard_map/all_to_all | solution.py:214
  77.1 5.1 %collective-permute-done.1.left = bf16[256,1024]{1,0:T(8,128)(2,1)S(1)} collective-permute-done((bf16[256,1024]{1,0:T(8,128)(2,1)}, bf16[256,1024]{1,0:T(8,128)(2,1)S(1)}, u32[]{:S(2)}, u32[]{:S(2)}) %collective-permute-start.1) | collective-permute-done | bytes 524320 | tf_op jit(solution)/shard_map/ppermute | solution.py:202
  83.2 2.2 %shard_map.106 = (bf16[128,1024]{1,0:T(8,128)(2,1)}, bf16[128,1024]{1,0:T(8,128)(2,1)}) custom-call(bf16[128,1024]{1,0:T(8,128)(2,1)} %get-tuple-element.47.fwd2, bf16[256,1024]{1,0:T(8,128)(2,1)} %copy-done.3, bf16[128,1024]{1,0:T(8,128)(2,1)} %get-tuple-element.49.bwd2, bf16[256,1024]{1,0:T(8,128)(2,1)} %copy-done.5), custom_call_target="tpu_custom_call" | custom-call | tf_op jit(solution)/shard_map/pallas_call | solution.py:179
  85.4 4.4 %shard_map.107 = (bf16[256,1024]{1,0:T(8,128)(2,1)}, bf16[256,1024]{1,0:T(8,128)(2,1)}, bf16[128,1024]{1,0:T(8,128)(2,1)}, bf16[128,1024]{1,0:T(8,128)(2,1)}, bf16[256,1024]{1,0:T(8,128)(2,1)}) custom-call(bf16[288,1024]{1,0:T(8,128)(2,1)} %get-tuple-element.53.xs_own, bf16[288,1024]{1,0:T(8,128)(2,1)} %get-tuple-element.54.xs_other, ...), custom_call_target="tpu_custom_call" | custom-call | tf_op jit(solution)/shard_map/pallas_call | solution.py:179
  89.8 1.3 %collective-permute-start.3 = (bf16[256,1024]{1,0:T(8,128)(2,1)}, bf16[256,1024]{1,0:T(8,128)(2,1)S(1)}, u32[]{:S(2)}, u32[]{:S(2)}) collective-permute-start(bf16[256,1024]{1,0:T(8,128)(2,1)} %get-tuple-element.57), channel_id=1, source_target_pairs={{0,1},{1,2},{2,3},{3,0},{4,5},{5,6},{6,7},{7,4},{8,9},{9,10},{10,1... | collective-permute-start | bytes 1572872 | tf_op jit(solution)/shard_map/ppermute | solution.py:202
  91.1 1.9 %collective-permute-start.4 = (bf16[256,1024]{1,0:T(8,128)(2,1)}, bf16[256,1024]{1,0:T(8,128)(2,1)S(1)}, u32[]{:S(2)}, u32[]{:S(2)}) collective-permute-start(bf16[256,1024]{1,0:T(8,128)(2,1)} %get-tuple-element.58), channel_id=1, source_target_pairs={{0,3},{1,0},{2,1},{3,2},{4,7},{5,4},{6,5},{7,6},{8,11},{9,8},{10,9... | collective-permute-start | bytes 1572872 | tf_op jit(solution)/shard_map/ppermute | solution.py:202
  93.2 3.1 %collective-permute-start.6 = (bf16[128,1024]{1,0:T(8,128)(2,1)S(1)}, bf16[128,1024]{1,0:T(8,128)(2,1)S(1)}, u32[]{:S(2)}, u32[]{:S(2)}) collective-permute-start(bf16[128,1024]{1,0:T(8,128)(2,1)S(1)} %copy-done.11), channel_id=1, source_target_pairs={{0,3},{1,0},{2,1},{3,2},{4,7},{5,4},{6,5},{7,6},{8,11},{9,8},{10,9... | collective-permute-start | bytes 786440 | tf_op jit(solution)/shard_map/ppermute | solution.py:202
  96.3 14.1 %collective-permute-done.5.left2 = bf16[128,1024]{1,0:T(8,128)(2,1)S(1)} collective-permute-done((bf16[128,1024]{1,0:T(8,128)(2,1)S(1)}, bf16[128,1024]{1,0:T(8,128)(2,1)S(1)}, u32[]{:S(2)}, u32[]{:S(2)}) %collective-permute-start.5) | collective-permute-done | bytes 262176 | tf_op jit(solution)/shard_map/ppermute | solution.py:202
  111.2 2.5 %shard_map.108 = bf16[256,1024]{1,0:T(8,128)(2,1)} custom-call(bf16[256,1024]{1,0:T(8,128)(2,1)} %get-tuple-element.59.own, bf16[256,1024]{1,0:T(8,128)(2,1)} %copy-done.3, bf16[256,1024]{1,0:T(8,128)(2,1)} %copy-done.5, bf16[128,1024]{1,0:T(8,128)(2,1)} %copy-done.9, bf16[128,1024]{1,0:T(8,128)(2,1)} %copy-done.10), custom_call_target="tpu_custom_call" | custom-call | tf_op jit(solution)/shard_map/pallas_call | solution.py:179
  114.7 2.2 %shard_map.109 = (bf16[128,1024]{1,0:T(8,128)(2,1)}, bf16[128,1024]{1,0:T(8,128)(2,1)}) custom-call(bf16[128,1024]{1,0:T(8,128)(2,1)} %get-tuple-element.56.fwd2, bf16[256,1024]{1,0:T(8,128)(2,1)} %copy-done.2, bf16[128,1024]{1,0:T(8,128)(2,1)} %get-tuple-element.61.bwd2, bf16[256,1024]{1,0:T(8,128)(2,1)} %copy-done.4), custom_call_target="tpu_custom_call" | custom-call | tf_op jit(solution)/shard_map/pallas_call | solution.py:179
  117.5 2.6 %collective-permute-start.8 = (bf16[128,1024]{1,0:T(8,128)(2,1)}, bf16[128,1024]{1,0:T(8,128)(2,1)S(1)}, u32[]{:S(2)}, u32[]{:S(2)}) collective-permute-start(bf16[128,1024]{1,0:T(8,128)(2,1)} %get-tuple-element.64), channel_id=1, source_target_pairs={{0,3},{1,0},{2,1},{3,2},{4,7},{5,4},{6,5},{7,6},{8,11},{9,8},{10,9... | collective-permute-start | bytes 786440 | tf_op jit(solution)/shard_map/ppermute | solution.py:202
  121.0 2.4 %shard_map.110 = (bf16[256,1024]{1,0:T(8,128)(2,1)}, bf16[256]{0:T(256)(128)(2,1)}) custom-call(bf16[32,10,8,128]{3,2,1,0:T(8,128)(2,1)} %copy-done.1, bf16[256]{0:T(256)(128)(2,1)} %gate_ref.3, s32[256]{0:T(256)} %expert_ref.3, s32[256]{0:T(256)} %slot_ref.3), custom_call_target="tpu_custom_call" | custom-call | tf_op jit(solution)/shard_map/pallas_call | solution.py:179
  123.4 1.9 %collective-permute-done.7.left2 = bf16[128,1024]{1,0:T(8,128)(2,1)S(1)} collective-permute-done((bf16[128,1024]{1,0:T(8,128)(2,1)}, bf16[128,1024]{1,0:T(8,128)(2,1)S(1)}, u32[]{:S(2)}, u32[]{:S(2)}) %collective-permute-start.7) | collective-permute-done | bytes 262176 | tf_op jit(solution)/shard_map/ppermute | solution.py:202
  126.2 2.5 %shard_map.111 = bf16[256,1024]{1,0:T(8,128)(2,1)} custom-call(bf16[256,1024]{1,0:T(8,128)(2,1)} %get-tuple-element.70.own, bf16[256,1024]{1,0:T(8,128)(2,1)} %copy-done.2, bf16[256,1024]{1,0:T(8,128)(2,1)} %copy-done.4, bf16[128,1024]{1,0:T(8,128)(2,1)} %copy-done.7, bf16[128,1024]{1,0:T(8,128)(2,1)} %copy-done.8), custom_call_target="tpu_custom_call" | custom-call | tf_op jit(solution)/shard_map/pallas_call | solution.py:179
  (37 shorter events, 6.1 us)
Async XLA Ops:
  3.5 42.6 %all-to-all-start = ((bf16[32,18,8,128]{3,2,1,0:T(8,128)(2,1)}), bf16[32,18,8,128]{3,2,1,0:T(8,128)(2,1)S(1)}, u32[]{:S(2)}, u32[]{:S(2)}) async-start(bf16[32,18,8,128]{3,2,1,0:T(8,128)(2,1)} %shard_map.102), calls=%async_computation | async-start | bytes 2359296 | tf_op jit(solution)/shard_map/all_to_all | solution.py:214
  46.0 1.1 copy-start
  46.0 6.2 %collective-permute-start = (bf16[32,18,8,128]{3,2,1,0:T(8,128)(2,1)S(1)}, bf16[32,18,8,128]{3,2,1,0:T(8,128)(2,1)S(1)}, u32[]{:S(2)}, u32[]{:S(2)}) collective-permute-start(bf16[32,18,8,128]{3,2,1,0:T(8,128)(2,1)S(1)} %all-to-all-done.raw_ref), channel_id=1, source_target_pairs={{0,4},{4,0},{1,5},{5,1},{2,6},{6,2},{3,7},{7,3},{8,12},{12,8},{9,1... | collective-permute-start | bytes 3538952 | tf_op jit(solution)/shard_map/ppermute | solution.py:241
  52.3 1.0 copy-start.6
  66.4 3.2 %collective-permute-start.9 = (bf16[32,10,8,128]{3,2,1,0:T(8,128)(2,1)}, bf16[32,10,8,128]{3,2,1,0:T(8,128)(2,1)S(1)}, u32[]{:S(2)}, u32[]{:S(2)}) collective-permute-start(bf16[32,10,8,128]{3,2,1,0:T(8,128)(2,1)} %get-tuple-element.66), channel_id=1, source_target_pairs={{0,4},{4,0},{1,5},{5,1},{2,6},{6,2},{3,7},{7,3},{8,12},{12,8},{9,1... | collective-permute-start | bytes 1966088 | tf_op jit(solution)/shard_map/ppermute | solution.py:273
  66.4 15.8 %collective-permute-start.1 = (bf16[256,1024]{1,0:T(8,128)(2,1)}, bf16[256,1024]{1,0:T(8,128)(2,1)S(1)}, u32[]{:S(2)}, u32[]{:S(2)}) collective-permute-start(bf16[256,1024]{1,0:T(8,128)(2,1)} %get-tuple-element.48), channel_id=1, source_target_pairs={{0,1},{1,2},{2,3},{3,0},{4,5},{5,6},{6,7},{7,4},{8,9},{9,10},{10,1... | collective-permute-start | bytes 1572872 | tf_op jit(solution)/shard_map/ppermute | solution.py:202
  67.9 14.3 %collective-permute-start.2 = (bf16[256,1024]{1,0:T(8,128)(2,1)}, bf16[256,1024]{1,0:T(8,128)(2,1)S(1)}, u32[]{:S(2)}, u32[]{:S(2)}) collective-permute-start(bf16[256,1024]{1,0:T(8,128)(2,1)} %get-tuple-element.50), channel_id=1, source_target_pairs={{0,3},{1,0},{2,1},{3,2},{4,7},{5,4},{6,5},{7,6},{8,11},{9,8},{10,9... | collective-permute-start | bytes 1572872 | tf_op jit(solution)/shard_map/ppermute | solution.py:202
  71.8 48.4 %all-to-all-start.1 = ((bf16[32,10,8,128]{3,2,1,0:T(8,128)(2,1)}), bf16[32,10,8,128]{3,2,1,0:T(8,128)(2,1)S(1)}, u32[]{:S(2)}, u32[]{:S(2)}) async-start(bf16[32,10,8,128]{3,2,1,0:T(8,128)(2,1)} %add_convert_fusion), calls=%async_computation.1 | async-start | bytes 1310720 | tf_op jit(solution)/shard_map/all_to_all | solution.py:214
  82.2 0.8 copy-start.3
  82.2 1.0 copy-start.5
  85.4 7.7 %copy-start.12 = (bf16[128,1024]{1,0:T(8,128)(2,1)S(1)}, bf16[128,1024]{1,0:T(8,128)(2,1)}, u32[]{:S(2)}) copy-start(bf16[128,1024]{1,0:T(8,128)(2,1)} %get-tuple-element.51) | copy-start | bytes 786436
  85.4 7.8 %copy-start.11 = (bf16[128,1024]{1,0:T(8,128)(2,1)S(1)}, bf16[128,1024]{1,0:T(8,128)(2,1)}, u32[]{:S(2)}) copy-start(bf16[128,1024]{1,0:T(8,128)(2,1)} %get-tuple-element.52) | copy-start | bytes 786436
  89.8 23.9 %collective-permute-start.3 = (bf16[256,1024]{1,0:T(8,128)(2,1)}, bf16[256,1024]{1,0:T(8,128)(2,1)S(1)}, u32[]{:S(2)}, u32[]{:S(2)}) collective-permute-start(bf16[256,1024]{1,0:T(8,128)(2,1)} %get-tuple-element.57), channel_id=1, source_target_pairs={{0,1},{1,2},{2,3},{3,0},{4,5},{5,6},{6,7},{7,4},{8,9},{9,10},{10,1... | collective-permute-start | bytes 1572872 | tf_op jit(solution)/shard_map/ppermute | solution.py:202
  91.1 22.6 %collective-permute-start.4 = (bf16[256,1024]{1,0:T(8,128)(2,1)}, bf16[256,1024]{1,0:T(8,128)(2,1)S(1)}, u32[]{:S(2)}, u32[]{:S(2)}) collective-permute-start(bf16[256,1024]{1,0:T(8,128)(2,1)} %get-tuple-element.58), channel_id=1, source_target_pairs={{0,3},{1,0},{2,1},{3,2},{4,7},{5,4},{6,5},{7,6},{8,11},{9,8},{10,9... | collective-permute-start | bytes 1572872 | tf_op jit(solution)/shard_map/ppermute | solution.py:202
  93.1 17.4 %collective-permute-start.5 = (bf16[128,1024]{1,0:T(8,128)(2,1)S(1)}, bf16[128,1024]{1,0:T(8,128)(2,1)S(1)}, u32[]{:S(2)}, u32[]{:S(2)}) collective-permute-start(bf16[128,1024]{1,0:T(8,128)(2,1)S(1)} %copy-done.12), channel_id=1, source_target_pairs={{0,1},{1,2},{2,3},{3,0},{4,5},{5,6},{6,7},{7,4},{8,9},{9,10},{10,1... | collective-permute-start | bytes 786440 | tf_op jit(solution)/shard_map/ppermute | solution.py:202
  93.2 17.2 %collective-permute-start.6 = (bf16[128,1024]{1,0:T(8,128)(2,1)S(1)}, bf16[128,1024]{1,0:T(8,128)(2,1)S(1)}, u32[]{:S(2)}, u32[]{:S(2)}) collective-permute-start(bf16[128,1024]{1,0:T(8,128)(2,1)S(1)} %copy-done.11), channel_id=1, source_target_pairs={{0,3},{1,0},{2,1},{3,2},{4,7},{5,4},{6,5},{7,6},{8,11},{9,8},{10,9... | collective-permute-start | bytes 786440 | tf_op jit(solution)/shard_map/ppermute | solution.py:202
  110.4 0.7 copy-start.9
  110.4 0.8 copy-start.10
  113.7 0.8 copy-start.2
  113.7 1.0 copy-start.4
  116.9 8.5 %collective-permute-start.7 = (bf16[128,1024]{1,0:T(8,128)(2,1)}, bf16[128,1024]{1,0:T(8,128)(2,1)S(1)}, u32[]{:S(2)}, u32[]{:S(2)}) collective-permute-start(bf16[128,1024]{1,0:T(8,128)(2,1)} %get-tuple-element.63), channel_id=1, source_target_pairs={{0,1},{1,2},{2,3},{3,0},{4,5},{5,6},{6,7},{7,4},{8,9},{9,10},{10,1... | collective-permute-start | bytes 786440 | tf_op jit(solution)/shard_map/ppermute | solution.py:202
  117.5 7.9 %collective-permute-start.8 = (bf16[128,1024]{1,0:T(8,128)(2,1)}, bf16[128,1024]{1,0:T(8,128)(2,1)S(1)}, u32[]{:S(2)}, u32[]{:S(2)}) collective-permute-start(bf16[128,1024]{1,0:T(8,128)(2,1)} %get-tuple-element.64), channel_id=1, source_target_pairs={{0,3},{1,0},{2,1},{3,2},{4,7},{5,4},{6,5},{7,6},{8,11},{9,8},{10,9... | collective-permute-start | bytes 786440 | tf_op jit(solution)/shard_map/ppermute | solution.py:202
  120.1 0.8 copy-start.1
  125.4 0.8 copy-start.8
  (1 other events, 0.7 us)

commit v4 on v1

--- a/solution.py
+++ b/solution.py
@@ -41,10 +41,10 @@
 def pack_kernel(x_ref, g_ref, gate_ref, expert_ref, slot_ref, out_ref, full, turn):
     groups = out_ref.shape[0]
     count = x_ref.shape[0]
-    place = slot_row(expert_ref[...], slot_ref[...], groups)
+    place = slot_row(expert_ref[...], slot_ref[...], groups).reshape(1, count)
     rows = lax.broadcasted_iota(jnp.int32, (9 * groups, count), 0)
     hit = rows == place
-    gate = gate_ref[...].astype(F32)
+    gate = gate_ref[...].astype(F32).reshape(1, count)
     for side, (ref, scale) in enumerate(((x_ref, 1.0), (g_ref, gate))):
         pick = jnp.where(hit, scale, 0.0).astype(BF)
         full[...] = matmul(pick, ref[...], ((1,), (0,)))
@@ -77,16 +77,14 @@
     own[...] = chunk(0)
 
 
-def expert_kernel(
-    mine_ref, other_ref, up_ref, down_ref, xs, dh, gate, fwd1, bwd1, fwd2, bwd2, own, ds, act, hid, dact, turn
-):
+def unpacked(mine_ref, other_ref, xs, ds, turn):
     groups = mine_ref.shape[0]
-    rows = 9 * groups
     for part, ref in enumerate((mine_ref, other_ref)):
-        from_tiles(ref, 0, xs, part * rows, groups, turn)
-        from_tiles(ref, 9, ds, part * rows, groups, turn)
-    hid[...] = matmul(xs[...], up_ref[0], ((1,), (0,)))
-    dact[...] = matmul(ds[...], down_ref[0], ((1,), (1,)))
+        from_tiles(ref, 0, xs, part * 9 * groups, groups, turn)
+        from_tiles(ref, 9, ds, part * 9 * groups, groups, turn)
+
+
+def activation(hid, dact, act, dh, gate):
     step = 32
 
     def block(i, carry):
@@ -102,15 +100,10 @@
         gate[at, :] = jnp.broadcast_to(total, (step, LANES))
         return carry
 
-    lax.fori_loop(0, 2 * rows // step, block, 0)
-    weight_parts(act, ds[...], lax.axis_index("dp"), fwd1, bwd1, fwd2, bwd2, own)
-
-
-def up_kernel(xs, dh, fwd1, bwd1, fwd2, bwd2, own):
-    weight_parts(xs, dh[...], lax.axis_index("dp"), fwd1, bwd1, fwd2, bwd2, own)
-
-
-def input_kernel(dh, gate, up_ref, mine_ref, other_ref, full, turn):
+    lax.fori_loop(0, hid.shape[0] // step, block, 0)
+
+
+def returned(dh, gate, up_ref, mine_ref, other_ref, full, turn):
     groups = mine_ref.shape[0]
     rows = 9 * groups
     full[...] = matmul(dh[...], up_ref[0], ((1,), (1,)))
@@ -127,11 +120,27 @@
         ref[:, 9] = jnp.where(lane < 64, first, turn[...]).astype(BF)
 
 
+def expert_kernel(
+    mine_ref, other_ref, up_ref, down_ref, xs, dh, keep, give, fwd1, bwd1, fwd2, bwd2, own, gate, ds, act, hid, dact, turn
+):
+    unpacked(mine_ref, other_ref, xs, ds, turn)
+    hid[...] = matmul(xs[...], up_ref[0], ((1,), (0,)))
+    dact[...] = matmul(ds[...], down_ref[0], ((1,), (1,)))
+    activation(hid, dact, act, dh, gate)
+    weight_parts(act, ds[...], lax.axis_index("dp"), fwd1, bwd1, fwd2, bwd2, own)
+    returned(dh, gate, up_ref, keep, give, hid, turn)
+
+
+def up_kernel(xs, dh, fwd1, bwd1, fwd2, bwd2, own):
+    weight_parts(xs, dh[...], lax.axis_index("dp"), fwd1, bwd1, fwd2, bwd2, own)
+
+
 def unpack_kernel(back_ref, gate_ref, expert_ref, slot_ref, out_ref, gate_out_ref, rowbuf, turn):
     groups = back_ref.shape[0]
     count = out_ref.shape[0]
     from_tiles(back_ref, 0, rowbuf, 0, groups, turn)
-    expert, slot = expert_ref[...], slot_ref[...]
+    expert = expert_ref[...].reshape(1, count)
+    slot = slot_ref[...].reshape(1, count)
     rows = lax.broadcasted_iota(jnp.int32, (9 * groups, count), 0)
     pick = jnp.where(rows == slot_row(expert, slot, groups), 1.0, 0.0).astype(BF)
     out_ref[...] = matmul(pick, rowbuf[...], ((0,), (0,))).astype(BF)
@@ -142,7 +151,8 @@
     low = matmul(gates, low, ((0,), (0,)))
     high = matmul(gates, high, ((0,), (0,)))
     total = low[0:1, :] + high[64:65, :]
-    gate_out_ref[...] = (total / gate_ref[...].astype(F32)).astype(BF)
+    gate = gate_ref[...].astype(F32).reshape(1, count)
+    gate_out_ref[...] = (total / gate).astype(BF).reshape(count)
 
 
 def call(kernel, out, scratch, *args):
@@ -161,21 +171,33 @@
     return jax.ShapeDtypeStruct(dims, dtype)
 
 
-def scattered(parts):
-    fwd1, bwd1, fwd2, bwd2, own = parts
-    half = fwd2.shape[0]
-    ahead = [(i, (i + 1) % 4) for i in range(4)]
-    behind = [(i, (i + 3) % 4) for i in range(4)]
-    left = lax.ppermute(fwd1, "dp", ahead)
-    right = lax.ppermute(bwd1, "dp", behind)
-    fwd2 = (fwd2.astype(F32) + left[:half].astype(F32)).astype(BF)
-    bwd2 = (bwd2.astype(F32) + right[half:].astype(F32)).astype(BF)
-    left2 = lax.ppermute(fwd2, "dp", ahead)
-    right2 = lax.ppermute(bwd2, "dp", behind)
-    wide = own.astype(F32)
-    low = wide[:half] + right[:half].astype(F32) + left2.astype(F32)
-    high = wide[half:] + left[half:].astype(F32) + right2.astype(F32)
-    return jnp.concatenate([low, high], axis=0).astype(BF)
+AHEAD = [(i, (i + 1) % 4) for i in range(4)]
+BEHIND = [(i, (i + 3) % 4) for i in range(4)]
+
+
+def ring(fwd, bwd):
+    return lax.ppermute(fwd, "dp", AHEAD), lax.ppermute(bwd, "dp", BEHIND)
+
+
+def second(parts, left, right):
+    half = parts[2].shape[0]
+    fwd = (parts[2].astype(F32) + left[:half].astype(F32)).astype(BF)
+    bwd = (parts[3].astype(F32) + right[half:].astype(F32)).astype(BF)
+    return fwd, bwd
+
+
+def total(own, left, right, left2, right2):
+    half, columns = left2.shape
+    split = lambda a: a.reshape(2, half, columns)
+    both = lambda a: jnp.broadcast_to(a[None], (2, half, columns))
+    low = lax.broadcasted_iota(jnp.int32, (2, half, columns), 0) == 0
+    first = jnp.where(low, split(right), split(left)).astype(F32)
+    then = jnp.where(low, both(left2), both(right2)).astype(F32)
+    return (split(own).astype(F32) + first + then).astype(BF).reshape(2 * half, columns)
+
+
+def after(value, earlier):
+    return lax.optimization_barrier((value, earlier))[0]
 
 
 def on_device(tokens_in, out_grad, gates, expert_ids, slot_ids, w_up, w_down):
@@ -183,9 +205,6 @@
     count, width = tokens_in.shape
     hidden = w_up.shape[2]
     rows = 9 * groups
-    expert_ids = expert_ids.reshape(1, count)
-    slot_ids = slot_ids.reshape(1, count)
-    gates = gates.reshape(1, count)
     turn = pltpu.VMEM((groups, 8, LANES), F32)
     swap = [(0, 1), (1, 0)]
     sent = call(
@@ -211,12 +230,12 @@
             shape(quarter, columns),
         )
 
-    xs, dh, gate, *down = call(
+    with jax.named_scope("expert_input"):
+      xs, dh, keep, give, *down = call(
         expert_kernel,
-        (shape(2 * rows, width), shape(2 * rows, hidden), shape(2 * rows, LANES, dtype=F32))
+        (shape(2 * rows, width), shape(2 * rows, hidden), shape(groups, 10, 8, LANES), shape(groups, 10, 8, LANES))
         + parts(hidden, width),
-        [
-            pltpu.VMEM((2 * rows, width), BF),
+        [pltpu.VMEM((2 * rows, LANES), F32), pltpu.VMEM((2 * rows, width), BF),
             pltpu.VMEM((2 * rows, hidden), BF),
             pltpu.VMEM((2 * rows, hidden), F32),
             pltpu.VMEM((2 * rows, hidden), F32),
@@ -226,31 +245,38 @@
         other,
         w_up,
         w_down,
-    )
-    up = call(up_kernel, parts(width, hidden), [], xs, dh)
-    keep, give = call(
-        input_kernel,
-        (shape(groups, 10, 8, LANES), shape(groups, 10, 8, LANES)),
-        [pltpu.VMEM((2 * rows, width), F32), turn],
-        dh,
-        gate,
-        w_up,
-    )
-    got = lax.ppermute(give, "core", swap)
+      )
+    with jax.named_scope("swap_back"):
+      got = lax.ppermute(give, "core", swap)
     both = (keep.astype(F32) + got.astype(F32)).astype(BF)
-    back = lax.all_to_all(both, "chip", split_axis=0, concat_axis=0, tiled=True)
-    down_grad = scattered(down)
-    up_grad = scattered(up)
-    in_grad, gate_grad = call(
-        unpack_kernel,
-        (shape(count, width), shape(1, count)),
-        [pltpu.VMEM((rows, width), BF), turn],
-        back,
-        gates,
-        expert_ids,
-        slot_ids,
-    )
-    return (in_grad, gate_grad.reshape(count), up_grad[None], down_grad[None])
+    with jax.named_scope("rows_back"):
+      back = lax.all_to_all(both, "chip", split_axis=0, concat_axis=0, tiled=True)
+    with jax.named_scope("unpack"):
+      in_grad, gate_grad = call(
+          unpack_kernel,
+          (shape(count, width), shape(count)),
+          [pltpu.VMEM((rows, width), BF), turn],
+          back,
+          gates,
+          expert_ids,
+          slot_ids,
+      )
+    with jax.named_scope("down_one"):
+      left_d, right_d = ring(down[0], down[1])
+    down2 = second(down, left_d, right_d)
+    with jax.named_scope("down_two"):
+      left_d2, right_d2 = ring(*down2)
+    with jax.named_scope("up"):
+      up = call(up_kernel, parts(width, hidden), [], xs, dh)
+    down_grad = total(down[4], left_d, right_d, left_d2, right_d2)
+    with jax.named_scope("up_one"):
+      left_u, right_u = ring(up[0], up[1])
+    up2 = second(up, left_u, right_u)
+    with jax.named_scope("up_two"):
+      left_u2, right_u2 = ring(*up2)
+    left_u2, right_u2, down_grad = lax.optimization_barrier((left_u2, right_u2, down_grad))
+    up_grad = total(up[4], left_u, right_u, left_u2, right_u2)
+    return (in_grad, gate_grad, up_grad[None], down_grad[None])
 
 
 def solution(mesh):

time: 114 us -> 108 us (0.947)
  other arithmetic: 11.5 us -> 3.9 us
  waiting for transfers between devices: 13.8 us -> 17.7 us
  Pallas kernels: 24.9 us -> 22 us
    ppermute x8, waiting for transfers between devices: 7.44 us -> 14.8 us  [ring(): return (lax.ppermute(fwd, 'dp', AHEAD), lax.ppermute(bwd, 'dp', BEHIND))]
    concatenate x4 -> x0, other arithmetic: 4.19 us -> none  [scattered(): return jnp.concatenate([low, high], axis=0).astype(BF)]
    all_to_all x1, waiting for transfers between devices: 3.47 us -> 0.01 us  [on_device(): back = lax.all_to_all(both, 'chip', split_axis=0, concat_axis=0, tiled=True)]
    pallas_call x5 -> x4, Pallas kernels: 24.9 us -> 22 us  [call(): pl.pallas_call(kernel, out_shape=out, in_specs=[whole] * len(args), out_s...]
    convert_element_type x6, other arithmetic: 5.07 us -> 2.86 us  [the longest x2 2.6 us: total(): (split(own).astype(F32) + first + then).astype(BF)]
    reshape x1 -> x0, local copies, waits for them, and re-layouts: 1.2 us -> none  [on_device(): gates = gates.reshape(1, count)]
    pallas_call x1 -> x0, other arithmetic: 1.18 us -> none  [call(): pl.pallas_call(kernel, out_shape=out, in_specs=[whole] * len(args), out_s...]
  transfers between devices with their start and end apart: 11 -> 11, of which waited for: 6 -> 7; matrix products, arithmetic and copies ran while one was open for 9% -> 4% of each run, Pallas kernels for 8% -> 4%
where the time goes in v4:
time: 108 us; the launch traced here: 107 us
  blocking collectives  43.5 us (40%)
  Pallas kernels  22 us (20%)
  waiting for transfers between devices  17.7 us (16%)
  starting transfers between devices  16.9 us (16%)
  other arithmetic  3.9 us (4%)
  local copies, waits for them, and re-layouts  2 us (2%)
    all_to_all x1, blocking collectives, on_device(): mine = lax.all_to_all(sent, 'chip', split_axis=0, concat_axis=0, tiled=True)  43.5 us
    pallas_call x4, Pallas kernels, call(): pl.pallas_call(kernel, out_shape=out, in_specs=[whole] * len(args), out_s...  22 us
    ppermute x8, waiting for transfers between devices, ring(): return (lax.ppermute(fwd, 'dp', AHEAD), lax.ppermute(bwd, 'dp', BEHIND))  14.8 us
    ppermute x8, starting transfers between devices, ring(): return (lax.ppermute(fwd, 'dp', AHEAD), lax.ppermute(bwd, 'dp', BEHIND))  11.8 us
    all_to_all x1, starting transfers between devices, on_device(): back = lax.all_to_all(both, 'chip', split_axis=0, concat_axis=0, tiled=True)  4.92 us
    ppermute x1, waiting for transfers between devices, on_device(): other = lax.ppermute(mine, 'core', swap)  2.84 us
    convert_element_type x2, other arithmetic, total(): (split(own).astype(F32) + first + then).astype(BF)  2.6 us
  transfers between devices with their start and end apart: 11, of which 7 were waited for; matrix products, arithmetic and copies ran while one was open for 4% of the time, Pallas kernels for 4%

profile of v4, /device:TPU:32, one launch (start us, length us, event | category | flops | bytes accessed | tf_op | source)
XLA Modules:
  0.0 106.7 jit_solution(2147242881357089558)
XLA Ops:
  0.6 2.8 %shard_map.102 = bf16[32,18,8,128]{3,2,1,0:T(8,128)(2,1)} custom-call(bf16[256,1024]{1,0:T(8,128)(2,1)} %x_ref.1, bf16[256,1024]{1,0:T(8,128)(2,1)} %g_ref.1, bf16[256]{0:T(256)(128)(2,1)} %gate_ref.3, s32[256]{0:T(256)} %expert_ref.3, s32[256]{0:T(256)} %slot_ref.3), custom_call_target="tpu_custom_call" | custom-call | tf_op jit(solution)/shard_map/pallas_call | solution.py:160
  3.4 43.5 %all_to_all.10.mine_ref = bf16[32,18,8,128]{3,2,1,0:T(8,128)(2,1)S(1)} all-to-all(bf16[32,18,8,128]{3,2,1,0:T(8,128)(2,1)} %shard_map.102), channel_id=1, replica_groups=mesh['chip'=32,'core'=2,'dp'=4] {'chip'}, dimensions={0} | all-to-all | bytes 2359296 | tf_op jit(solution)/shard_map/all_to_all | solution.py:220
  46.9 2.8 %collective-permute-done.other_ref = bf16[32,18,8,128]{3,2,1,0:T(8,128)(2,1)S(1)} collective-permute-done((bf16[32,18,8,128]{3,2,1,0:T(8,128)(2,1)S(1)}, bf16[32,18,8,128]{3,2,1,0:T(8,128)(2,1)S(1)}, u32[]{:S(2)}, u32[]{:S(2)}) %collective-permute-start) | collective-permute-done | bytes 1179680 | tf_op jit(solution)/shard_map/ppermute | solution.py:221
  49.8 1.0 copy-done.2
  50.8 12.5 %expert_input.1 = (bf16[576,1024]{1,0:T(8,128)(2,1)}, bf16[576,1024]{1,0:T(8,128)(2,1)}, bf16[32,10,8,128]{3,2,1,0:T(8,128)(2,1)}, bf16[32,10,8,128]{3,2,1,0:T(8...) custom-call(bf16[32,18,8,128]{3,2,1,0:T(8,128)(2,1)} %copy-done, ...), custom_call_target="tpu_custom_call" | custom-call | tf_op jit(solution)/shard_map/expert_input/pallas_call | solution.py:160
  63.5 1.5 %collective-permute-start.7 = (bf16[256,1024]{1,0:T(8,128)(2,1)}, bf16[256,1024]{1,0:T(8,128)(2,1)S(1)}, u32[]{:S(2)}, u32[]{:S(2)}) collective-permute-start(bf16[256,1024]{1,0:T(8,128)(2,1)} %get-tuple-element.36), channel_id=1, source_target_pairs={{0,1},{1,2},{2,3},{3,0},{4,5},{5,6},{6,7},{7,4},{8,9},{9,10},{10,1... | collective-permute-start | bytes 1572872 | tf_op jit(solution)/shard_map/down_one/ppermute | solution.py:179
  65.0 1.7 %collective-permute-start.6 = (bf16[256,1024]{1,0:T(8,128)(2,1)}, bf16[256,1024]{1,0:T(8,128)(2,1)S(1)}, u32[]{:S(2)}, u32[]{:S(2)}) collective-permute-start(bf16[256,1024]{1,0:T(8,128)(2,1)} %get-tuple-element.35), channel_id=1, source_target_pairs={{0,3},{1,0},{2,1},{3,2},{4,7},{5,4},{6,5},{7,6},{8,11},{9,8},{10,9... | collective-permute-start | bytes 1572872 | tf_op jit(solution)/shard_map/down_one/ppermute | solution.py:179
  66.7 4.3 %up.1 = (bf16[256,1024]{1,0:T(8,128)(2,1)}, bf16[256,1024]{1,0:T(8,128)(2,1)}, bf16[128,1024]{1,0:T(8,128)(2,1)}, bf16[128,1024]{1,0:T(8,128)(2,1)}, bf16[256,1024]{1,0:T(8,128)(2,1)}) custom-call(bf16[576,1024]{1,0:T(8,128)(2,1)} %get-tuple-element.27.xs, bf16[576,1024]{1,0:T(8,128)(2,1)} %get-tuple-element.28.dh), custom_call_target="tpu_custom_call" | custom-call | tf_op jit(solution)/shard_map/up/pallas_call | solution.py:160
  71.0 1.6 %collective-permute-start.2 = (bf16[256,1024]{1,0:T(8,128)(2,1)}, bf16[256,1024]{1,0:T(8,128)(2,1)S(1)}, u32[]{:S(2)}, u32[]{:S(2)}) collective-permute-start(bf16[256,1024]{1,0:T(8,128)(2,1)} %get-tuple-element.30), channel_id=1, source_target_pairs={{0,3},{1,0},{2,1},{3,2},{4,7},{5,4},{6,5},{7,6},{8,11},{9,8},{10,9... | collective-permute-start | bytes 1572872 | tf_op jit(solution)/shard_map/up_one/ppermute | solution.py:179
  72.6 0.5 collective-permute-start.3
  73.0 1.0 add_convert_fusion
  74.1 4.9 %all-to-all-start.1 = ((bf16[32,10,8,128]{3,2,1,0:T(8,128)(2,1)}), bf16[32,10,8,128]{3,2,1,0:T(8,128)(2,1)S(1)}, u32[]{:S(2)}, u32[]{:S(2)}) async-start(bf16[32,10,8,128]{3,2,1,0:T(8,128)(2,1)} %add_convert_fusion), calls=%async_computation.1 | async-start | bytes 1310720 | tf_op jit(solution)/shard_map/rows_back/all_to_all | solution.py:253
  79.0 0.6 collective-permute-done.7
  80.2 3.0 %collective-permute-start.9 = (bf16[128,1024]{1,0:T(8,128)(2,1)S(1)}, bf16[128,1024]{1,0:T(8,128)(2,1)S(1)}, u32[]{:S(2)}, u32[]{:S(2)}) collective-permute-start(bf16[128,1024]{1,0:T(8,128)(2,1)S(1)} %add_convert_fusion.3), channel_id=1, source_target_pairs={{0,3},{1,0},{2,1},{3,2},{4,7},{5,4},{6,5},{7,6},{8,11},{9,8},{10,9... | collective-permute-start | bytes 786440 | tf_op jit(solution)/shard_map/down_two/ppermute | solution.py:179
  83.2 8.0 %collective-permute-done.2 = bf16[256,1024]{1,0:T(8,128)(2,1)S(1)} collective-permute-done((bf16[256,1024]{1,0:T(8,128)(2,1)}, bf16[256,1024]{1,0:T(8,128)(2,1)S(1)}, u32[]{:S(2)}, u32[]{:S(2)}) %collective-permute-start.2) | collective-permute-done | bytes 524320 | tf_op jit(solution)/shard_map/up_one/ppermute | solution.py:179
  91.3 3.0 %collective-permute-start.5 = (bf16[128,1024]{1,0:T(8,128)(2,1)S(1)}, bf16[128,1024]{1,0:T(8,128)(2,1)S(1)}, u32[]{:S(2)}, u32[]{:S(2)}) collective-permute-start(bf16[128,1024]{1,0:T(8,128)(2,1)S(1)} %add_convert_fusion.5), channel_id=1, source_target_pairs={{0,3},{1,0},{2,1},{3,2},{4,7},{5,4},{6,5},{7,6},{8,11},{9,8},{10,9... | collective-permute-start | bytes 786440 | tf_op jit(solution)/shard_map/up_two/ppermute | solution.py:179
  94.6 1.4 %collective-permute-done.8 = bf16[128,1024]{1,0:T(8,128)(2,1)S(1)} collective-permute-done((bf16[128,1024]{1,0:T(8,128)(2,1)S(1)}, bf16[128,1024]{1,0:T(8,128)(2,1)S(1)}, u32[]{:S(2)}, u32[]{:S(2)}) %collective-permute-start.8) | collective-permute-done | bytes 262176 | tf_op jit(solution)/shard_map/down_two/ppermute | solution.py:179
  96.0 0.9 collective-permute-done.9
  96.8 1.3 %add_convert_fusion.2 = bf16[256,1024]{1,0:T(8,128)(2,1)} fusion(bf16[256,1024]{1,0:T(8,128)(2,1)S(1)} %copy-done.4, bf16[256,1024]{1,0:T(8,128)(2,1)S(1)} %collective-permute-done.6, bf16[256,1024]{1,0:T(8,128)(2,1)S(1)} %collective-permute-done.7, pred[256]{0:T(512)(128)(4,1)S(1)} %broadcast_bitcast_fusion, ...), kind=kLoop, calls=%fused_computation.2 | loop fusion | flops 2097152 | bytes 2621696 | tf_op jit(solution)/shard_map/convert_element_type | solution.py:196
  98.1 3.4 %collective-permute-done.5 = bf16[128,1024]{1,0:T(8,128)(2,1)S(1)} collective-permute-done((bf16[128,1024]{1,0:T(8,128)(2,1)S(1)}, bf16[128,1024]{1,0:T(8,128)(2,1)S(1)}, u32[]{:S(2)}, u32[]{:S(2)}) %collective-permute-start.5) | collective-permute-done | bytes 262176 | tf_op jit(solution)/shard_map/up_two/ppermute | solution.py:179
  101.6 0.5 collective-permute-done.4
  102.1 1.3 %fusion = bf16[1,256,1024]{2,1,0:T(8,128)(2,1)} fusion(bf16[256,1024]{1,0:T(8,128)(2,1)S(1)} %copy-done.5, bf16[256,1024]{1,0:T(8,128)(2,1)S(1)} %collective-permute-done.2, bf16[256,1024]{1,0:T(8,128)(2,1)S(1)} %collective-permute-done.3, pred[256]{0:T(512)(128)(4,1)S(1)} %broadcast_bitcast_fusion, bf16[128,1024]{1,0:T(8,128)(2,1)S(1)} %collective-permute-done.5, ...), kind=kLoop, calls=%fused_computation.3 | loop fusion | flops 2097152 | bytes 2621696 | tf_op jit(solution)/shard_map/convert_element_type | solution.py:196
  103.4 0.9 copy-done.1
  104.2 2.4 %unpack.1 = (bf16[256,1024]{1,0:T(8,128)(2,1)}, bf16[256]{0:T(256)(128)(2,1)}) custom-call(bf16[32,10,8,128]{3,2,1,0:T(8,128)(2,1)} %copy-done.1, bf16[256]{0:T(256)(128)(2,1)} %gate_ref.3, s32[256]{0:T(256)} %expert_ref.3, s32[256]{0:T(256)} %slot_ref.3), custom_call_target="tpu_custom_call" | custom-call | tf_op jit(solution)/shard_map/unpack/pallas_call | solution.py:160
  (32 shorter events, 1.0 us)
Async XLA Ops:
  46.9 2.9 %copy-start = (bf16[32,18,8,128]{3,2,1,0:T(8,128)(2,1)}, bf16[32,18,8,128]{3,2,1,0:T(8,128)(2,1)S(1)}, u32[]{:S(2)}) copy-start(bf16[32,18,8,128]{3,2,1,0:T(8,128)(2,1)S(1)} %all_to_all.10.mine_ref) | copy-start | bytes 3538948
  46.9 2.8 %collective-permute-start = (bf16[32,18,8,128]{3,2,1,0:T(8,128)(2,1)S(1)}, bf16[32,18,8,128]{3,2,1,0:T(8,128)(2,1)S(1)}, u32[]{:S(2)}, u32[]{:S(2)}) collective-permute-start(bf16[32,18,8,128]{3,2,1,0:T(8,128)(2,1)S(1)} %all_to_all.10.mine_ref), channel_id=1, source_target_pairs={{0,4},{4,0},{1,5},{5,1},{2,6},{6,2},{3,7},{7,3},{8,12},{12,8},{9,1... | collective-permute-start | bytes 3538952 | tf_op jit(solution)/shard_map/ppermute | solution.py:221
  49.8 1.0 copy-start.2
  63.3 9.8 %copy-start.3 = (bf16[32,10,8,128]{3,2,1,0:T(8,128)(2,1)S(1)}, bf16[32,10,8,128]{3,2,1,0:T(8,128)(2,1)}, u32[]{:S(2)}) copy-start(bf16[32,10,8,128]{3,2,1,0:T(8,128)(2,1)} %get-tuple-element.23) | copy-start | bytes 1966084
  63.3 9.8 %collective-permute-start.1 = (bf16[32,10,8,128]{3,2,1,0:T(8,128)(2,1)}, bf16[32,10,8,128]{3,2,1,0:T(8,128)(2,1)S(1)}, u32[]{:S(2)}, u32[]{:S(2)}) collective-permute-start(bf16[32,10,8,128]{3,2,1,0:T(8,128)(2,1)} %get-tuple-element.24), channel_id=1, source_target_pairs={{0,4},{4,0},{1,5},{5,1},{2,6},{6,2},{3,7},{7,3},{8,12},{12,8},{9,1... | collective-permute-start | bytes 1966088 | tf_op jit(solution)/shard_map/swap_back/ppermute | solution.py:250
  63.5 16.2 %collective-permute-start.7 = (bf16[256,1024]{1,0:T(8,128)(2,1)}, bf16[256,1024]{1,0:T(8,128)(2,1)S(1)}, u32[]{:S(2)}, u32[]{:S(2)}) collective-permute-start(bf16[256,1024]{1,0:T(8,128)(2,1)} %get-tuple-element.36), channel_id=1, source_target_pairs={{0,1},{1,2},{2,3},{3,0},{4,5},{5,6},{6,7},{7,4},{8,9},{9,10},{10,1... | collective-permute-start | bytes 1572872 | tf_op jit(solution)/shard_map/down_one/ppermute | solution.py:179
  65.0 15.1 %collective-permute-start.6 = (bf16[256,1024]{1,0:T(8,128)(2,1)}, bf16[256,1024]{1,0:T(8,128)(2,1)S(1)}, u32[]{:S(2)}, u32[]{:S(2)}) collective-permute-start(bf16[256,1024]{1,0:T(8,128)(2,1)} %get-tuple-element.35), channel_id=1, source_target_pairs={{0,3},{1,0},{2,1},{3,2},{4,7},{5,4},{6,5},{7,6},{8,11},{9,8},{10,9... | collective-permute-start | bytes 1572872 | tf_op jit(solution)/shard_map/down_one/ppermute | solution.py:179
  71.0 20.2 %collective-permute-start.2 = (bf16[256,1024]{1,0:T(8,128)(2,1)}, bf16[256,1024]{1,0:T(8,128)(2,1)S(1)}, u32[]{:S(2)}, u32[]{:S(2)}) collective-permute-start(bf16[256,1024]{1,0:T(8,128)(2,1)} %get-tuple-element.30), channel_id=1, source_target_pairs={{0,3},{1,0},{2,1},{3,2},{4,7},{5,4},{6,5},{7,6},{8,11},{9,8},{10,9... | collective-permute-start | bytes 1572872 | tf_op jit(solution)/shard_map/up_one/ppermute | solution.py:179
  72.6 21.8 %collective-permute-start.3 = (bf16[256,1024]{1,0:T(8,128)(2,1)}, bf16[256,1024]{1,0:T(8,128)(2,1)S(1)}, u32[]{:S(2)}, u32[]{:S(2)}) collective-permute-start(bf16[256,1024]{1,0:T(8,128)(2,1)} %get-tuple-element.31), channel_id=1, source_target_pairs={{0,1},{1,2},{2,3},{3,0},{4,5},{5,6},{6,7},{7,4},{8,9},{9,10},{10,1... | collective-permute-start | bytes 1572872 | tf_op jit(solution)/shard_map/up_one/ppermute | solution.py:179
  73.0 6.6 %copy-start.8 = (bf16[128,1024]{1,0:T(8,128)(2,1)S(1)}, bf16[128,1024]{1,0:T(8,128)(2,1)}, u32[]{:S(2)}) copy-start(bf16[128,1024]{1,0:T(8,128)(2,1)} %get-tuple-element.37) | copy-start | bytes 786436
  74.1 6.0 %copy-start.6 = (bf16[128,1024]{1,0:T(8,128)(2,1)S(1)}, bf16[128,1024]{1,0:T(8,128)(2,1)}, u32[]{:S(2)}) copy-start(bf16[128,1024]{1,0:T(8,128)(2,1)} %get-tuple-element.38) | copy-start | bytes 786436
  74.1 17.1 %copy-start.9 = (bf16[128,1024]{1,0:T(8,128)(2,1)S(1)}, bf16[128,1024]{1,0:T(8,128)(2,1)}, u32[]{:S(2)}) copy-start(bf16[128,1024]{1,0:T(8,128)(2,1)} %get-tuple-element.33) | copy-start | bytes 786436
  74.1 29.3 %all-to-all-start.1 = ((bf16[32,10,8,128]{3,2,1,0:T(8,128)(2,1)}), bf16[32,10,8,128]{3,2,1,0:T(8,128)(2,1)S(1)}, u32[]{:S(2)}, u32[]{:S(2)}) async-start(bf16[32,10,8,128]{3,2,1,0:T(8,128)(2,1)} %add_convert_fusion), calls=%async_computation.1 | async-start | bytes 1310720 | tf_op jit(solution)/shard_map/rows_back/all_to_all | solution.py:253
  79.0 15.3 %copy-start.7 = (bf16[128,1024]{1,0:T(8,128)(2,1)S(1)}, bf16[128,1024]{1,0:T(8,128)(2,1)}, u32[]{:S(2)}) copy-start(bf16[128,1024]{1,0:T(8,128)(2,1)} %get-tuple-element.32) | copy-start | bytes 786436
  79.7 17.1 %copy-start.4 = (bf16[256,1024]{1,0:T(8,128)(2,1)S(1)}, bf16[256,1024]{1,0:T(8,128)(2,1)}, u32[]{:S(2)}) copy-start(bf16[256,1024]{1,0:T(8,128)(2,1)} %get-tuple-element.34) | copy-start | bytes 1572868
  79.8 16.2 %collective-permute-start.8 = (bf16[128,1024]{1,0:T(8,128)(2,1)S(1)}, bf16[128,1024]{1,0:T(8,128)(2,1)S(1)}, u32[]{:S(2)}, u32[]{:S(2)}) collective-permute-start(bf16[128,1024]{1,0:T(8,128)(2,1)S(1)} %add_convert_fusion.4), channel_id=1, source_target_pairs={{0,1},{1,2},{2,3},{3,0},{4,5},{5,6},{6,7},{7,4},{8,9},{9,10},{10,1... | collective-permute-start | bytes 786440 | tf_op jit(solution)/shard_map/down_two/ppermute | solution.py:179
  80.2 16.6 %collective-permute-start.9 = (bf16[128,1024]{1,0:T(8,128)(2,1)S(1)}, bf16[128,1024]{1,0:T(8,128)(2,1)S(1)}, u32[]{:S(2)}, u32[]{:S(2)}) collective-permute-start(bf16[128,1024]{1,0:T(8,128)(2,1)S(1)} %add_convert_fusion.3), channel_id=1, source_target_pairs={{0,3},{1,0},{2,1},{3,2},{4,7},{5,4},{6,5},{7,6},{8,11},{9,8},{10,9... | collective-permute-start | bytes 786440 | tf_op jit(solution)/shard_map/down_two/ppermute | solution.py:179
  91.3 10.3 %collective-permute-start.5 = (bf16[128,1024]{1,0:T(8,128)(2,1)S(1)}, bf16[128,1024]{1,0:T(8,128)(2,1)S(1)}, u32[]{:S(2)}, u32[]{:S(2)}) collective-permute-start(bf16[128,1024]{1,0:T(8,128)(2,1)S(1)} %add_convert_fusion.5), channel_id=1, source_target_pairs={{0,3},{1,0},{2,1},{3,2},{4,7},{5,4},{6,5},{7,6},{8,11},{9,8},{10,9... | collective-permute-start | bytes 786440 | tf_op jit(solution)/shard_map/up_two/ppermute | solution.py:179
  94.4 7.7 %collective-permute-start.4 = (bf16[128,1024]{1,0:T(8,128)(2,1)S(1)}, bf16[128,1024]{1,0:T(8,128)(2,1)S(1)}, u32[]{:S(2)}, u32[]{:S(2)}) collective-permute-start(bf16[128,1024]{1,0:T(8,128)(2,1)S(1)} %add_convert_fusion.6), channel_id=1, source_target_pairs={{0,1},{1,2},{2,3},{3,0},{4,5},{5,6},{6,7},{7,4},{8,9},{9,10},{10,1... | collective-permute-start | bytes 786440 | tf_op jit(solution)/shard_map/up_two/ppermute | solution.py:179
  96.8 5.2 %copy-start.5 = (bf16[256,1024]{1,0:T(8,128)(2,1)S(1)}, bf16[256,1024]{1,0:T(8,128)(2,1)}, u32[]{:S(2)}) copy-start(bf16[256,1024]{1,0:T(8,128)(2,1)} %get-tuple-element.29) | copy-start | bytes 1572868
  103.4 0.9 copy-start.1

commit v5 on v4

--- a/solution.py
+++ b/solution.py
@@ -57,31 +57,26 @@
         )
 
 
-def weight_parts(lhs_ref, rhs, me, fwd1, bwd1, fwd2, bwd2, own):
+def weight_parts(lhs_ref, rhs, me, fwd1, bwd1, fwd2, bwd2, own, held, sems):
     half = own.shape[0] // 2
     size = 2 * half
-
-    def chunk(step):
+    low, high = pl.ds(0, half), pl.ds(half, half)
+    both = pl.ds(0, size)
+    places = (
+        (2, ((low, fwd1.at[low]), (high, bwd1.at[high]))),
+        (1, ((high, fwd1.at[high]), (low, fwd2))),
+        (3, ((low, bwd1.at[low]), (high, bwd2))),
+        (0, ((both, own),)),
+    )
+    copies = []
+    for step, targets in places:
         at = pl.multiple_of(lax.rem(me + step, 4) * size, size)
-        return matmul(lhs_ref[:, pl.ds(at, size)], rhs, ((0,), (0,))).astype(BF)
-
-    far = chunk(2)
-    fwd1[:half] = far[:half]
-    bwd1[half:] = far[half:]
-    right = chunk(1)
-    fwd1[half:] = right[half:]
-    fwd2[...] = right[:half]
-    left = chunk(3)
-    bwd1[:half] = left[:half]
-    bwd2[...] = left[half:]
-    own[...] = chunk(0)
-
-
-def unpacked(mine_ref, other_ref, xs, ds, turn):
-    groups = mine_ref.shape[0]
-    for part, ref in enumerate((mine_ref, other_ref)):
-        from_tiles(ref, 0, xs, part * 9 * groups, groups, turn)
-        from_tiles(ref, 9, ds, part * 9 * groups, groups, turn)
+        held[step] = matmul(lhs_ref[:, pl.ds(at, size)], rhs, ((0,), (0,))).astype(BF)
+        for rows, target in targets:
+            copy = pltpu.make_async_copy(held.at[step, rows], target, sems.at[len(copies)])
+            copy.start()
+            copies.append(copy)
+    return copies
 
 
 def activation(hid, dact, act, dh, gate):
@@ -121,18 +116,41 @@
 
 
 def expert_kernel(
-    mine_ref, other_ref, up_ref, down_ref, xs, dh, keep, give, fwd1, bwd1, fwd2, bwd2, own, gate, ds, act, hid, dact, turn
+    mine_ref, other_hbm, up_hbm, down_hbm,
+    xs, dh, keep, give, fwd1, bwd1, fwd2, bwd2, own,
+    gate, ds, act, hid, dact, turn, other_ref, up_ref, down_ref, held, out_sems, in_sems,
 ):
-    unpacked(mine_ref, other_ref, xs, ds, turn)
+    loads = [
+        pltpu.make_async_copy(source, target, in_sems.at[n])
+        for n, (source, target) in enumerate(
+            ((other_hbm, other_ref), (up_hbm, up_ref), (down_hbm, down_ref))
+        )
+    ]
+    for load in loads:
+        load.start()
+    groups = mine_ref.shape[0]
+    rows = 9 * groups
+    from_tiles(mine_ref, 0, xs, 0, groups, turn)
+    from_tiles(mine_ref, 9, ds, 0, groups, turn)
+    loads[0].wait()
+    from_tiles(other_ref, 0, xs, rows, groups, turn)
+    from_tiles(other_ref, 9, ds, rows, groups, turn)
+    loads[1].wait()
     hid[...] = matmul(xs[...], up_ref[0], ((1,), (0,)))
+    loads[2].wait()
     dact[...] = matmul(ds[...], down_ref[0], ((1,), (1,)))
     activation(hid, dact, act, dh, gate)
-    weight_parts(act, ds[...], lax.axis_index("dp"), fwd1, bwd1, fwd2, bwd2, own)
+    me = lax.axis_index("dp")
+    stores = weight_parts(act, ds[...], me, fwd1, bwd1, fwd2, bwd2, own, held, out_sems)
     returned(dh, gate, up_ref, keep, give, hid, turn)
-
-
-def up_kernel(xs, dh, fwd1, bwd1, fwd2, bwd2, own):
-    weight_parts(xs, dh[...], lax.axis_index("dp"), fwd1, bwd1, fwd2, bwd2, own)
+    for store in stores:
+        store.wait()
+
+
+def up_kernel(xs, dh, fwd1, bwd1, fwd2, bwd2, own, held, out_sems):
+    me = lax.axis_index("dp")
+    for store in weight_parts(xs, dh[...], me, fwd1, bwd1, fwd2, bwd2, own, held, out_sems):
+        store.wait()
 
 
 def unpack_kernel(back_ref, gate_ref, expert_ref, slot_ref, out_ref, gate_out_ref, rowbuf, turn):
@@ -155,13 +173,17 @@
     gate_out_ref[...] = (total / gate).astype(BF).reshape(count)
 
 
-def call(kernel, out, scratch, *args):
-    whole = pl.BlockSpec(memory_space=pltpu.VMEM)
+def call(kernel, out, scratch, *args, far_in=(), far_out=()):
+    near = pl.BlockSpec(memory_space=pltpu.VMEM)
+    far = pl.BlockSpec(memory_space=pltpu.HBM)
+    several = isinstance(out, tuple)
+    count = len(out) if several else 1
+    specs = tuple(far if n in far_out else near for n in range(count))
     return pl.pallas_call(
         kernel,
         out_shape=out,
-        in_specs=[whole] * len(args),
-        out_specs=jax.tree.map(lambda _: whole, out),
+        in_specs=[far if n in far_in else near for n in range(len(args))],
+        out_specs=specs if several else near,
         scratch_shapes=scratch,
         compiler_params=pltpu.CompilerParams(vmem_limit_bytes=VMEM),
     )(*args)
@@ -230,27 +252,64 @@
             shape(quarter, columns),
         )
 
+    held = pltpu.VMEM((4, hidden // 4, width), BF)
+    out_sems = pltpu.SemaphoreType.DMA((7,))
     with jax.named_scope("expert_input"):
-      xs, dh, keep, give, *down = call(
-        expert_kernel,
-        (shape(2 * rows, width), shape(2 * rows, hidden), shape(groups, 10, 8, LANES), shape(groups, 10, 8, LANES))
-        + parts(hidden, width),
-        [pltpu.VMEM((2 * rows, LANES), F32), pltpu.VMEM((2 * rows, width), BF),
-            pltpu.VMEM((2 * rows, hidden), BF),
-            pltpu.VMEM((2 * rows, hidden), F32),
-            pltpu.VMEM((2 * rows, hidden), F32),
-            turn,
-        ],
-        mine,
-        other,
-        w_up,
-        w_down,
-      )
+        xs, dh, keep, give, *down = call(
+            expert_kernel,
+            (
+                shape(2 * rows, width),
+                shape(2 * rows, hidden),
+                shape(groups, 10, 8, LANES),
+                shape(groups, 10, 8, LANES),
+            )
+            + parts(hidden, width),
+            [
+                pltpu.VMEM((2 * rows, LANES), F32),
+                pltpu.VMEM((2 * rows, width), BF),
+                pltpu.VMEM((2 * rows, hidden), BF),
+                pltpu.VMEM((2 * rows, hidden), F32),
+                pltpu.VMEM((2 * rows, hidden), F32),
+                turn,
+                pltpu.VMEM((groups, 18, 8, LANES), BF),
+                pltpu.VMEM((1, width, hidden), BF),
+                pltpu.VMEM((1, hidden, width), BF),
+                held,
+                out_sems,
+                pltpu.SemaphoreType.DMA((3,)),
+            ],
+            mine,
+            other,
+            w_up,
+            w_down,
+            far_in=(1, 2, 3),
+            far_out=(4, 5, 6, 7, 8),
+        )
+    with jax.named_scope("down_one"):
+      left_d, right_d = ring(down[0], down[1])
     with jax.named_scope("swap_back"):
       got = lax.ppermute(give, "core", swap)
+    with jax.named_scope("up"):
+      up = call(
+            up_kernel,
+            parts(width, hidden),
+            [pltpu.VMEM((4, width // 4, hidden), BF), out_sems],
+            xs,
+            dh,
+            far_out=(0, 1, 2, 3, 4),
+        )
+    with jax.named_scope("up_one"):
+      left_u, right_u = ring(up[0], up[1])
     both = (keep.astype(F32) + got.astype(F32)).astype(BF)
     with jax.named_scope("rows_back"):
       back = lax.all_to_all(both, "chip", split_axis=0, concat_axis=0, tiled=True)
+    down2 = second(down, left_d, right_d)
+    with jax.named_scope("down_two"):
+      left_d2, right_d2 = ring(*down2)
+    up2 = second(up, left_u, right_u)
+    with jax.named_scope("up_two"):
+      left_u2, right_u2 = ring(*up2)
+    down_grad = total(down[4], left_d, right_d, left_d2, right_d2)
     with jax.named_scope("unpack"):
       in_grad, gate_grad = call(
           unpack_kernel,
@@ -261,19 +320,7 @@
           expert_ids,
           slot_ids,
       )
-    with jax.named_scope("down_one"):
-      left_d, right_d = ring(down[0], down[1])
-    down2 = second(down, left_d, right_d)
-    with jax.named_scope("down_two"):
-      left_d2, right_d2 = ring(*down2)
-    with jax.named_scope("up"):
-      up = call(up_kernel, parts(width, hidden), [], xs, dh)
-    down_grad = total(down[4], left_d, right_d, left_d2, right_d2)
-    with jax.named_scope("up_one"):
-      left_u, right_u = ring(up[0], up[1])
-    up2 = second(up, left_u, right_u)
-    with jax.named_scope("up_two"):
-      left_u2, right_u2 = ring(*up2)
+    left_u2, right_u2, in_grad = lax.optimization_barrier((left_u2, right_u2, in_grad))
     left_u2, right_u2, down_grad = lax.optimization_barrier((left_u2, right_u2, down_grad))
     up_grad = total(up[4], left_u, right_u, left_u2, right_u2)
     return (in_grad, gate_grad, up_grad[None], down_grad[None])

time: 108 us -> 107 us (level)
  waiting for transfers between devices: 17.7 us -> 14.5 us
  other arithmetic: 3.9 us -> 5.61 us
  Pallas kernels: 22 us -> 23.1 us
    ppermute x8, waiting for transfers between devices: 14.8 us -> 10.7 us  [ring(): return (lax.ppermute(fwd, 'dp', AHEAD), lax.ppermute(bwd, 'dp', BEHIND))]
    pallas_call x4, Pallas kernels: 22 us -> 23.1 us  [call(): pl.pallas_call(kernel, out_shape=out, in_specs=[far if n in far_in else n...]
  transfers between devices with their start and end apart: 11 -> 11, of which waited for: 7 -> 7; matrix products, arithmetic and copies ran while one was open for 4% -> 3% of each run, Pallas kernels for 4% -> 6%
where the time goes in v5:
time: 107 us; the launch traced here: 106 us
  blocking collectives  43.5 us (41%)
  Pallas kernels  23.1 us (22%)
  starting transfers between devices  16.8 us (16%)
  waiting for transfers between devices  14.5 us (14%)
  other arithmetic  5.61 us (5%)
  local copies, waits for them, and re-layouts  2 us (2%)
    all_to_all x1, blocking collectives, on_device(): mine = lax.all_to_all(sent, 'chip', split_axis=0, concat_axis=0, tiled=True)  43.5 us
    pallas_call x4, Pallas kernels, call(): pl.pallas_call(kernel, out_shape=out, in_specs=[far if n in far_in else n...  23.1 us
    ppermute x8, starting transfers between devices, ring(): return (lax.ppermute(fwd, 'dp', AHEAD), lax.ppermute(bwd, 'dp', BEHIND))  11.8 us
    ppermute x8, waiting for transfers between devices, ring(): return (lax.ppermute(fwd, 'dp', AHEAD), lax.ppermute(bwd, 'dp', BEHIND))  10.7 us
    all_to_all x1, starting transfers between devices, on_device(): back = lax.all_to_all(both, 'chip', split_axis=0, concat_axis=0, tiled=True)  4.74 us
    convert_element_type x2, other arithmetic, total(): (split(own).astype(F32) + first + then).astype(BF)  3.6 us
    ppermute x1, waiting for transfers between devices, on_device(): other = lax.ppermute(mine, 'core', swap)  2.84 us
  transfers between devices with their start and end apart: 11, of which 7 were waited for; matrix products, arithmetic and copies ran while one was open for 3% of the time, Pallas kernels for 6%

profile of v5, /device:TPU:32, one launch (start us, length us, event | category | flops | bytes accessed | tf_op | source)
XLA Modules:
  0.0 106.2 jit_solution(12582631113361563903)
XLA Ops:
  0.6 2.8 %shard_map.102 = bf16[32,18,8,128]{3,2,1,0:T(8,128)(2,1)} custom-call(bf16[256,1024]{1,0:T(8,128)(2,1)} %x_ref.1, bf16[256,1024]{1,0:T(8,128)(2,1)} %g_ref.1, bf16[256]{0:T(256)(128)(2,1)} %gate_ref.3, s32[256]{0:T(256)} %expert_ref.3, s32[256]{0:T(256)} %slot_ref.3), custom_call_target="tpu_custom_call" | custom-call | tf_op jit(solution)/shard_map/pallas_call | solution.py:182
  3.4 43.5 %all_to_all.10.mine_ref = bf16[32,18,8,128]{3,2,1,0:T(8,128)(2,1)S(1)} all-to-all(bf16[32,18,8,128]{3,2,1,0:T(8,128)(2,1)} %shard_map.102), channel_id=1, replica_groups=mesh['chip'=32,'core'=2,'dp'=4] {'chip'}, dimensions={0} | all-to-all | bytes 2359296 | tf_op jit(solution)/shard_map/all_to_all | solution.py:242
  46.9 2.8 %collective-permute-done.other_hbm = bf16[32,18,8,128]{3,2,1,0:T(8,128)(2,1)S(1)} collective-permute-done((bf16[32,18,8,128]{3,2,1,0:T(8,128)(2,1)S(1)}, bf16[32,18,8,128]{3,2,1,0:T(8,128)(2,1)S(1)}, u32[]{:S(2)}, u32[]{:S(2)}) %collective-permute-start) | collective-permute-done | bytes 1179680 | tf_op jit(solution)/shard_map/ppermute | solution.py:243
  49.8 1.0 copy-done.2
  50.8 13.6 %expert_input.1 = (bf16[576,1024]{1,0:T(8,128)(2,1)}, bf16[576,1024]{1,0:T(8,128)(2,1)}, bf16[32,10,8,128]{3,2,1,0:T(8,128)(2,1)}, bf16[32,10,8,128]{3,2,1,0:T(8...) custom-call(bf16[32,18,8,128]{3,2,1,0:T(8,128)(2,1)} %copy-done, ...), custom_call_target="tpu_custom_call" | custom-call | tf_op jit(solution)/shard_map/expert_input/pallas_call | solution.py:182
  64.6 1.5 %collective-permute-start.7 = (bf16[256,1024]{1,0:T(8,128)(2,1)}, bf16[256,1024]{1,0:T(8,128)(2,1)S(1)}, u32[]{:S(2)}, u32[]{:S(2)}) collective-permute-start(bf16[256,1024]{1,0:T(8,128)(2,1)} %get-tuple-element.42), channel_id=1, source_target_pairs={{0,1},{1,2},{2,3},{3,0},{4,5},{5,6},{6,7},{7,4},{8,9},{9,10},{10,1... | collective-permute-start | bytes 1572872 | tf_op jit(solution)/shard_map/down_one/ppermute | solution.py:201
  66.1 1.8 %collective-permute-start.6 = (bf16[256,1024]{1,0:T(8,128)(2,1)}, bf16[256,1024]{1,0:T(8,128)(2,1)S(1)}, u32[]{:S(2)}, u32[]{:S(2)}) collective-permute-start(bf16[256,1024]{1,0:T(8,128)(2,1)} %get-tuple-element.41), channel_id=1, source_target_pairs={{0,3},{1,0},{2,1},{3,2},{4,7},{5,4},{6,5},{7,6},{8,11},{9,8},{10,9... | collective-permute-start | bytes 1572872 | tf_op jit(solution)/shard_map/down_one/ppermute | solution.py:201
  67.9 4.3 %up.1 = (bf16[256,1024]{1,0:T(8,128)(2,1)}, bf16[256,1024]{1,0:T(8,128)(2,1)}, bf16[128,1024]{1,0:T(8,128)(2,1)}, bf16[128,1024]{1,0:T(8,128)(2,1)}, bf16[256,1024]{1,0:T(8,128)(2,1)}) custom-call(bf16[576,1024]{1,0:T(8,128)(2,1)} %get-tuple-element.26.xs, bf16[576,1024]{1,0:T(8,128)(2,1)} %get-tuple-element.27.dh), custom_call_target="tpu_custom_call" | custom-call | tf_op jit(solution)/shard_map/up/pallas_call | solution.py:182
  72.2 1.6 %collective-permute-start.3 = (bf16[256,1024]{1,0:T(8,128)(2,1)}, bf16[256,1024]{1,0:T(8,128)(2,1)S(1)}, u32[]{:S(2)}, u32[]{:S(2)}) collective-permute-start(bf16[256,1024]{1,0:T(8,128)(2,1)} %get-tuple-element.31), channel_id=1, source_target_pairs={{0,3},{1,0},{2,1},{3,2},{4,7},{5,4},{6,5},{7,6},{8,11},{9,8},{10,9... | collective-permute-start | bytes 1572872 | tf_op jit(solution)/shard_map/up_one/ppermute | solution.py:201
  73.8 0.5 collective-permute-start.1
  74.3 1.0 add_convert_fusion
  75.3 4.7 %all-to-all-start.1 = ((bf16[32,10,8,128]{3,2,1,0:T(8,128)(2,1)}), bf16[32,10,8,128]{3,2,1,0:T(8,128)(2,1)S(1)}, u32[]{:S(2)}, u32[]{:S(2)}) async-start(bf16[32,10,8,128]{3,2,1,0:T(8,128)(2,1)} %add_convert_fusion), calls=%async_computation.1 | async-start | bytes 1310720 | tf_op jit(solution)/shard_map/rows_back/all_to_all | solution.py:305
  80.1 0.7 collective-permute-done.7
  81.3 3.0 %collective-permute-start.9 = (bf16[128,1024]{1,0:T(8,128)(2,1)S(1)}, bf16[128,1024]{1,0:T(8,128)(2,1)S(1)}, u32[]{:S(2)}, u32[]{:S(2)}) collective-permute-start(bf16[128,1024]{1,0:T(8,128)(2,1)S(1)} %add_convert_fusion.3), channel_id=1, source_target_pairs={{0,3},{1,0},{2,1},{3,2},{4,7},{5,4},{6,5},{7,6},{8,11},{9,8},{10,9... | collective-permute-start | bytes 786440 | tf_op jit(solution)/shard_map/down_two/ppermute | solution.py:201
  84.3 8.0 %collective-permute-done.3 = bf16[256,1024]{1,0:T(8,128)(2,1)S(1)} collective-permute-done((bf16[256,1024]{1,0:T(8,128)(2,1)}, bf16[256,1024]{1,0:T(8,128)(2,1)S(1)}, u32[]{:S(2)}, u32[]{:S(2)}) %collective-permute-start.3) | collective-permute-done | bytes 524320 | tf_op jit(solution)/shard_map/up_one/ppermute | solution.py:201
  92.3 0.8 add_convert_fusion.5
  93.1 3.0 %collective-permute-start.4 = (bf16[128,1024]{1,0:T(8,128)(2,1)}, bf16[128,1024]{1,0:T(8,128)(2,1)}, u32[]{:S(2)}, u32[]{:S(2)}) collective-permute-start(bf16[128,1024]{1,0:T(8,128)(2,1)} %add_convert_fusion.5), channel_id=1, source_target_pairs={{0,3},{1,0},{2,1},{3,2},{4,7},{5,4},{6,5},{7,6},{8,11},{9,8},{10,9... | collective-permute-start | bytes 786440 | tf_op jit(solution)/shard_map/up_two/ppermute | solution.py:201
  96.3 0.8 collective-permute-done.8
  97.1 0.9 collective-permute-done.9
  98.0 1.3 %add_convert_fusion.2 = bf16[256,1024]{1,0:T(8,128)(2,1)} fusion(bf16[256,1024]{1,0:T(8,128)(2,1)S(1)} %copy-done.5, bf16[256,1024]{1,0:T(8,128)(2,1)S(1)} %collective-permute-done.6, bf16[256,1024]{1,0:T(8,128)(2,1)S(1)} %collective-permute-done.7, pred[256]{0:T(512)(128)(4,1)S(1)} %broadcast_bitcast_fusion, ...), kind=kLoop, calls=%fused_computation.2 | loop fusion | flops 2097152 | bytes 2621696 | tf_op jit(solution)/shard_map/convert_element_type | solution.py:218
  99.3 0.9 all-to-all-done.1.back_ref
  100.2 0.9 copy-done.1
  101.0 2.4 %unpack.1 = (bf16[256,1024]{1,0:T(8,128)(2,1)}, bf16[256]{0:T(256)(128)(2,1)}) custom-call(bf16[32,10,8,128]{3,2,1,0:T(8,128)(2,1)} %copy-done.1, bf16[256]{0:T(256)(128)(2,1)} %gate_ref.3, s32[256]{0:T(256)} %expert_ref.3, s32[256]{0:T(256)} %slot_ref.3), custom_call_target="tpu_custom_call" | custom-call | tf_op jit(solution)/shard_map/unpack/pallas_call | solution.py:182
  103.9 2.3 %fusion = bf16[1,256,1024]{2,1,0:T(8,128)(2,1)} fusion(bf16[256,1024]{1,0:T(8,128)(2,1)S(1)} %copy-done.4, bf16[256,1024]{1,0:T(8,128)(2,1)S(1)} %collective-permute-done.3, bf16[256,1024]{1,0:T(8,128)(2,1)S(1)} %collective-permute-done.1, pred[256]{0:T(512)(128)(4,1)S(1)} %broadcast_bitcast_fusion, bf16[128,1024]{1,0:T(8,128)(2,1)} %collective-permute-done.4, ...), kind=kLoop, calls=%fused_computation.3 | loop fusion | flops 2097152 | bytes 2621696 | tf_op jit(solution)/shard_map/convert_element_type | solution.py:218
  (32 shorter events, 1.4 us)
Async XLA Ops:
  46.9 2.9 %copy-start = (bf16[32,18,8,128]{3,2,1,0:T(8,128)(2,1)}, bf16[32,18,8,128]{3,2,1,0:T(8,128)(2,1)S(1)}, u32[]{:S(2)}) copy-start(bf16[32,18,8,128]{3,2,1,0:T(8,128)(2,1)S(1)} %all_to_all.10.mine_ref) | copy-start | bytes 3538948
  46.9 2.8 %collective-permute-start = (bf16[32,18,8,128]{3,2,1,0:T(8,128)(2,1)S(1)}, bf16[32,18,8,128]{3,2,1,0:T(8,128)(2,1)S(1)}, u32[]{:S(2)}, u32[]{:S(2)}) collective-permute-start(bf16[32,18,8,128]{3,2,1,0:T(8,128)(2,1)S(1)} %all_to_all.10.mine_ref), channel_id=1, source_target_pairs={{0,4},{4,0},{1,5},{5,1},{2,6},{6,2},{3,7},{7,3},{8,12},{12,8},{9,1... | collective-permute-start | bytes 3538952 | tf_op jit(solution)/shard_map/ppermute | solution.py:243
  49.8 1.0 copy-start.2
  64.4 9.9 %copy-start.3 = (bf16[32,10,8,128]{3,2,1,0:T(8,128)(2,1)S(1)}, bf16[32,10,8,128]{3,2,1,0:T(8,128)(2,1)}, u32[]{:S(2)}) copy-start(bf16[32,10,8,128]{3,2,1,0:T(8,128)(2,1)} %get-tuple-element.32) | copy-start | bytes 1966084
  64.4 9.9 %collective-permute-start.5 = (bf16[32,10,8,128]{3,2,1,0:T(8,128)(2,1)}, bf16[32,10,8,128]{3,2,1,0:T(8,128)(2,1)S(1)}, u32[]{:S(2)}, u32[]{:S(2)}) collective-permute-start(bf16[32,10,8,128]{3,2,1,0:T(8,128)(2,1)} %get-tuple-element.33), channel_id=1, source_target_pairs={{0,4},{4,0},{1,5},{5,1},{2,6},{6,2},{3,7},{7,3},{8,12},{12,8},{9,1... | collective-permute-start | bytes 1966088 | tf_op jit(solution)/shard_map/swap_back/ppermute | solution.py:291
  64.6 16.2 %collective-permute-start.7 = (bf16[256,1024]{1,0:T(8,128)(2,1)}, bf16[256,1024]{1,0:T(8,128)(2,1)S(1)}, u32[]{:S(2)}, u32[]{:S(2)}) collective-permute-start(bf16[256,1024]{1,0:T(8,128)(2,1)} %get-tuple-element.42), channel_id=1, source_target_pairs={{0,1},{1,2},{2,3},{3,0},{4,5},{5,6},{6,7},{7,4},{8,9},{9,10},{10,1... | collective-permute-start | bytes 1572872 | tf_op jit(solution)/shard_map/down_one/ppermute | solution.py:201
  66.1 15.1 %collective-permute-start.6 = (bf16[256,1024]{1,0:T(8,128)(2,1)}, bf16[256,1024]{1,0:T(8,128)(2,1)S(1)}, u32[]{:S(2)}, u32[]{:S(2)}) collective-permute-start(bf16[256,1024]{1,0:T(8,128)(2,1)} %get-tuple-element.41), channel_id=1, source_target_pairs={{0,3},{1,0},{2,1},{3,2},{4,7},{5,4},{6,5},{7,6},{8,11},{9,8},{10,9... | collective-permute-start | bytes 1572872 | tf_op jit(solution)/shard_map/down_one/ppermute | solution.py:201
  72.2 20.1 %collective-permute-start.3 = (bf16[256,1024]{1,0:T(8,128)(2,1)}, bf16[256,1024]{1,0:T(8,128)(2,1)S(1)}, u32[]{:S(2)}, u32[]{:S(2)}) collective-permute-start(bf16[256,1024]{1,0:T(8,128)(2,1)} %get-tuple-element.31), channel_id=1, source_target_pairs={{0,3},{1,0},{2,1},{3,2},{4,7},{5,4},{6,5},{7,6},{8,11},{9,8},{10,9... | collective-permute-start | bytes 1572872 | tf_op jit(solution)/shard_map/up_one/ppermute | solution.py:201
  73.8 22.2 %collective-permute-start.1 = (bf16[256,1024]{1,0:T(8,128)(2,1)}, bf16[256,1024]{1,0:T(8,128)(2,1)S(1)}, u32[]{:S(2)}, u32[]{:S(2)}) collective-permute-start(bf16[256,1024]{1,0:T(8,128)(2,1)} %get-tuple-element.29), channel_id=1, source_target_pairs={{0,1},{1,2},{2,3},{3,0},{4,5},{5,6},{6,7},{7,4},{8,9},{9,10},{10,1... | collective-permute-start | bytes 1572872 | tf_op jit(solution)/shard_map/up_one/ppermute | solution.py:201
  74.3 6.5 %copy-start.8 = (bf16[128,1024]{1,0:T(8,128)(2,1)S(1)}, bf16[128,1024]{1,0:T(8,128)(2,1)}, u32[]{:S(2)}) copy-start(bf16[128,1024]{1,0:T(8,128)(2,1)} %get-tuple-element.43) | copy-start | bytes 786436
  75.3 5.9 %copy-start.6 = (bf16[128,1024]{1,0:T(8,128)(2,1)S(1)}, bf16[128,1024]{1,0:T(8,128)(2,1)}, u32[]{:S(2)}) copy-start(bf16[128,1024]{1,0:T(8,128)(2,1)} %get-tuple-element.44) | copy-start | bytes 786436
  75.3 17.0 %copy-start.9 = (bf16[128,1024]{1,0:T(8,128)(2,1)S(1)}, bf16[128,1024]{1,0:T(8,128)(2,1)}, u32[]{:S(2)}) copy-start(bf16[128,1024]{1,0:T(8,128)(2,1)} %get-tuple-element.30) | copy-start | bytes 786436
  75.3 24.8 %all-to-all-start.1 = ((bf16[32,10,8,128]{3,2,1,0:T(8,128)(2,1)}), bf16[32,10,8,128]{3,2,1,0:T(8,128)(2,1)S(1)}, u32[]{:S(2)}, u32[]{:S(2)}) async-start(bf16[32,10,8,128]{3,2,1,0:T(8,128)(2,1)} %add_convert_fusion), calls=%async_computation.1 | async-start | bytes 1310720 | tf_op jit(solution)/shard_map/rows_back/all_to_all | solution.py:305
  80.1 16.0 %copy-start.7 = (bf16[128,1024]{1,0:T(8,128)(2,1)S(1)}, bf16[128,1024]{1,0:T(8,128)(2,1)}, u32[]{:S(2)}) copy-start(bf16[128,1024]{1,0:T(8,128)(2,1)} %get-tuple-element.28) | copy-start | bytes 786436
  80.9 17.1 %copy-start.5 = (bf16[256,1024]{1,0:T(8,128)(2,1)S(1)}, bf16[256,1024]{1,0:T(8,128)(2,1)}, u32[]{:S(2)}) copy-start(bf16[256,1024]{1,0:T(8,128)(2,1)} %get-tuple-element.40) | copy-start | bytes 1572868
  80.9 16.2 %collective-permute-start.8 = (bf16[128,1024]{1,0:T(8,128)(2,1)S(1)}, bf16[128,1024]{1,0:T(8,128)(2,1)S(1)}, u32[]{:S(2)}, u32[]{:S(2)}) collective-permute-start(bf16[128,1024]{1,0:T(8,128)(2,1)S(1)} %add_convert_fusion.4), channel_id=1, source_target_pairs={{0,1},{1,2},{2,3},{3,0},{4,5},{5,6},{6,7},{7,4},{8,9},{9,10},{10,1... | collective-permute-start | bytes 786440 | tf_op jit(solution)/shard_map/down_two/ppermute | solution.py:201
  81.3 16.6 %collective-permute-start.9 = (bf16[128,1024]{1,0:T(8,128)(2,1)S(1)}, bf16[128,1024]{1,0:T(8,128)(2,1)S(1)}, u32[]{:S(2)}, u32[]{:S(2)}) collective-permute-start(bf16[128,1024]{1,0:T(8,128)(2,1)S(1)} %add_convert_fusion.3), channel_id=1, source_target_pairs={{0,3},{1,0},{2,1},{3,2},{4,7},{5,4},{6,5},{7,6},{8,11},{9,8},{10,9... | collective-permute-start | bytes 786440 | tf_op jit(solution)/shard_map/down_two/ppermute | solution.py:201
  93.1 10.4 %collective-permute-start.4 = (bf16[128,1024]{1,0:T(8,128)(2,1)}, bf16[128,1024]{1,0:T(8,128)(2,1)}, u32[]{:S(2)}, u32[]{:S(2)}) collective-permute-start(bf16[128,1024]{1,0:T(8,128)(2,1)} %add_convert_fusion.5), channel_id=1, source_target_pairs={{0,3},{1,0},{2,1},{3,2},{4,7},{5,4},{6,5},{7,6},{8,11},{9,8},{10,9... | collective-permute-start | bytes 786440 | tf_op jit(solution)/shard_map/up_two/ppermute | solution.py:201
  96.1 7.8 %collective-permute-start.2 = (bf16[128,1024]{1,0:T(8,128)(2,1)S(1)}, bf16[128,1024]{1,0:T(8,128)(2,1)}, u32[]{:S(2)}, u32[]{:S(2)}) collective-permute-start(bf16[128,1024]{1,0:T(8,128)(2,1)S(1)} %add_convert_fusion.6), channel_id=1, source_target_pairs={{0,1},{1,2},{2,3},{3,0},{4,5},{5,6},{6,7},{7,4},{8,9},{9,10},{10,1... | collective-permute-start | bytes 786440 | tf_op jit(solution)/shard_map/up_two/ppermute | solution.py:201
  98.0 6.0 %copy-start.4 = (bf16[256,1024]{1,0:T(8,128)(2,1)S(1)}, bf16[256,1024]{1,0:T(8,128)(2,1)}, u32[]{:S(2)}) copy-start(bf16[256,1024]{1,0:T(8,128)(2,1)} %get-tuple-element.37) | copy-start | bytes 1572868
  100.2 0.9 copy-start.1

commit v6 on v4

--- a/solution.py
+++ b/solution.py
@@ -85,19 +85,24 @@
 
 
 def activation(hid, dact, act, dh, gate):
-    step = 32
+    step = 64
 
     def block(i, carry):
         at = pl.ds(pl.multiple_of(i * step, step), step)
-        v = hid[at, :]
-        d = dact[at, :]
-        cdf = 0.5 * (1.0 + lax.erf(v * 0.7071067811865476))
-        pdf = jnp.exp(-0.5 * v * v) * 0.3989422804014327
-        a = (v * cdf).astype(BF)
-        act[at, :] = a
-        dh[at, :] = (d * (cdf + v * pdf)).astype(BF)
-        total = jnp.sum(a.astype(F32) * d, axis=1, keepdims=True)
-        gate[at, :] = jnp.broadcast_to(total, (step, LANES))
+        total = None
+        for start in range(0, hid.shape[1], LANES):
+            cols = pl.ds(start, LANES)
+            v = hid[at, cols]
+            d = dact[at, cols]
+            cdf = 0.5 * (1.0 + lax.erf(v * 0.7071067811865476))
+            pdf = jnp.exp(-0.5 * v * v) * 0.3989422804014327
+            a = (v * cdf).astype(BF)
+            act[at, cols] = a
+            dh[at, cols] = (d * (cdf + v * pdf)).astype(BF)
+            part = a.astype(F32) * d
+            total = part if total is None else total + part
+        row = jnp.sum(total, axis=1, keepdims=True)
+        gate[at, :] = jnp.broadcast_to(row, (step, LANES))
         return carry
 
     lax.fori_loop(0, hid.shape[0] // step, block, 0)
@@ -186,14 +191,17 @@
     return fwd, bwd
 
 
-def total(own, left, right, left2, right2):
+def early(own, left, right):
+    low = lax.broadcasted_iota(jnp.int32, own.shape, 0) < own.shape[0] // 2
+    return lax.optimization_barrier(own.astype(F32) + jnp.where(low, right, left).astype(F32))
+
+
+def total(begun, left2, right2):
     half, columns = left2.shape
-    split = lambda a: a.reshape(2, half, columns)
     both = lambda a: jnp.broadcast_to(a[None], (2, half, columns))
     low = lax.broadcasted_iota(jnp.int32, (2, half, columns), 0) == 0
-    first = jnp.where(low, split(right), split(left)).astype(F32)
     then = jnp.where(low, both(left2), both(right2)).astype(F32)
-    return (split(own).astype(F32) + first + then).astype(BF).reshape(2 * half, columns)
+    return (begun.reshape(2, half, columns) + then).astype(BF).reshape(2 * half, columns)
 
 
 def after(value, earlier):
@@ -246,11 +254,24 @@
         w_up,
         w_down,
       )
+    with jax.named_scope("down_one"):
+      left_d, right_d = ring(down[0], down[1])
     with jax.named_scope("swap_back"):
       got = lax.ppermute(give, "core", swap)
+    with jax.named_scope("up"):
+      up = call(up_kernel, parts(width, hidden), [], xs, dh)
+    with jax.named_scope("up_one"):
+      left_u, right_u = ring(up[0], up[1])
     both = (keep.astype(F32) + got.astype(F32)).astype(BF)
     with jax.named_scope("rows_back"):
       back = lax.all_to_all(both, "chip", split_axis=0, concat_axis=0, tiled=True)
+    down2 = second(down, left_d, right_d)
+    with jax.named_scope("down_two"):
+      left_d2, right_d2 = ring(*down2)
+    up2 = second(up, left_u, right_u)
+    with jax.named_scope("up_two"):
+      left_u2, right_u2 = ring(*up2)
+    down_grad = total(early(down[4], left_d, right_d), left_d2, right_d2)
     with jax.named_scope("unpack"):
       in_grad, gate_grad = call(
           unpack_kernel,
@@ -261,21 +282,9 @@
           expert_ids,
           slot_ids,
       )
-    with jax.named_scope("down_one"):
-      left_d, right_d = ring(down[0], down[1])
-    down2 = second(down, left_d, right_d)
-    with jax.named_scope("down_two"):
-      left_d2, right_d2 = ring(*down2)
-    with jax.named_scope("up"):
-      up = call(up_kernel, parts(width, hidden), [], xs, dh)
-    down_grad = total(down[4], left_d, right_d, left_d2, right_d2)
-    with jax.named_scope("up_one"):
-      left_u, right_u = ring(up[0], up[1])
-    up2 = second(up, left_u, right_u)
-    with jax.named_scope("up_two"):
-      left_u2, right_u2 = ring(*up2)
+    left_u2, right_u2, in_grad = lax.optimization_barrier((left_u2, right_u2, in_grad))
     left_u2, right_u2, down_grad = lax.optimization_barrier((left_u2, right_u2, down_grad))
-    up_grad = total(up[4], left_u, right_u, left_u2, right_u2)
+    up_grad = total(early(up[4], left_u, right_u), left_u2, right_u2)
     return (in_grad, gate_grad, up_grad[None], down_grad[None])
 
 

time: 108 us -> 106 us (0.981)
  waiting for transfers between devices: 17.7 us -> 11.9 us
  other arithmetic: 3.9 us -> 7.81 us
  starting transfers between devices: 16.9 us -> 18 us
    ppermute x8, waiting for transfers between devices: 14.8 us -> 7.53 us  [ring(): return (lax.ppermute(fwd, 'dp', AHEAD), lax.ppermute(bwd, 'dp', BEHIND))]
    add x0 -> x1, other arithmetic: none -> 1.86 us  [early(): own.astype(F32) + jnp.where(low, right, left).astype(F32)]
    all_to_all x1, waiting for transfers between devices: 0.01 us -> 1.47 us  [on_device(): back = lax.all_to_all(both, 'chip', split_axis=0, concat_axis=0, tiled=True)]
  transfers between devices with their start and end apart: 11 -> 11, of which waited for: 7 -> 4; matrix products, arithmetic and copies ran while one was open for 4% -> 6% of each run, Pallas kernels for 4% -> 6%
where the time goes in v6:
time: 106 us; the launch traced here: 105 us
  blocking collectives  43.5 us (41%)
  Pallas kernels  21.3 us (20%)
  starting transfers between devices  18 us (17%)
  waiting for transfers between devices  11.9 us (11%)
  other arithmetic  7.81 us (7%)
  local copies, waits for them, and re-layouts  2 us (2%)
    all_to_all x1, blocking collectives, on_device(): mine = lax.all_to_all(sent, 'chip', split_axis=0, concat_axis=0, tiled=True)  43.5 us
    pallas_call x4, Pallas kernels, call(): pl.pallas_call(kernel, out_shape=out, in_specs=[whole] * len(args), out_s...  21.3 us
    ppermute x8, starting transfers between devices, ring(): return (lax.ppermute(fwd, 'dp', AHEAD), lax.ppermute(bwd, 'dp', BEHIND))  12.8 us
    ppermute x8, waiting for transfers between devices, ring(): return (lax.ppermute(fwd, 'dp', AHEAD), lax.ppermute(bwd, 'dp', BEHIND))  7.53 us
    all_to_all x1, starting transfers between devices, on_device(): back = lax.all_to_all(both, 'chip', split_axis=0, concat_axis=0, tiled=True)  4.92 us
    convert_element_type x2, other arithmetic, total(): (begun.reshape(2, half, columns) + then).astype(BF)  3.13 us
    ppermute x1, waiting for transfers between devices, on_device(): other = lax.ppermute(mine, 'core', swap)  2.84 us
  transfers between devices with their start and end apart: 11, of which 4 were waited for; matrix products, arithmetic and copies ran while one was open for 6% of the time, Pallas kernels for 6%

profile of v6, /device:TPU:32, one launch (start us, length us, event | category | flops | bytes accessed | tf_op | source)
XLA Modules:
  0.0 105.2 jit_solution(13238609838569844513)
XLA Ops:
  0.6 2.8 %shard_map.102 = bf16[32,18,8,128]{3,2,1,0:T(8,128)(2,1)} custom-call(bf16[256,1024]{1,0:T(8,128)(2,1)} %x_ref.1, bf16[256,1024]{1,0:T(8,128)(2,1)} %g_ref.1, bf16[256]{0:T(256)(128)(2,1)} %gate_ref.3, s32[256]{0:T(256)} %expert_ref.3, s32[256]{0:T(256)} %slot_ref.3), custom_call_target="tpu_custom_call" | custom-call | tf_op jit(solution)/shard_map/pallas_call | solution.py:165
  3.4 43.5 %all_to_all.10.mine_ref = bf16[32,18,8,128]{3,2,1,0:T(8,128)(2,1)S(1)} all-to-all(bf16[32,18,8,128]{3,2,1,0:T(8,128)(2,1)} %shard_map.102), channel_id=1, replica_groups=mesh['chip'=32,'core'=2,'dp'=4] {'chip'}, dimensions={0} | all-to-all | bytes 2359296 | tf_op jit(solution)/shard_map/all_to_all | solution.py:228
  46.9 2.8 %collective-permute-done.other_ref = bf16[32,18,8,128]{3,2,1,0:T(8,128)(2,1)S(1)} collective-permute-done((bf16[32,18,8,128]{3,2,1,0:T(8,128)(2,1)S(1)}, bf16[32,18,8,128]{3,2,1,0:T(8,128)(2,1)S(1)}, u32[]{:S(2)}, u32[]{:S(2)}) %collective-permute-start) | collective-permute-done | bytes 1179680 | tf_op jit(solution)/shard_map/ppermute | solution.py:229
  49.8 1.0 copy-done.2
  50.8 11.8 %expert_input.1 = (bf16[576,1024]{1,0:T(8,128)(2,1)}, bf16[576,1024]{1,0:T(8,128)(2,1)}, bf16[32,10,8,128]{3,2,1,0:T(8,128)(2,1)}, bf16[32,10,8,128]{3,2,1,0:T(8...) custom-call(bf16[32,18,8,128]{3,2,1,0:T(8,128)(2,1)} %copy-done, ...), custom_call_target="tpu_custom_call" | custom-call | tf_op jit(solution)/shard_map/expert_input/pallas_call | solution.py:165
  62.6 0.2 collective-permute-start.5
  62.9 1.5 %collective-permute-start.7 = (bf16[256,1024]{1,0:T(8,128)(2,1)}, bf16[256,1024]{1,0:T(8,128)(2,1)S(1)}, u32[]{:S(2)}, u32[]{:S(2)}) collective-permute-start(bf16[256,1024]{1,0:T(8,128)(2,1)} %get-tuple-element.42), channel_id=1, source_target_pairs={{0,1},{1,2},{2,3},{3,0},{4,5},{5,6},{6,7},{7,4},{8,9},{9,10},{10,1... | collective-permute-start | bytes 1572872 | tf_op jit(solution)/shard_map/down_one/ppermute | solution.py:184
  64.4 1.7 %collective-permute-start.6 = (bf16[256,1024]{1,0:T(8,128)(2,1)}, bf16[256,1024]{1,0:T(8,128)(2,1)S(1)}, u32[]{:S(2)}, u32[]{:S(2)}) collective-permute-start(bf16[256,1024]{1,0:T(8,128)(2,1)} %get-tuple-element.41), channel_id=1, source_target_pairs={{0,3},{1,0},{2,1},{3,2},{4,7},{5,4},{6,5},{7,6},{8,11},{9,8},{10,9... | collective-permute-start | bytes 1572872 | tf_op jit(solution)/shard_map/down_one/ppermute | solution.py:184
  66.2 4.3 %up.1 = (bf16[256,1024]{1,0:T(8,128)(2,1)}, bf16[256,1024]{1,0:T(8,128)(2,1)}, bf16[128,1024]{1,0:T(8,128)(2,1)}, bf16[128,1024]{1,0:T(8,128)(2,1)}, bf16[256,1024]{1,0:T(8,128)(2,1)}) custom-call(bf16[576,1024]{1,0:T(8,128)(2,1)} %get-tuple-element.26.xs, bf16[576,1024]{1,0:T(8,128)(2,1)} %get-tuple-element.27.dh), custom_call_target="tpu_custom_call" | custom-call | tf_op jit(solution)/shard_map/up/pallas_call | solution.py:165
  70.5 0.3 collective-permute-start.1
  70.7 3.0 %collective-permute-start.3 = (bf16[256,1024]{1,0:T(8,128)(2,1)}, bf16[256,1024]{1,0:T(8,128)(2,1)S(1)}, u32[]{:S(2)}, u32[]{:S(2)}) collective-permute-start(bf16[256,1024]{1,0:T(8,128)(2,1)} %get-tuple-element.31), channel_id=1, source_target_pairs={{0,3},{1,0},{2,1},{3,2},{4,7},{5,4},{6,5},{7,6},{8,11},{9,8},{10,9... | collective-permute-start | bytes 1572872 | tf_op jit(solution)/shard_map/up_one/ppermute | solution.py:184
  73.7 1.0 add_convert_fusion
  74.7 4.9 %all-to-all-start.1 = ((bf16[32,10,8,128]{3,2,1,0:T(8,128)(2,1)}), bf16[32,10,8,128]{3,2,1,0:T(8,128)(2,1)S(1)}, u32[]{:S(2)}, u32[]{:S(2)}) async-start(bf16[32,10,8,128]{3,2,1,0:T(8,128)(2,1)} %add_convert_fusion), calls=%async_computation.1 | async-start | bytes 1310720 | tf_op jit(solution)/shard_map/rows_back/all_to_all | solution.py:267
  80.0 3.3 %collective-permute-start.9 = (bf16[128,1024]{1,0:T(8,128)(2,1)S(1)}, bf16[128,1024]{1,0:T(8,128)(2,1)S(1)}, u32[]{:S(2)}, u32[]{:S(2)}) collective-permute-start(bf16[128,1024]{1,0:T(8,128)(2,1)S(1)} %add_convert_fusion.3), channel_id=1, source_target_pairs={{0,3},{1,0},{2,1},{3,2},{4,7},{5,4},{6,5},{7,6},{8,11},{9,8},{10,9... | collective-permute-start | bytes 786440 | tf_op jit(solution)/shard_map/down_two/ppermute | solution.py:184
  83.3 7.4 %collective-permute-done.3 = bf16[256,1024]{1,0:T(8,128)(2,1)S(1)} collective-permute-done((bf16[256,1024]{1,0:T(8,128)(2,1)}, bf16[256,1024]{1,0:T(8,128)(2,1)S(1)}, u32[]{:S(2)}, u32[]{:S(2)}) %collective-permute-start.3) | collective-permute-done | bytes 524320 | tf_op jit(solution)/shard_map/up_one/ppermute | solution.py:184
  90.7 0.9 add_convert_fusion.5
  91.5 3.0 %collective-permute-start.4 = (bf16[128,1024]{1,0:T(8,128)(2,1)}, bf16[128,1024]{1,0:T(8,128)(2,1)S(1)}, u32[]{:S(2)}, u32[]{:S(2)}) collective-permute-start(bf16[128,1024]{1,0:T(8,128)(2,1)} %add_convert_fusion.5), channel_id=1, source_target_pairs={{0,3},{1,0},{2,1},{3,2},{4,7},{5,4},{6,5},{7,6},{8,11},{9,8},{10,9... | collective-permute-start | bytes 786440 | tf_op jit(solution)/shard_map/up_two/ppermute | solution.py:184
  94.5 0.8 add_convert_fusion.6
  95.3 1.9 %convert_add_fusion = (f32[256,1024]{1,0:T(8,128)S(1)}, f32[256,1024]{1,0:T(8,128)S(1)}) fusion(bf16[256,1024]{1,0:T(8,128)(2,1)S(1)} %copy-done.5, bf16[256,1024]{1,0:T(8,128)(2,1)S(1)} %collective-permute-done.6, bf16[256,1024]{1,0:T(8,128)(2,1)S(1)} %collective-permute-done.7, pred[256]{0:T(512)(128)(4,1)S(1)} %iota_compare_fusion, ...), kind=kLoop, calls=%fused_computation.3 | loop fusion | flops 2097152 | bytes 5243136 | tf_op jit(solution)/shard_map/add | solution.py:196
  97.2 1.1 %add_convert_fusion.2 = bf16[256,1024]{1,0:T(8,128)(2,1)} fusion(f32[256,1024]{1,0:T(8,128)S(1)} %get-tuple-element.48, pred[256]{0:T(512)(128)(4,1)S(1)} %broadcast_bitcast_fusion, bf16[128,1024]{1,0:T(8,128)(2,1)S(1)} %collective-permute-done.9, bf16[128,1024]{1,0:T(8,128)(2,1)S(1)} %collective-permute-done.8), kind=kLoop, calls=%fused_computation.2 | loop fusion | flops 1048576 | bytes 2097408 | tf_op jit(solution)/shard_map/convert_element_type | solution.py:204
  98.3 1.5 %all-to-all-done.1.back_ref = bf16[32,10,8,128]{3,2,1,0:T(8,128)(2,1)S(1)} async-done(((bf16[32,10,8,128]{3,2,1,0:T(8,128)(2,1)}), bf16[32,10,8,128]{3,2,1,0:T(8,128)(2,1)S(1)}, u32[]{:S(2)}, u32[]{:S(2)}) %all-to-all-start.1) | async-done | bytes 655392 | tf_op jit(solution)/shard_map/rows_back/all_to_all | solution.py:267
  99.8 0.9 copy-done.1
  100.6 2.4 %unpack.1 = (bf16[256,1024]{1,0:T(8,128)(2,1)}, bf16[256]{0:T(256)(128)(2,1)}) custom-call(bf16[32,10,8,128]{3,2,1,0:T(8,128)(2,1)} %copy-done.1, bf16[256]{0:T(256)(128)(2,1)} %gate_ref.3, s32[256]{0:T(256)} %expert_ref.3, s32[256]{0:T(256)} %slot_ref.3), custom_call_target="tpu_custom_call" | custom-call | tf_op jit(solution)/shard_map/unpack/pallas_call | solution.py:165
  103.2 2.0 %fusion = bf16[1,256,1024]{2,1,0:T(8,128)(2,1)} fusion(f32[256,1024]{1,0:T(8,128)S(1)} %get-tuple-element.49, pred[256]{0:T(512)(128)(4,1)S(1)} %broadcast_bitcast_fusion, bf16[128,1024]{1,0:T(8,128)(2,1)S(1)} %collective-permute-done.4, bf16[128,1024]{1,0:T(8,128)(2,1)} %collective-permute-done.2), kind=kLoop, calls=%fused_computation.5 | loop fusion | flops 1048576 | bytes 2097408 | tf_op jit(solution)/shard_map/convert_element_type | solution.py:204
  (36 shorter events, 0.5 us)
Async XLA Ops:
  46.9 2.9 %copy-start = (bf16[32,18,8,128]{3,2,1,0:T(8,128)(2,1)}, bf16[32,18,8,128]{3,2,1,0:T(8,128)(2,1)S(1)}, u32[]{:S(2)}) copy-start(bf16[32,18,8,128]{3,2,1,0:T(8,128)(2,1)S(1)} %all_to_all.10.mine_ref) | copy-start | bytes 3538948
  46.9 2.8 %collective-permute-start = (bf16[32,18,8,128]{3,2,1,0:T(8,128)(2,1)S(1)}, bf16[32,18,8,128]{3,2,1,0:T(8,128)(2,1)S(1)}, u32[]{:S(2)}, u32[]{:S(2)}) collective-permute-start(bf16[32,18,8,128]{3,2,1,0:T(8,128)(2,1)S(1)} %all_to_all.10.mine_ref), channel_id=1, source_target_pairs={{0,4},{4,0},{1,5},{5,1},{2,6},{6,2},{3,7},{7,3},{8,12},{12,8},{9,1... | collective-permute-start | bytes 3538952 | tf_op jit(solution)/shard_map/ppermute | solution.py:229
  49.8 1.0 copy-start.2
  62.6 11.1 %copy-start.4 = (bf16[32,10,8,128]{3,2,1,0:T(8,128)(2,1)S(1)}, bf16[32,10,8,128]{3,2,1,0:T(8,128)(2,1)}, u32[]{:S(2)}) copy-start(bf16[32,10,8,128]{3,2,1,0:T(8,128)(2,1)} %get-tuple-element.32) | copy-start | bytes 1966084
  62.6 11.1 %collective-permute-start.5 = (bf16[32,10,8,128]{3,2,1,0:T(8,128)(2,1)}, bf16[32,10,8,128]{3,2,1,0:T(8,128)(2,1)S(1)}, u32[]{:S(2)}, u32[]{:S(2)}) collective-permute-start(bf16[32,10,8,128]{3,2,1,0:T(8,128)(2,1)} %get-tuple-element.33), channel_id=1, source_target_pairs={{0,4},{4,0},{1,5},{5,1},{2,6},{6,2},{3,7},{7,3},{8,12},{12,8},{9,1... | collective-permute-start | bytes 1966088 | tf_op jit(solution)/shard_map/swap_back/ppermute | solution.py:260
  62.9 16.8 %collective-permute-start.7 = (bf16[256,1024]{1,0:T(8,128)(2,1)}, bf16[256,1024]{1,0:T(8,128)(2,1)S(1)}, u32[]{:S(2)}, u32[]{:S(2)}) collective-permute-start(bf16[256,1024]{1,0:T(8,128)(2,1)} %get-tuple-element.42), channel_id=1, source_target_pairs={{0,1},{1,2},{2,3},{3,0},{4,5},{5,6},{6,7},{7,4},{8,9},{9,10},{10,1... | collective-permute-start | bytes 1572872 | tf_op jit(solution)/shard_map/down_one/ppermute | solution.py:184
  64.4 15.4 %collective-permute-start.6 = (bf16[256,1024]{1,0:T(8,128)(2,1)}, bf16[256,1024]{1,0:T(8,128)(2,1)S(1)}, u32[]{:S(2)}, u32[]{:S(2)}) collective-permute-start(bf16[256,1024]{1,0:T(8,128)(2,1)} %get-tuple-element.41), channel_id=1, source_target_pairs={{0,3},{1,0},{2,1},{3,2},{4,7},{5,4},{6,5},{7,6},{8,11},{9,8},{10,9... | collective-permute-start | bytes 1572872 | tf_op jit(solution)/shard_map/down_one/ppermute | solution.py:184
  70.5 24.0 %collective-permute-start.1 = (bf16[256,1024]{1,0:T(8,128)(2,1)}, bf16[256,1024]{1,0:T(8,128)(2,1)S(1)}, u32[]{:S(2)}, u32[]{:S(2)}) collective-permute-start(bf16[256,1024]{1,0:T(8,128)(2,1)} %get-tuple-element.29), channel_id=1, source_target_pairs={{0,1},{1,2},{2,3},{3,0},{4,5},{5,6},{6,7},{7,4},{8,9},{9,10},{10,1... | collective-permute-start | bytes 1572872 | tf_op jit(solution)/shard_map/up_one/ppermute | solution.py:184
  70.7 19.9 %collective-permute-start.3 = (bf16[256,1024]{1,0:T(8,128)(2,1)}, bf16[256,1024]{1,0:T(8,128)(2,1)S(1)}, u32[]{:S(2)}, u32[]{:S(2)}) collective-permute-start(bf16[256,1024]{1,0:T(8,128)(2,1)} %get-tuple-element.31), channel_id=1, source_target_pairs={{0,3},{1,0},{2,1},{3,2},{4,7},{5,4},{6,5},{7,6},{8,11},{9,8},{10,9... | collective-permute-start | bytes 1572872 | tf_op jit(solution)/shard_map/up_one/ppermute | solution.py:184
  73.7 6.0 %copy-start.9 = (bf16[128,1024]{1,0:T(8,128)(2,1)S(1)}, bf16[128,1024]{1,0:T(8,128)(2,1)}, u32[]{:S(2)}) copy-start(bf16[128,1024]{1,0:T(8,128)(2,1)} %get-tuple-element.43) | copy-start | bytes 786436
  74.7 5.2 %copy-start.7 = (bf16[128,1024]{1,0:T(8,128)(2,1)S(1)}, bf16[128,1024]{1,0:T(8,128)(2,1)}, u32[]{:S(2)}) copy-start(bf16[128,1024]{1,0:T(8,128)(2,1)} %get-tuple-element.44) | copy-start | bytes 786436
  74.7 15.9 %copy-start.10 = (bf16[128,1024]{1,0:T(8,128)(2,1)S(1)}, bf16[128,1024]{1,0:T(8,128)(2,1)}, u32[]{:S(2)}) copy-start(bf16[128,1024]{1,0:T(8,128)(2,1)} %get-tuple-element.30) | copy-start | bytes 786436
  74.7 25.0 %all-to-all-start.1 = ((bf16[32,10,8,128]{3,2,1,0:T(8,128)(2,1)}), bf16[32,10,8,128]{3,2,1,0:T(8,128)(2,1)S(1)}, u32[]{:S(2)}, u32[]{:S(2)}) async-start(bf16[32,10,8,128]{3,2,1,0:T(8,128)(2,1)} %add_convert_fusion), calls=%async_computation.1 | async-start | bytes 1310720 | tf_op jit(solution)/shard_map/rows_back/all_to_all | solution.py:267
  79.7 14.8 %copy-start.8 = (bf16[128,1024]{1,0:T(8,128)(2,1)S(1)}, bf16[128,1024]{1,0:T(8,128)(2,1)}, u32[]{:S(2)}) copy-start(bf16[128,1024]{1,0:T(8,128)(2,1)} %get-tuple-element.28) | copy-start | bytes 786436
  79.8 15.5 %copy-start.5 = (bf16[256,1024]{1,0:T(8,128)(2,1)S(1)}, bf16[256,1024]{1,0:T(8,128)(2,1)}, u32[]{:S(2)}) copy-start(bf16[256,1024]{1,0:T(8,128)(2,1)} %get-tuple-element.40) | copy-start | bytes 1572868
  79.8 15.5 %copy-start.6 = (bf16[256,1024]{1,0:T(8,128)(2,1)S(1)}, bf16[256,1024]{1,0:T(8,128)(2,1)}, u32[]{:S(2)}) copy-start(bf16[256,1024]{1,0:T(8,128)(2,1)} %get-tuple-element.37) | copy-start | bytes 1572868
  79.8 17.4 %collective-permute-start.8 = (bf16[128,1024]{1,0:T(8,128)(2,1)S(1)}, bf16[128,1024]{1,0:T(8,128)(2,1)S(1)}, u32[]{:S(2)}, u32[]{:S(2)}) collective-permute-start(bf16[128,1024]{1,0:T(8,128)(2,1)S(1)} %add_convert_fusion.4), channel_id=1, source_target_pairs={{0,1},{1,2},{2,3},{3,0},{4,5},{5,6},{6,7},{7,4},{8,9},{9,10},{10,1... | collective-permute-start | bytes 786440 | tf_op jit(solution)/shard_map/down_two/ppermute | solution.py:184
  80.0 17.2 %collective-permute-start.9 = (bf16[128,1024]{1,0:T(8,128)(2,1)S(1)}, bf16[128,1024]{1,0:T(8,128)(2,1)S(1)}, u32[]{:S(2)}, u32[]{:S(2)}) collective-permute-start(bf16[128,1024]{1,0:T(8,128)(2,1)S(1)} %add_convert_fusion.3), channel_id=1, source_target_pairs={{0,3},{1,0},{2,1},{3,2},{4,7},{5,4},{6,5},{7,6},{8,11},{9,8},{10,9... | collective-permute-start | bytes 786440 | tf_op jit(solution)/shard_map/down_two/ppermute | solution.py:184
  90.7 4.6 %copy-start.3 = (bf16[256,1024]{1,0:T(8,128)(2,1)}, bf16[256,1024]{1,0:T(8,128)(2,1)S(1)}, u32[]{:S(2)}) copy-start(bf16[256,1024]{1,0:T(8,128)(2,1)S(1)} %collective-permute-done.3) | copy-start | bytes 1572868
  91.5 11.5 %collective-permute-start.4 = (bf16[128,1024]{1,0:T(8,128)(2,1)}, bf16[128,1024]{1,0:T(8,128)(2,1)S(1)}, u32[]{:S(2)}, u32[]{:S(2)}) collective-permute-start(bf16[128,1024]{1,0:T(8,128)(2,1)} %add_convert_fusion.5), channel_id=1, source_target_pairs={{0,3},{1,0},{2,1},{3,2},{4,7},{5,4},{6,5},{7,6},{8,11},{9,8},{10,9... | collective-permute-start | bytes 786440 | tf_op jit(solution)/shard_map/up_two/ppermute | solution.py:184
  95.3 7.9 %collective-permute-start.2 = (bf16[128,1024]{1,0:T(8,128)(2,1)}, bf16[128,1024]{1,0:T(8,128)(2,1)}, u32[]{:S(2)}, u32[]{:S(2)}) collective-permute-start(bf16[128,1024]{1,0:T(8,128)(2,1)} %add_convert_fusion.6), channel_id=1, source_target_pairs={{0,1},{1,2},{2,3},{3,0},{4,5},{5,6},{6,7},{7,4},{8,9},{9,10},{10,1... | collective-permute-start | bytes 786440 | tf_op jit(solution)/shard_map/up_two/ppermute | solution.py:184
  99.7 0.9 copy-start.1

commit v7 on v6

--- a/solution.py
+++ b/solution.py
@@ -126,18 +126,15 @@
 
 
 def expert_kernel(
-    mine_ref, other_ref, up_ref, down_ref, xs, dh, keep, give, fwd1, bwd1, fwd2, bwd2, own, gate, ds, act, hid, dact, turn
+    mine_ref, other_ref, up_ref, down_ref, keep, give, fwd1, bwd1, fwd2, bwd2, own, ufwd1, ubwd1, ufwd2, ubwd2, uown, xs, dh, gate, ds, act, hid, dact, turn
 ):
     unpacked(mine_ref, other_ref, xs, ds, turn)
     hid[...] = matmul(xs[...], up_ref[0], ((1,), (0,)))
     dact[...] = matmul(ds[...], down_ref[0], ((1,), (1,)))
     activation(hid, dact, act, dh, gate)
     weight_parts(act, ds[...], lax.axis_index("dp"), fwd1, bwd1, fwd2, bwd2, own)
+    weight_parts(xs, dh[...], lax.axis_index("dp"), ufwd1, ubwd1, ufwd2, ubwd2, uown)
     returned(dh, gate, up_ref, keep, give, hid, turn)
-
-
-def up_kernel(xs, dh, fwd1, bwd1, fwd2, bwd2, own):
-    weight_parts(xs, dh[...], lax.axis_index("dp"), fwd1, bwd1, fwd2, bwd2, own)
 
 
 def unpack_kernel(back_ref, gate_ref, expert_ref, slot_ref, out_ref, gate_out_ref, rowbuf, turn):
@@ -193,7 +190,8 @@
 
 def early(own, left, right):
     low = lax.broadcasted_iota(jnp.int32, own.shape, 0) < own.shape[0] // 2
-    return lax.optimization_barrier(own.astype(F32) + jnp.where(low, right, left).astype(F32))
+    begun = own.astype(F32) + jnp.where(low, right, left).astype(F32)
+    return lax.optimization_barrier(begun.astype(BF))
 
 
 def total(begun, left2, right2):
@@ -201,7 +199,7 @@
     both = lambda a: jnp.broadcast_to(a[None], (2, half, columns))
     low = lax.broadcasted_iota(jnp.int32, (2, half, columns), 0) == 0
     then = jnp.where(low, both(left2), both(right2)).astype(F32)
-    return (begun.reshape(2, half, columns) + then).astype(BF).reshape(2 * half, columns)
+    return (begun.reshape(2, half, columns).astype(F32) + then).astype(BF).reshape(2 * half, columns)
 
 
 def after(value, earlier):
@@ -238,12 +236,11 @@
             shape(quarter, columns),
         )
 
-    with jax.named_scope("expert_input"):
-      xs, dh, keep, give, *down = call(
+    with jax.named_scope("all"):
+      keep, give, *both_parts = call(
         expert_kernel,
-        (shape(2 * rows, width), shape(2 * rows, hidden), shape(groups, 10, 8, LANES), shape(groups, 10, 8, LANES))
-        + parts(hidden, width),
-        [pltpu.VMEM((2 * rows, LANES), F32), pltpu.VMEM((2 * rows, width), BF),
+        (shape(groups, 10, 8, LANES), shape(groups, 10, 8, LANES)) + parts(hidden, width) + parts(width, hidden),
+        [pltpu.VMEM((2 * rows, width), BF), pltpu.VMEM((2 * rows, hidden), BF), pltpu.VMEM((2 * rows, LANES), F32), pltpu.VMEM((2 * rows, width), BF),
             pltpu.VMEM((2 * rows, hidden), BF),
             pltpu.VMEM((2 * rows, hidden), F32),
             pltpu.VMEM((2 * rows, hidden), F32),
@@ -254,12 +251,11 @@
         w_up,
         w_down,
       )
+    down, up = both_parts[:5], both_parts[5:]
     with jax.named_scope("down_one"):
       left_d, right_d = ring(down[0], down[1])
     with jax.named_scope("swap_back"):
       got = lax.ppermute(give, "core", swap)
-    with jax.named_scope("up"):
-      up = call(up_kernel, parts(width, hidden), [], xs, dh)
     with jax.named_scope("up_one"):
       left_u, right_u = ring(up[0], up[1])
     both = (keep.astype(F32) + got.astype(F32)).astype(BF)

time: 106 us -> 107 us (level)
  waiting for transfers between devices: 11.9 us -> 16 us
  Pallas kernels: 21.3 us -> 18.7 us
    ppermute x8, waiting for transfers between devices: 7.53 us -> 13.1 us  [ring(): return (lax.ppermute(fwd, 'dp', AHEAD), lax.ppermute(bwd, 'dp', BEHIND))]
    pallas_call x4 -> x3, Pallas kernels: 21.3 us -> 18.7 us  [call(): pl.pallas_call(kernel, out_shape=out, in_specs=[whole] * len(args), out_s...]
    add x1 -> x0, other arithmetic: 1.86 us -> none  [early(): own.astype(F32) + jnp.where(low, right, left).astype(F32)]
    all_to_all x1, waiting for transfers between devices: 1.47 us -> 0.01 us  [on_device(): back = lax.all_to_all(both, 'chip', split_axis=0, concat_axis=0, tiled=True)]
    convert_element_type x1, other arithmetic: 1.03 us -> 2.17 us  [on_device(): both = (keep.astype(F32) + got.astype(F32)).astype(BF)]
    convert_element_type x2 -> x3, other arithmetic: 3.13 us -> 4.15 us  [the longest x2 3.31 us: total(): (begun.reshape(2, half, columns).astype(F32) + then).astype(BF)]
  transfers between devices with their start and end apart: 11 -> 11, of which waited for: 4 -> 6; matrix products, arithmetic and copies ran while one was open for 6% -> 5% of each run, Pallas kernels for 6% -> 2%
where the time goes in v7:
time: 107 us; the launch traced here: 106 us
  blocking collectives  43.5 us (41%)
  Pallas kernels  18.7 us (17%)
  starting transfers between devices  18.1 us (17%)
  waiting for transfers between devices  16 us (15%)
  other arithmetic  7.3 us (7%)
  local copies, waits for them, and re-layouts  1.99 us (2%)
    all_to_all x1, blocking collectives, on_device(): mine = lax.all_to_all(sent, 'chip', split_axis=0, concat_axis=0, tiled=True)  43.5 us
    pallas_call x3, Pallas kernels, call(): pl.pallas_call(kernel, out_shape=out, in_specs=[whole] * len(args), out_s...  18.7 us
    ppermute x8, waiting for transfers between devices, ring(): return (lax.ppermute(fwd, 'dp', AHEAD), lax.ppermute(bwd, 'dp', BEHIND))  13.1 us
    ppermute x8, starting transfers between devices, ring(): return (lax.ppermute(fwd, 'dp', AHEAD), lax.ppermute(bwd, 'dp', BEHIND))  12.9 us
    all_to_all x1, starting transfers between devices, on_device(): back = lax.all_to_all(both, 'chip', split_axis=0, concat_axis=0, tiled=True)  4.92 us
    convert_element_type x2, other arithmetic, total(): (begun.reshape(2, half, columns).astype(F32) + then).astype(BF)  3.31 us
    ppermute x1, waiting for transfers between devices, on_device(): other = lax.ppermute(mine, 'core', swap)  2.84 us
    convert_element_type x1, other arithmetic, on_device(): both = (keep.astype(F32) + got.astype(F32)).astype(BF)  2.17 us
  transfers between devices with their start and end apart: 11, of which 6 were waited for; matrix products, arithmetic and copies ran while one was open for 5% of the time, Pallas kernels for 2%

profile of v7, /device:TPU:32, one launch (start us, length us, event | category | flops | bytes accessed | tf_op | source)
XLA Modules:
  0.0 106.2 jit_solution(7763318840647491901)
XLA Ops:
  0.6 2.8 %shard_map.102 = bf16[32,18,8,128]{3,2,1,0:T(8,128)(2,1)} custom-call(bf16[256,1024]{1,0:T(8,128)(2,1)} %x_ref.1, bf16[256,1024]{1,0:T(8,128)(2,1)} %g_ref.1, bf16[256]{0:T(256)(128)(2,1)} %gate_ref.3, s32[256]{0:T(256)} %expert_ref.3, s32[256]{0:T(256)} %slot_ref.3), custom_call_target="tpu_custom_call" | custom-call | tf_op jit(solution)/shard_map/pallas_call | solution.py:162
  3.4 43.5 %all_to_all.10.mine_ref = bf16[32,18,8,128]{3,2,1,0:T(8,128)(2,1)S(1)} all-to-all(bf16[32,18,8,128]{3,2,1,0:T(8,128)(2,1)} %shard_map.102), channel_id=1, replica_groups=mesh['chip'=32,'core'=2,'dp'=4] {'chip'}, dimensions={0} | all-to-all | bytes 2359296 | tf_op jit(solution)/shard_map/all_to_all | solution.py:226
  46.9 2.8 %collective-permute-done.other_ref = bf16[32,18,8,128]{3,2,1,0:T(8,128)(2,1)S(1)} collective-permute-done((bf16[32,18,8,128]{3,2,1,0:T(8,128)(2,1)S(1)}, bf16[32,18,8,128]{3,2,1,0:T(8,128)(2,1)S(1)}, u32[]{:S(2)}, u32[]{:S(2)}) %collective-permute-start) | collective-permute-done | bytes 1179680 | tf_op jit(solution)/shard_map/ppermute | solution.py:227
  49.8 1.0 copy-done.2
  50.8 13.5 %all.1 = (bf16[32,10,8,128]{3,2,1,0:T(8,128)(2,1)}, bf16[32,10,8,128]{3,2,1,0:T(8,128)(2,1)}, bf16[256,1024]{1,0:T(8,128)(2,1)}, bf16[256,1024]{1,0:T(8,128)(2,1...) custom-call(bf16[32,18,8,128]{3,2,1,0:T(8,128)(2,1)} %copy-done, ...), custom_call_target="tpu_custom_call" | custom-call | tf_op jit(solution)/shard_map/all/pallas_call | solution.py:162
  64.5 1.5 %collective-permute-start.7 = (bf16[256,1024]{1,0:T(8,128)(2,1)}, bf16[256,1024]{1,0:T(8,128)(2,1)S(1)}, u32[]{:S(2)}, u32[]{:S(2)}) collective-permute-start(bf16[256,1024]{1,0:T(8,128)(2,1)} %get-tuple-element.38), channel_id=1, source_target_pairs={{0,1},{1,2},{2,3},{3,0},{4,5},{5,6},{6,7},{7,4},{8,9},{9,10},{10,1... | collective-permute-start | bytes 1572872 | tf_op jit(solution)/shard_map/down_one/ppermute | solution.py:181
  66.1 1.7 %collective-permute-start.6 = (bf16[256,1024]{1,0:T(8,128)(2,1)}, bf16[256,1024]{1,0:T(8,128)(2,1)S(1)}, u32[]{:S(2)}, u32[]{:S(2)}) collective-permute-start(bf16[256,1024]{1,0:T(8,128)(2,1)} %get-tuple-element.37), channel_id=1, source_target_pairs={{0,3},{1,0},{2,1},{3,2},{4,7},{5,4},{6,5},{7,6},{8,11},{9,8},{10,9... | collective-permute-start | bytes 1572872 | tf_op jit(solution)/shard_map/down_one/ppermute | solution.py:181
  68.1 3.0 %collective-permute-start.3 = (bf16[256,1024]{1,0:T(8,128)(2,1)}, bf16[256,1024]{1,0:T(8,128)(2,1)S(1)}, u32[]{:S(2)}, u32[]{:S(2)}) collective-permute-start(bf16[256,1024]{1,0:T(8,128)(2,1)} %get-tuple-element.27), channel_id=1, source_target_pairs={{0,3},{1,0},{2,1},{3,2},{4,7},{5,4},{6,5},{7,6},{8,11},{9,8},{10,9... | collective-permute-start | bytes 1572872 | tf_op jit(solution)/shard_map/up_one/ppermute | solution.py:181
  71.0 2.2 %add_convert_fusion = bf16[32,10,8,128]{3,2,1,0:T(8,128)(2,1)} fusion(bf16[32,10,8,128]{3,2,1,0:T(8,128)(2,1)S(1)} %collective-permute-done.5, bf16[32,10,8,128]{3,2,1,0:T(8,128)(2,1)} %get-tuple-element.28), kind=kLoop, calls=%fused_computation | loop fusion | flops 1310720 | bytes 1966080 | tf_op jit(solution)/shard_map/convert_element_type | solution.py:261
  73.2 4.9 %all-to-all-start.1 = ((bf16[32,10,8,128]{3,2,1,0:T(8,128)(2,1)}), bf16[32,10,8,128]{3,2,1,0:T(8,128)(2,1)S(1)}, u32[]{:S(2)}, u32[]{:S(2)}) async-start(bf16[32,10,8,128]{3,2,1,0:T(8,128)(2,1)} %add_convert_fusion), calls=%async_computation.1 | async-start | bytes 1310720 | tf_op jit(solution)/shard_map/rows_back/all_to_all | solution.py:263
  78.2 2.5 %collective-permute-done.7 = bf16[256,1024]{1,0:T(8,128)(2,1)S(1)} collective-permute-done((bf16[256,1024]{1,0:T(8,128)(2,1)}, bf16[256,1024]{1,0:T(8,128)(2,1)S(1)}, u32[]{:S(2)}, u32[]{:S(2)}) %collective-permute-start.7) | collective-permute-done | bytes 524320 | tf_op jit(solution)/shard_map/down_one/ppermute | solution.py:181
  80.7 0.4 collective-permute-start.8
  81.2 3.0 %collective-permute-start.9 = (bf16[128,1024]{1,0:T(8,128)(2,1)S(1)}, bf16[128,1024]{1,0:T(8,128)(2,1)S(1)}, u32[]{:S(2)}, u32[]{:S(2)}) collective-permute-start(bf16[128,1024]{1,0:T(8,128)(2,1)S(1)} %add_convert_fusion.5), channel_id=1, source_target_pairs={{0,3},{1,0},{2,1},{3,2},{4,7},{5,4},{6,5},{7,6},{8,11},{9,8},{10,9... | collective-permute-start | bytes 786440 | tf_op jit(solution)/shard_map/down_two/ppermute | solution.py:181
  84.2 8.1 %collective-permute-done.3 = bf16[256,1024]{1,0:T(8,128)(2,1)S(1)} collective-permute-done((bf16[256,1024]{1,0:T(8,128)(2,1)}, bf16[256,1024]{1,0:T(8,128)(2,1)S(1)}, u32[]{:S(2)}, u32[]{:S(2)}) %collective-permute-start.3) | collective-permute-done | bytes 524320 | tf_op jit(solution)/shard_map/up_one/ppermute | solution.py:181
  92.3 3.0 %collective-permute-start.4 = (bf16[128,1024]{1,0:T(8,128)(2,1)S(1)}, bf16[128,1024]{1,0:T(8,128)(2,1)}, u32[]{:S(2)}, u32[]{:S(2)}) collective-permute-start(bf16[128,1024]{1,0:T(8,128)(2,1)S(1)} %add_convert_fusion.7), channel_id=1, source_target_pairs={{0,3},{1,0},{2,1},{3,2},{4,7},{5,4},{6,5},{7,6},{8,11},{9,8},{10,9... | collective-permute-start | bytes 786440 | tf_op jit(solution)/shard_map/up_two/ppermute | solution.py:181
  95.4 0.8 add_convert_fusion.8
  96.2 0.8 add_convert_fusion.3
  97.0 0.9 collective-permute-done.9
  97.9 1.1 %add_convert_fusion.2 = bf16[256,1024]{1,0:T(8,128)(2,1)} fusion(bf16[256,1024]{1,0:T(8,128)(2,1)S(1)} %get-tuple-element.44, pred[256]{0:T(512)(128)(4,1)S(1)} %broadcast_bitcast_fusion, bf16[128,1024]{1,0:T(8,128)(2,1)S(1)} %collective-permute-done.9, bf16[128,1024]{1,0:T(8,128)(2,1)S(1)} %collective-permute-done.8), kind=kLoop, calls=%fused_computation.2 | loop fusion | flops 1310720 | bytes 1573120 | tf_op jit(solution)/shard_map/convert_element_type | solution.py:202
  99.0 0.9 copy-done.1
  99.9 2.4 %unpack.1 = (bf16[256,1024]{1,0:T(8,128)(2,1)}, bf16[256]{0:T(256)(128)(2,1)}) custom-call(bf16[32,10,8,128]{3,2,1,0:T(8,128)(2,1)} %copy-done.1, bf16[256]{0:T(256)(128)(2,1)} %gate_ref.3, s32[256]{0:T(256)} %expert_ref.3, s32[256]{0:T(256)} %slot_ref.3), custom_call_target="tpu_custom_call" | custom-call | tf_op jit(solution)/shard_map/unpack/pallas_call | solution.py:162
  102.4 0.4 collective-permute-done.4
  102.7 1.3 %collective-permute-done.2 = bf16[128,1024]{1,0:T(8,128)(2,1)} collective-permute-done((bf16[128,1024]{1,0:T(8,128)(2,1)}, bf16[128,1024]{1,0:T(8,128)(2,1)}, u32[]{:S(2)}, u32[]{:S(2)}) %collective-permute-start.2) | collective-permute-done | bytes 262176 | tf_op jit(solution)/shard_map/up_two/ppermute | solution.py:181
  104.1 2.2 %fusion = bf16[1,256,1024]{2,1,0:T(8,128)(2,1)} fusion(bf16[256,1024]{1,0:T(8,128)(2,1)S(1)} %get-tuple-element.45, pred[256]{0:T(512)(128)(4,1)S(1)} %broadcast_bitcast_fusion, bf16[128,1024]{1,0:T(8,128)(2,1)} %collective-permute-done.4, bf16[128,1024]{1,0:T(8,128)(2,1)} %collective-permute-done.2), kind=kLoop, calls=%fused_computation.5 | loop fusion | flops 1310720 | bytes 1573120 | tf_op jit(solution)/shard_map/convert_element_type | solution.py:202
  (31 shorter events, 0.8 us)
Async XLA Ops:
  46.9 2.9 %copy-start = (bf16[32,18,8,128]{3,2,1,0:T(8,128)(2,1)}, bf16[32,18,8,128]{3,2,1,0:T(8,128)(2,1)S(1)}, u32[]{:S(2)}) copy-start(bf16[32,18,8,128]{3,2,1,0:T(8,128)(2,1)S(1)} %all_to_all.10.mine_ref) | copy-start | bytes 3538948
  46.9 2.8 %collective-permute-start = (bf16[32,18,8,128]{3,2,1,0:T(8,128)(2,1)S(1)}, bf16[32,18,8,128]{3,2,1,0:T(8,128)(2,1)S(1)}, u32[]{:S(2)}, u32[]{:S(2)}) collective-permute-start(bf16[32,18,8,128]{3,2,1,0:T(8,128)(2,1)S(1)} %all_to_all.10.mine_ref), channel_id=1, source_target_pairs={{0,4},{4,0},{1,5},{5,1},{2,6},{6,2},{3,7},{7,3},{8,12},{12,8},{9,1... | collective-permute-start | bytes 3538952 | tf_op jit(solution)/shard_map/ppermute | solution.py:227
  49.8 1.0 copy-start.2
  64.2 6.8 %collective-permute-start.5 = (bf16[32,10,8,128]{3,2,1,0:T(8,128)(2,1)}, bf16[32,10,8,128]{3,2,1,0:T(8,128)(2,1)S(1)}, u32[]{:S(2)}, u32[]{:S(2)}) collective-permute-start(bf16[32,10,8,128]{3,2,1,0:T(8,128)(2,1)} %get-tuple-element.29), channel_id=1, source_target_pairs={{0,4},{4,0},{1,5},{5,1},{2,6},{6,2},{3,7},{7,3},{8,12},{12,8},{9,1... | collective-permute-start | bytes 1966088 | tf_op jit(solution)/shard_map/swap_back/ppermute | solution.py:258
  64.5 16.2 %collective-permute-start.7 = (bf16[256,1024]{1,0:T(8,128)(2,1)}, bf16[256,1024]{1,0:T(8,128)(2,1)S(1)}, u32[]{:S(2)}, u32[]{:S(2)}) collective-permute-start(bf16[256,1024]{1,0:T(8,128)(2,1)} %get-tuple-element.38), channel_id=1, source_target_pairs={{0,1},{1,2},{2,3},{3,0},{4,5},{5,6},{6,7},{7,4},{8,9},{9,10},{10,1... | collective-permute-start | bytes 1572872 | tf_op jit(solution)/shard_map/down_one/ppermute | solution.py:181
  66.1 15.1 %collective-permute-start.6 = (bf16[256,1024]{1,0:T(8,128)(2,1)}, bf16[256,1024]{1,0:T(8,128)(2,1)S(1)}, u32[]{:S(2)}, u32[]{:S(2)}) collective-permute-start(bf16[256,1024]{1,0:T(8,128)(2,1)} %get-tuple-element.37), channel_id=1, source_target_pairs={{0,3},{1,0},{2,1},{3,2},{4,7},{5,4},{6,5},{7,6},{8,11},{9,8},{10,9... | collective-permute-start | bytes 1572872 | tf_op jit(solution)/shard_map/down_one/ppermute | solution.py:181
  67.8 27.6 %collective-permute-start.1 = (bf16[256,1024]{1,0:T(8,128)(2,1)}, bf16[256,1024]{1,0:T(8,128)(2,1)S(1)}, u32[]{:S(2)}, u32[]{:S(2)}) collective-permute-start(bf16[256,1024]{1,0:T(8,128)(2,1)} %get-tuple-element.25), channel_id=1, source_target_pairs={{0,1},{1,2},{2,3},{3,0},{4,5},{5,6},{6,7},{7,4},{8,9},{9,10},{10,1... | collective-permute-start | bytes 1572872 | tf_op jit(solution)/shard_map/up_one/ppermute | solution.py:181
  68.1 24.2 %collective-permute-start.3 = (bf16[256,1024]{1,0:T(8,128)(2,1)}, bf16[256,1024]{1,0:T(8,128)(2,1)S(1)}, u32[]{:S(2)}, u32[]{:S(2)}) collective-permute-start(bf16[256,1024]{1,0:T(8,128)(2,1)} %get-tuple-element.27), channel_id=1, source_target_pairs={{0,3},{1,0},{2,1},{3,2},{4,7},{5,4},{6,5},{7,6},{8,11},{9,8},{10,9... | collective-permute-start | bytes 1572872 | tf_op jit(solution)/shard_map/up_one/ppermute | solution.py:181
  71.0 9.6 %copy-start.8 = (bf16[128,1024]{1,0:T(8,128)(2,1)S(1)}, bf16[128,1024]{1,0:T(8,128)(2,1)}, u32[]{:S(2)}) copy-start(bf16[128,1024]{1,0:T(8,128)(2,1)} %get-tuple-element.39) | copy-start | bytes 786436
  73.2 7.9 %copy-start.7 = (bf16[128,1024]{1,0:T(8,128)(2,1)S(1)}, bf16[128,1024]{1,0:T(8,128)(2,1)}, u32[]{:S(2)}) copy-start(bf16[128,1024]{1,0:T(8,128)(2,1)} %get-tuple-element.40) | copy-start | bytes 786436
  73.2 19.1 %copy-start.6 = (bf16[128,1024]{1,0:T(8,128)(2,1)S(1)}, bf16[128,1024]{1,0:T(8,128)(2,1)}, u32[]{:S(2)}) copy-start(bf16[128,1024]{1,0:T(8,128)(2,1)} %get-tuple-element.26) | copy-start | bytes 786436
  73.2 25.8 %all-to-all-start.1 = ((bf16[32,10,8,128]{3,2,1,0:T(8,128)(2,1)}), bf16[32,10,8,128]{3,2,1,0:T(8,128)(2,1)S(1)}, u32[]{:S(2)}, u32[]{:S(2)}) async-start(bf16[32,10,8,128]{3,2,1,0:T(8,128)(2,1)} %add_convert_fusion), calls=%async_computation.1 | async-start | bytes 1310720 | tf_op jit(solution)/shard_map/rows_back/all_to_all | solution.py:263
  78.2 17.2 %copy-start.5 = (bf16[128,1024]{1,0:T(8,128)(2,1)S(1)}, bf16[128,1024]{1,0:T(8,128)(2,1)}, u32[]{:S(2)}) copy-start(bf16[128,1024]{1,0:T(8,128)(2,1)} %get-tuple-element.24) | copy-start | bytes 786436
  80.7 15.4 %copy-start.3 = (bf16[256,1024]{1,0:T(8,128)(2,1)S(1)}, bf16[256,1024]{1,0:T(8,128)(2,1)}, u32[]{:S(2)}) copy-start(bf16[256,1024]{1,0:T(8,128)(2,1)} %get-tuple-element.36) | copy-start | bytes 1572868
  80.7 15.4 %copy-start.4 = (bf16[256,1024]{1,0:T(8,128)(2,1)S(1)}, bf16[256,1024]{1,0:T(8,128)(2,1)}, u32[]{:S(2)}) copy-start(bf16[256,1024]{1,0:T(8,128)(2,1)} %get-tuple-element.33) | copy-start | bytes 1572868
  80.7 16.3 %collective-permute-start.8 = (bf16[128,1024]{1,0:T(8,128)(2,1)S(1)}, bf16[128,1024]{1,0:T(8,128)(2,1)S(1)}, u32[]{:S(2)}, u32[]{:S(2)}) collective-permute-start(bf16[128,1024]{1,0:T(8,128)(2,1)S(1)} %add_convert_fusion.6), channel_id=1, source_target_pairs={{0,1},{1,2},{2,3},{3,0},{4,5},{5,6},{6,7},{7,4},{8,9},{9,10},{10,1... | collective-permute-start | bytes 786440 | tf_op jit(solution)/shard_map/down_two/ppermute | solution.py:181
  81.2 16.7 %collective-permute-start.9 = (bf16[128,1024]{1,0:T(8,128)(2,1)S(1)}, bf16[128,1024]{1,0:T(8,128)(2,1)S(1)}, u32[]{:S(2)}, u32[]{:S(2)}) collective-permute-start(bf16[128,1024]{1,0:T(8,128)(2,1)S(1)} %add_convert_fusion.5), channel_id=1, source_target_pairs={{0,3},{1,0},{2,1},{3,2},{4,7},{5,4},{6,5},{7,6},{8,11},{9,8},{10,9... | collective-permute-start | bytes 786440 | tf_op jit(solution)/shard_map/down_two/ppermute | solution.py:181
  92.3 10.4 %collective-permute-start.4 = (bf16[128,1024]{1,0:T(8,128)(2,1)S(1)}, bf16[128,1024]{1,0:T(8,128)(2,1)}, u32[]{:S(2)}, u32[]{:S(2)}) collective-permute-start(bf16[128,1024]{1,0:T(8,128)(2,1)S(1)} %add_convert_fusion.7), channel_id=1, source_target_pairs={{0,3},{1,0},{2,1},{3,2},{4,7},{5,4},{6,5},{7,6},{8,11},{9,8},{10,9... | collective-permute-start | bytes 786440 | tf_op jit(solution)/shard_map/up_two/ppermute | solution.py:181
  96.2 7.9 %collective-permute-start.2 = (bf16[128,1024]{1,0:T(8,128)(2,1)}, bf16[128,1024]{1,0:T(8,128)(2,1)}, u32[]{:S(2)}, u32[]{:S(2)}) collective-permute-start(bf16[128,1024]{1,0:T(8,128)(2,1)} %add_convert_fusion.8), channel_id=1, source_target_pairs={{0,1},{1,2},{2,3},{3,0},{4,5},{5,6},{6,7},{7,4},{8,9},{9,10},{10,1... | collective-permute-start | bytes 786440 | tf_op jit(solution)/shard_map/up_two/ppermute | solution.py:181
  99.0 0.9 copy-start.1

commit v8 on v6

--- a/solution.py
+++ b/solution.py
@@ -9,7 +9,7 @@
 
 BF = jnp.bfloat16
 F32 = jnp.float32
-VMEM = 56 * 1024 * 1024
+MIB = 1024 * 1024
 LANES = 128
 
 
@@ -160,7 +160,7 @@
     gate_out_ref[...] = (total / gate).astype(BF).reshape(count)
 
 
-def call(kernel, out, scratch, *args):
+def call(kernel, room, out, scratch, *args):
     whole = pl.BlockSpec(memory_space=pltpu.VMEM)
     return pl.pallas_call(
         kernel,
@@ -168,7 +168,7 @@
         in_specs=[whole] * len(args),
         out_specs=jax.tree.map(lambda _: whole, out),
         scratch_shapes=scratch,
-        compiler_params=pltpu.CompilerParams(vmem_limit_bytes=VMEM),
+        compiler_params=pltpu.CompilerParams(vmem_limit_bytes=room * MIB),
     )(*args)
 
 
@@ -217,6 +217,7 @@
     swap = [(0, 1), (1, 0)]
     sent = call(
         pack_kernel,
+        10,
         shape(groups, 18, 8, LANES),
         [pltpu.VMEM((rows, width), F32), turn],
         tokens_in,
@@ -241,6 +242,7 @@
     with jax.named_scope("expert_input"):
       xs, dh, keep, give, *down = call(
         expert_kernel,
+        28,
         (shape(2 * rows, width), shape(2 * rows, hidden), shape(groups, 10, 8, LANES), shape(groups, 10, 8, LANES))
         + parts(hidden, width),
         [pltpu.VMEM((2 * rows, LANES), F32), pltpu.VMEM((2 * rows, width), BF),
@@ -259,7 +261,7 @@
     with jax.named_scope("swap_back"):
       got = lax.ppermute(give, "core", swap)
     with jax.named_scope("up"):
-      up = call(up_kernel, parts(width, hidden), [], xs, dh)
+      up = call(up_kernel, 12, parts(width, hidden), [], xs, dh)
     with jax.named_scope("up_one"):
       left_u, right_u = ring(up[0], up[1])
     both = (keep.astype(F32) + got.astype(F32)).astype(BF)
@@ -275,6 +277,7 @@
     with jax.named_scope("unpack"):
       in_grad, gate_grad = call(
           unpack_kernel,
+          8,
           (shape(count, width), shape(count)),
           [pltpu.VMEM((rows, width), BF), turn],
           back,

time: 106 us -> 102 us (0.962)
  Pallas kernels: 21.3 us -> 11.9 us
  other arithmetic: 7.81 us -> 10.3 us
  local copies, waits for them, and re-layouts: 2 us -> 4.19 us
  waiting for transfers between devices: 11.9 us -> 13.5 us
    pallas_call x4, Pallas kernels: 21.3 us -> 11.9 us  [call(): pl.pallas_call(kernel, out_shape=out, in_specs=[whole] * len(args), out_s...]
    ppermute x8, waiting for transfers between devices: 7.53 us -> 10.6 us  [ring(): return (lax.ppermute(fwd, 'dp', AHEAD), lax.ppermute(bwd, 'dp', BEHIND))]
    unnamed x22 -> x20, local copies, waits for them, and re-layouts: 1.92 us -> 4.12 us
    convert_element_type x2, other arithmetic: 0.84 us -> 2.74 us  [second(): fwd = (parts[2].astype(F32) + left[:half].astype(F32)).astype(BF)]
    all_to_all x1, waiting for transfers between devices: 1.47 us -> 0.01 us  [on_device(): back = lax.all_to_all(both, 'chip', split_axis=0, concat_axis=0, tiled=True)]
    convert_element_type x2, other arithmetic: 0.94 us -> 2.03 us  [second(): bwd = (parts[3].astype(F32) + right[half:].astype(F32)).astype(BF)]
  transfers between devices with their start and end apart: 11 -> 11, of which waited for: 4 -> 4; matrix products, arithmetic and copies ran while one was open for 6% -> 9% of each run, Pallas kernels for 6% -> 3%
where the time goes in v8:
time: 102 us
  blocking collectives  43.4 us (43%)
  starting transfers between devices  17.9 us (18%)
  waiting for transfers between devices  13.5 us (13%)
  Pallas kernels  11.9 us (12%)
  other arithmetic  10.3 us (10%)
  local copies, waits for them, and re-layouts  4.19 us (4%)
    all_to_all x1, blocking collectives, on_device(): mine = lax.all_to_all(sent, 'chip', split_axis=0, concat_axis=0, tiled=True)  43.4 us
    ppermute x8, starting transfers between devices, ring(): return (lax.ppermute(fwd, 'dp', AHEAD), lax.ppermute(bwd, 'dp', BEHIND))  12.9 us
    pallas_call x4, Pallas kernels, call(): pl.pallas_call(kernel, out_shape=out, in_specs=[whole] * len(args), out_s...  11.9 us
    ppermute x8, waiting for transfers between devices, ring(): return (lax.ppermute(fwd, 'dp', AHEAD), lax.ppermute(bwd, 'dp', BEHIND))  10.6 us
    all_to_all x1, starting transfers between devices, on_device(): back = lax.all_to_all(both, 'chip', split_axis=0, concat_axis=0, tiled=True)  4.79 us
    unnamed x20, local copies, waits for them, and re-layouts  4.12 us
    ppermute x1, waiting for transfers between devices, on_device(): other = lax.ppermute(mine, 'core', swap)  2.84 us
    convert_element_type x2, other arithmetic, second(): fwd = (parts[2].astype(F32) + left[:half].astype(F32)).astype(BF)  2.74 us
  transfers between devices with their start and end apart: 11, of which 4 were waited for; matrix products, arithmetic and copies ran while one was open for 9% of the time, Pallas kernels for 3%

profile of v8, /device:TPU:32, one launch (start us, length us, event | category | flops | bytes accessed | tf_op | source)
XLA Modules:
  0.0 101.9 jit_solution(11413300568536056557)
XLA Ops:
  0.6 1.0 %copy-done.2 = bf16[256,1024]{1,0:T(8,128)(2,1)S(1)} copy-done((bf16[256,1024]{1,0:T(8,128)(2,1)S(1)}, bf16[256,1024]{1,0:T(8,128)(2,1)}, u32[]{:S(2)}) %copy-start.2) | copy-done | bytes 524312
  1.7 1.0 %copy-done.3 = bf16[256,1024]{1,0:T(8,128)(2,1)S(1)} copy-done((bf16[256,1024]{1,0:T(8,128)(2,1)S(1)}, bf16[256,1024]{1,0:T(8,128)(2,1)}, u32[]{:S(2)}) %copy-start.3) | copy-done | bytes 524312
  5.3 43.4 %all_to_all.10.mine_ref = bf16[32,18,8,128]{3,2,1,0:T(8,128)(2,1)S(1)} all-to-all(bf16[32,18,8,128]{3,2,1,0:T(8,128)(2,1)S(1)} %shard_map.102), channel_id=1, replica_groups=mesh['chip'=32,'core'=2,'dp'=4] {'chip'}, dimensions={0} | all-to-all | bytes 2359296 | tf_op jit(solution)/shard_map/all_to_all | solution.py:229
  48.7 2.8 %collective-permute-done.other_ref = bf16[32,18,8,128]{3,2,1,0:T(8,128)(2,1)S(1)} collective-permute-done((bf16[32,18,8,128]{3,2,1,0:T(8,128)(2,1)S(1)}, bf16[32,18,8,128]{3,2,1,0:T(8,128)(2,1)S(1)}, u32[]{:S(2)}, u32[]{:S(2)}) %collective-permute-start) | collective-permute-done | bytes 1179680 | tf_op jit(solution)/shard_map/ppermute | solution.py:230
  51.6 7.8 %expert_input.1 = (bf16[576,1024]{1,0:T(8,128)(2,1)S(1)}, bf16[576,1024]{1,0:T(8,128)(2,1)S(1)}, bf16[32,10,8,128]{3,2,1,0:T(8,128)(2,1)S(1)}, bf16[32,10,8,128]...) custom-call(bf16[32,18,8,128]{3,2,1,0:T(8,128)(2,1)S(1)} %all_to_all, ...), custom_call_target="tpu_custom_call" | custom-call | tf_op jit(solution)/shard_map/expert_input/pallas_call | solution.py:165
  59.6 1.5 %collective-permute-start.7 = (bf16[256,1024]{1,0:T(8,128)(2,1)}, bf16[256,1024]{1,0:T(8,128)(2,1)}, u32[]{:S(2)}, u32[]{:S(2)}) collective-permute-start(bf16[256,1024]{1,0:T(8,128)(2,1)} %get-tuple-element.42), channel_id=1, source_target_pairs={{0,1},{1,2},{2,3},{3,0},{4,5},{5,6},{6,7},{7,4},{8,9},{9,10},{10,1... | collective-permute-start | bytes 1572872 | tf_op jit(solution)/shard_map/down_one/ppermute | solution.py:184
  61.2 1.7 %collective-permute-start.6 = (bf16[256,1024]{1,0:T(8,128)(2,1)S(1)}, bf16[256,1024]{1,0:T(8,128)(2,1)}, u32[]{:S(2)}, u32[]{:S(2)}) collective-permute-start(bf16[256,1024]{1,0:T(8,128)(2,1)S(1)} %get-tuple-element.41), channel_id=1, source_target_pairs={{0,3},{1,0},{2,1},{3,2},{4,7},{5,4},{6,5},{7,6},{8,11},{9,8},{10,9... | collective-permute-start | bytes 1572872 | tf_op jit(solution)/shard_map/down_one/ppermute | solution.py:184
  62.9 2.2 %up.1 = (bf16[256,1024]{1,0:T(8,128)(2,1)}, bf16[256,1024]{1,0:T(8,128)(2,1)}, bf16[128,1024]{1,0:T(8,128)(2,1)S(1)}, bf16[128,1024]{1,0:T(8,128)(2,1)S(1)}, bf16[256,1024]{1,0:T(8,128)(2,1)S(1)}) custom-call(bf16[576,1024]{1,0:T(8,128)(2,1)S(1)} %get-tuple-element.26.xs, bf16[576,1024]{1,0:T(8,128)(2,1)S(1)} %get-tuple-element.27.dh), custom_call_target="tpu_custom_call" | custom-call | tf_op jit(solution)/shard_map/up/pallas_call | solution.py:165
  65.4 3.0 %collective-permute-start.3 = (bf16[256,1024]{1,0:T(8,128)(2,1)}, bf16[256,1024]{1,0:T(8,128)(2,1)}, u32[]{:S(2)}, u32[]{:S(2)}) collective-permute-start(bf16[256,1024]{1,0:T(8,128)(2,1)} %get-tuple-element.31), channel_id=1, source_target_pairs={{0,3},{1,0},{2,1},{3,2},{4,7},{5,4},{6,5},{7,6},{8,11},{9,8},{10,9... | collective-permute-start | bytes 1572872 | tf_op jit(solution)/shard_map/up_one/ppermute | solution.py:184
  68.4 1.0 %add_convert_fusion = bf16[32,10,8,128]{3,2,1,0:T(8,128)(2,1)} fusion(bf16[32,10,8,128]{3,2,1,0:T(8,128)(2,1)S(1)} %collective-permute-done.5, bf16[32,10,8,128]{3,2,1,0:T(8,128)(2,1)S(1)} %get-tuple-element.32), kind=kLoop, calls=%fused_computation | loop fusion | flops 1310720 | bytes 1966080 | tf_op jit(solution)/shard_map/convert_element_type | solution.py:267
  69.4 4.8 %all-to-all-start.1 = ((bf16[32,10,8,128]{3,2,1,0:T(8,128)(2,1)}), bf16[32,10,8,128]{3,2,1,0:T(8,128)(2,1)S(1)}, u32[]{:S(2)}, u32[]{:S(2)}) async-start(bf16[32,10,8,128]{3,2,1,0:T(8,128)(2,1)} %add_convert_fusion), calls=%async_computation.1 | async-start | bytes 1310720 | tf_op jit(solution)/shard_map/rows_back/all_to_all | solution.py:269
  74.2 1.7 %collective-permute-done.7 = bf16[256,1024]{1,0:T(8,128)(2,1)} collective-permute-done((bf16[256,1024]{1,0:T(8,128)(2,1)}, bf16[256,1024]{1,0:T(8,128)(2,1)}, u32[]{:S(2)}, u32[]{:S(2)}) %collective-permute-start.7) | collective-permute-done | bytes 524320 | tf_op jit(solution)/shard_map/down_one/ppermute | solution.py:184
  75.9 1.0 add_convert_fusion.4
  77.3 1.0 add_convert_fusion.3
  78.3 3.0 %collective-permute-start.9 = (bf16[128,1024]{1,0:T(8,128)(2,1)S(1)}, bf16[128,1024]{1,0:T(8,128)(2,1)S(1)}, u32[]{:S(2)}, u32[]{:S(2)}) collective-permute-start(bf16[128,1024]{1,0:T(8,128)(2,1)S(1)} %add_convert_fusion.3), channel_id=1, source_target_pairs={{0,3},{1,0},{2,1},{3,2},{4,7},{5,4},{6,5},{7,6},{8,11},{9,8},{10,9... | collective-permute-start | bytes 786440 | tf_op jit(solution)/shard_map/down_two/ppermute | solution.py:184
  81.3 6.0 %collective-permute-done.3 = bf16[256,1024]{1,0:T(8,128)(2,1)} collective-permute-done((bf16[256,1024]{1,0:T(8,128)(2,1)}, bf16[256,1024]{1,0:T(8,128)(2,1)}, u32[]{:S(2)}, u32[]{:S(2)}) %collective-permute-start.3) | collective-permute-done | bytes 524320 | tf_op jit(solution)/shard_map/up_one/ppermute | solution.py:184
  87.3 1.0 add_convert_fusion.5
  88.3 3.0 %collective-permute-start.4 = (bf16[128,1024]{1,0:T(8,128)(2,1)S(1)}, bf16[128,1024]{1,0:T(8,128)(2,1)S(1)}, u32[]{:S(2)}, u32[]{:S(2)}) collective-permute-start(bf16[128,1024]{1,0:T(8,128)(2,1)S(1)} %add_convert_fusion.5), channel_id=1, source_target_pairs={{0,3},{1,0},{2,1},{3,2},{4,7},{5,4},{6,5},{7,6},{8,11},{9,8},{10,9... | collective-permute-start | bytes 786440 | tf_op jit(solution)/shard_map/up_two/ppermute | solution.py:184
  91.3 1.7 %add_convert_fusion.6 = bf16[128,1024]{1,0:T(8,128)(2,1)} fusion(bf16[128,1024]{1,0:T(8,128)(2,1)S(1)} %get-tuple-element.28, bf16[256,1024]{1,0:T(8,128)(2,1)} %collective-permute-done.1), kind=kLoop, calls=%fused_computation.11 | loop fusion | flops 524288 | bytes 786432 | tf_op jit(solution)/shard_map/convert_element_type | solution.py:189
  93.1 2.3 %convert_add_fusion = (f32[256,1024]{1,0:T(8,128)S(1)}, f32[256,1024]{1,0:T(8,128)S(1)}) fusion(bf16[256,1024]{1,0:T(8,128)(2,1)S(1)} %get-tuple-element.40, bf16[256,1024]{1,0:T(8,128)(2,1)} %collective-permute-done.6, bf16[256,1024]{1,0:T(8,128)(2,1)} %collective-permute-done.7, pred[256]{0:T(512)(128)(4,1)S(1)} %iota_compare_fusion, ...), kind=kLoop, calls=%fused_computation.3 | loop fusion | flops 2097152 | bytes 5243136 | tf_op jit(solution)/shard_map/add | solution.py:196
  95.5 1.1 %add_convert_fusion.2 = bf16[256,1024]{1,0:T(8,128)(2,1)} fusion(f32[256,1024]{1,0:T(8,128)S(1)} %get-tuple-element.48, pred[256]{0:T(512)(128)(4,1)S(1)} %broadcast_bitcast_fusion, bf16[128,1024]{1,0:T(8,128)(2,1)S(1)} %collective-permute-done.9, bf16[128,1024]{1,0:T(8,128)(2,1)S(1)} %collective-permute-done.8), kind=kLoop, calls=%fused_computation.2 | loop fusion | flops 1048576 | bytes 2097408 | tf_op jit(solution)/shard_map/convert_element_type | solution.py:204
  96.6 1.3 %unpack.1 = (bf16[256,1024]{1,0:T(8,128)(2,1)}, bf16[256]{0:T(256)(128)(2,1)}) custom-call(bf16[32,10,8,128]{3,2,1,0:T(8,128)(2,1)S(1)} %all-to-all-done.1.back_ref, bf16[256]{0:T(256)(128)(2,1)S(1)} %copy-done.9, s32[256]{0:T(256)S(1)} %copy-done.5, s32[256]{0:T(256)S(1)} %copy-done.7), custom_call_target="tpu_custom_call" | custom-call | tf_op jit(solution)/shard_map/unpack/pallas_call | solution.py:165
  97.9 2.9 %collective-permute-done.2 = bf16[128,1024]{1,0:T(8,128)(2,1)S(1)} collective-permute-done((bf16[128,1024]{1,0:T(8,128)(2,1)}, bf16[128,1024]{1,0:T(8,128)(2,1)S(1)}, u32[]{:S(2)}, u32[]{:S(2)}) %collective-permute-start.2) | collective-permute-done | bytes 262176 | tf_op jit(solution)/shard_map/up_two/ppermute | solution.py:184
  100.9 1.1 %fusion = bf16[1,256,1024]{2,1,0:T(8,128)(2,1)} fusion(f32[256,1024]{1,0:T(8,128)S(1)} %get-tuple-element.49, pred[256]{0:T(512)(128)(4,1)S(1)} %broadcast_bitcast_fusion, bf16[128,1024]{1,0:T(8,128)(2,1)S(1)} %collective-permute-done.4, bf16[128,1024]{1,0:T(8,128)(2,1)S(1)} %collective-permute-done.2), kind=kLoop, calls=%fused_computation.5 | loop fusion | flops 1048576 | bytes 2097408 | tf_op jit(solution)/shard_map/convert_element_type | solution.py:204
  (34 shorter events, 3.6 us)
Async XLA Ops:
  0.6 1.0 %copy-start.2 = (bf16[256,1024]{1,0:T(8,128)(2,1)S(1)}, bf16[256,1024]{1,0:T(8,128)(2,1)}, u32[]{:S(2)}) copy-start(bf16[256,1024]{1,0:T(8,128)(2,1)} %x_ref.1) | copy-start | bytes 1572868
  1.7 1.0 %copy-start.3 = (bf16[256,1024]{1,0:T(8,128)(2,1)S(1)}, bf16[256,1024]{1,0:T(8,128)(2,1)}, u32[]{:S(2)}) copy-start(bf16[256,1024]{1,0:T(8,128)(2,1)} %g_ref.1) | copy-start | bytes 1572868
  2.7 0.7 copy-start.4
  3.4 0.7 copy-start.6
  4.1 0.7 copy-start.8
  4.7 46.8 %copy-start.1 = (bf16[1,1024,1024]{2,1,0:T(8,128)(2,1)S(1)}, bf16[1,1024,1024]{2,1,0:T(8,128)(2,1)}, u32[]{:S(2)}) copy-start(bf16[1,1024,1024]{2,1,0:T(8,128)(2,1)} %down_ref.1) | copy-start | bytes 6291460
  5.3 46.3 %copy-start = (bf16[1,1024,1024]{2,1,0:T(8,128)(2,1)S(1)}, bf16[1,1024,1024]{2,1,0:T(8,128)(2,1)}, u32[]{:S(2)}) copy-start(bf16[1,1024,1024]{2,1,0:T(8,128)(2,1)} %up_ref.1) | copy-start | bytes 6291460
  48.7 2.8 %collective-permute-start = (bf16[32,18,8,128]{3,2,1,0:T(8,128)(2,1)S(1)}, bf16[32,18,8,128]{3,2,1,0:T(8,128)(2,1)S(1)}, u32[]{:S(2)}, u32[]{:S(2)}) collective-permute-start(bf16[32,18,8,128]{3,2,1,0:T(8,128)(2,1)S(1)} %all_to_all.10.mine_ref), channel_id=1, source_target_pairs={{0,4},{4,0},{1,5},{5,1},{2,6},{6,2},{3,7},{7,3},{8,12},{12,8},{9,1... | collective-permute-start | bytes 3538952 | tf_op jit(solution)/shard_map/ppermute | solution.py:230
  59.4 9.0 %collective-permute-start.5 = (bf16[32,10,8,128]{3,2,1,0:T(8,128)(2,1)S(1)}, bf16[32,10,8,128]{3,2,1,0:T(8,128)(2,1)S(1)}, u32[]{:S(2)}, u32[]{:S(2)}) collective-permute-start(bf16[32,10,8,128]{3,2,1,0:T(8,128)(2,1)S(1)} %get-tuple-element.33), channel_id=1, source_target_pairs={{0,4},{4,0},{1,5},{5,1},{2,6},{6,2},{3,7},{7,3},{8,12},{12,8},{9,1... | collective-permute-start | bytes 1966088 | tf_op jit(solution)/shard_map/swap_back/ppermute | solution.py:262
  59.6 16.3 %collective-permute-start.7 = (bf16[256,1024]{1,0:T(8,128)(2,1)}, bf16[256,1024]{1,0:T(8,128)(2,1)}, u32[]{:S(2)}, u32[]{:S(2)}) collective-permute-start(bf16[256,1024]{1,0:T(8,128)(2,1)} %get-tuple-element.42), channel_id=1, source_target_pairs={{0,1},{1,2},{2,3},{3,0},{4,5},{5,6},{6,7},{7,4},{8,9},{9,10},{10,1... | collective-permute-start | bytes 1572872 | tf_op jit(solution)/shard_map/down_one/ppermute | solution.py:184
  61.2 16.1 %collective-permute-start.6 = (bf16[256,1024]{1,0:T(8,128)(2,1)S(1)}, bf16[256,1024]{1,0:T(8,128)(2,1)}, u32[]{:S(2)}, u32[]{:S(2)}) collective-permute-start(bf16[256,1024]{1,0:T(8,128)(2,1)S(1)} %get-tuple-element.41), channel_id=1, source_target_pairs={{0,3},{1,0},{2,1},{3,2},{4,7},{5,4},{6,5},{7,6},{8,11},{9,8},{10,9... | collective-permute-start | bytes 1572872 | tf_op jit(solution)/shard_map/down_one/ppermute | solution.py:184
  65.1 26.2 %collective-permute-start.1 = (bf16[256,1024]{1,0:T(8,128)(2,1)}, bf16[256,1024]{1,0:T(8,128)(2,1)}, u32[]{:S(2)}, u32[]{:S(2)}) collective-permute-start(bf16[256,1024]{1,0:T(8,128)(2,1)} %get-tuple-element.29), channel_id=1, source_target_pairs={{0,1},{1,2},{2,3},{3,0},{4,5},{5,6},{6,7},{7,4},{8,9},{9,10},{10,1... | collective-permute-start | bytes 1572872 | tf_op jit(solution)/shard_map/up_one/ppermute | solution.py:184
  65.4 21.9 %collective-permute-start.3 = (bf16[256,1024]{1,0:T(8,128)(2,1)}, bf16[256,1024]{1,0:T(8,128)(2,1)}, u32[]{:S(2)}, u32[]{:S(2)}) collective-permute-start(bf16[256,1024]{1,0:T(8,128)(2,1)} %get-tuple-element.31), channel_id=1, source_target_pairs={{0,3},{1,0},{2,1},{3,2},{4,7},{5,4},{6,5},{7,6},{8,11},{9,8},{10,9... | collective-permute-start | bytes 1572872 | tf_op jit(solution)/shard_map/up_one/ppermute | solution.py:184
  69.4 27.2 %all-to-all-start.1 = ((bf16[32,10,8,128]{3,2,1,0:T(8,128)(2,1)}), bf16[32,10,8,128]{3,2,1,0:T(8,128)(2,1)S(1)}, u32[]{:S(2)}, u32[]{:S(2)}) async-start(bf16[32,10,8,128]{3,2,1,0:T(8,128)(2,1)} %add_convert_fusion), calls=%async_computation.1 | async-start | bytes 1310720 | tf_op jit(solution)/shard_map/rows_back/all_to_all | solution.py:269
  76.9 18.5 %collective-permute-start.8 = (bf16[128,1024]{1,0:T(8,128)(2,1)S(1)}, bf16[128,1024]{1,0:T(8,128)(2,1)S(1)}, u32[]{:S(2)}, u32[]{:S(2)}) collective-permute-start(bf16[128,1024]{1,0:T(8,128)(2,1)S(1)} %add_convert_fusion.4), channel_id=1, source_target_pairs={{0,1},{1,2},{2,3},{3,0},{4,5},{5,6},{6,7},{7,4},{8,9},{9,10},{10,1... | collective-permute-start | bytes 786440 | tf_op jit(solution)/shard_map/down_two/ppermute | solution.py:184
  78.3 17.2 %collective-permute-start.9 = (bf16[128,1024]{1,0:T(8,128)(2,1)S(1)}, bf16[128,1024]{1,0:T(8,128)(2,1)S(1)}, u32[]{:S(2)}, u32[]{:S(2)}) collective-permute-start(bf16[128,1024]{1,0:T(8,128)(2,1)S(1)} %add_convert_fusion.3), channel_id=1, source_target_pairs={{0,3},{1,0},{2,1},{3,2},{4,7},{5,4},{6,5},{7,6},{8,11},{9,8},{10,9... | collective-permute-start | bytes 786440 | tf_op jit(solution)/shard_map/down_two/ppermute | solution.py:184
  88.3 9.6 %collective-permute-start.4 = (bf16[128,1024]{1,0:T(8,128)(2,1)S(1)}, bf16[128,1024]{1,0:T(8,128)(2,1)S(1)}, u32[]{:S(2)}, u32[]{:S(2)}) collective-permute-start(bf16[128,1024]{1,0:T(8,128)(2,1)S(1)} %add_convert_fusion.5), channel_id=1, source_target_pairs={{0,3},{1,0},{2,1},{3,2},{4,7},{5,4},{6,5},{7,6},{8,11},{9,8},{10,9... | collective-permute-start | bytes 786440 | tf_op jit(solution)/shard_map/up_two/ppermute | solution.py:184
  93.1 7.8 %collective-permute-start.2 = (bf16[128,1024]{1,0:T(8,128)(2,1)}, bf16[128,1024]{1,0:T(8,128)(2,1)S(1)}, u32[]{:S(2)}, u32[]{:S(2)}) collective-permute-start(bf16[128,1024]{1,0:T(8,128)(2,1)} %add_convert_fusion.6), channel_id=1, source_target_pairs={{0,1},{1,2},{2,3},{3,0},{4,5},{5,6},{6,7},{7,4},{8,9},{9,10},{10,1... | collective-permute-start | bytes 786440 | tf_op jit(solution)/shard_map/up_two/ppermute | solution.py:184
  95.4 1.2 %copy-start.5 = (s32[256]{0:T(256)S(1)}, s32[256]{0:T(256)}, u32[]{:S(2)}) copy-start(s32[256]{0:T(256)} %expert_ref.3) | copy-start | bytes 3076
  95.4 1.2 %copy-start.7 = (s32[256]{0:T(256)S(1)}, s32[256]{0:T(256)}, u32[]{:S(2)}) copy-start(s32[256]{0:T(256)} %slot_ref.3) | copy-start | bytes 3076
  95.4 1.1 %copy-start.9 = (bf16[256]{0:T(256)(128)(2,1)S(1)}, bf16[256]{0:T(256)(128)(2,1)}, u32[]{:S(2)}) copy-start(bf16[256]{0:T(256)(128)(2,1)} %gate_ref.3) | copy-start | bytes 1540

commit v9 on v8

--- a/solution.py
+++ b/solution.py
@@ -191,17 +191,14 @@
     return fwd, bwd
 
 
-def early(own, left, right):
-    low = lax.broadcasted_iota(jnp.int32, own.shape, 0) < own.shape[0] // 2
-    return lax.optimization_barrier(own.astype(F32) + jnp.where(low, right, left).astype(F32))
-
-
-def total(begun, left2, right2):
+def total(own, left, right, left2, right2):
     half, columns = left2.shape
+    split = lambda a: a.reshape(2, half, columns)
     both = lambda a: jnp.broadcast_to(a[None], (2, half, columns))
     low = lax.broadcasted_iota(jnp.int32, (2, half, columns), 0) == 0
+    first = jnp.where(low, split(right), split(left)).astype(F32)
     then = jnp.where(low, both(left2), both(right2)).astype(F32)
-    return (begun.reshape(2, half, columns) + then).astype(BF).reshape(2 * half, columns)
+    return (split(own).astype(F32) + first + then).astype(BF).reshape(2 * half, columns)
 
 
 def after(value, earlier):
@@ -217,7 +214,7 @@
     swap = [(0, 1), (1, 0)]
     sent = call(
         pack_kernel,
-        10,
+        56,
         shape(groups, 18, 8, LANES),
         [pltpu.VMEM((rows, width), F32), turn],
         tokens_in,
@@ -273,7 +270,7 @@
     up2 = second(up, left_u, right_u)
     with jax.named_scope("up_two"):
       left_u2, right_u2 = ring(*up2)
-    down_grad = total(early(down[4], left_d, right_d), left_d2, right_d2)
+    down_grad = total(down[4], left_d, right_d, left_d2, right_d2)
     with jax.named_scope("unpack"):
       in_grad, gate_grad = call(
           unpack_kernel,
@@ -287,7 +284,7 @@
       )
     left_u2, right_u2, in_grad = lax.optimization_barrier((left_u2, right_u2, in_grad))
     left_u2, right_u2, down_grad = lax.optimization_barrier((left_u2, right_u2, down_grad))
-    up_grad = total(early(up[4], left_u, right_u), left_u2, right_u2)
+    up_grad = total(up[4], left_u, right_u, left_u2, right_u2)
     return (in_grad, gate_grad, up_grad[None], down_grad[None])
 
 

time: 102 us -> 101 us (level)
  local copies, waits for them, and re-layouts: 4.19 us -> 0.09 us
  Pallas kernels: 11.9 us -> 14.3 us
  waiting for transfers between devices: 13.5 us -> 15.3 us
  starting transfers between devices: 17.9 us -> 16.8 us
    unnamed x20 -> x10, local copies, waits for them, and re-layouts: 4.12 us -> 0.02 us
    convert_element_type x2, other arithmetic: 2.18 us -> 4.99 us  [total(): (split(own).astype(F32) + first + then).astype(BF)]
    pallas_call x4, Pallas kernels: 11.9 us -> 14.3 us  [call(): pl.pallas_call(kernel, out_shape=out, in_specs=[whole] * len(args), out_s...]
    add x1 -> x0, other arithmetic: 2.32 us -> none  [early(): own.astype(F32) + jnp.where(low, right, left).astype(F32)]
    ppermute x8, waiting for transfers between devices: 10.6 us -> 12.5 us  [ring(): return (lax.ppermute(fwd, 'dp', AHEAD), lax.ppermute(bwd, 'dp', BEHIND))]
    ppermute x8, starting transfers between devices: 12.9 us -> 11.8 us  [ring(): return (lax.ppermute(fwd, 'dp', AHEAD), lax.ppermute(bwd, 'dp', BEHIND))]
  transfers between devices with their start and end apart: 11 -> 11, of which waited for: 4 -> 6; matrix products, arithmetic and copies ran while one was open for 9% -> 8% of each run, Pallas kernels for 3% -> 4%
where the time goes in v9:
time: 101 us
  blocking collectives  43.6 us (43%)
  starting transfers between devices  16.8 us (17%)
  waiting for transfers between devices  15.3 us (15%)
  Pallas kernels  14.3 us (14%)
  other arithmetic  10.1 us (10%)
    all_to_all x1, blocking collectives, on_device(): mine = lax.all_to_all(sent, 'chip', split_axis=0, concat_axis=0, tiled=True)  43.6 us
    pallas_call x4, Pallas kernels, call(): pl.pallas_call(kernel, out_shape=out, in_specs=[whole] * len(args), out_s...  14.3 us
    ppermute x8, waiting for transfers between devices, ring(): return (lax.ppermute(fwd, 'dp', AHEAD), lax.ppermute(bwd, 'dp', BEHIND))  12.5 us
    ppermute x8, starting transfers between devices, ring(): return (lax.ppermute(fwd, 'dp', AHEAD), lax.ppermute(bwd, 'dp', BEHIND))  11.8 us
    convert_element_type x2, other arithmetic, total(): (split(own).astype(F32) + first + then).astype(BF)  4.99 us
    all_to_all x1, starting transfers between devices, on_device(): back = lax.all_to_all(both, 'chip', split_axis=0, concat_axis=0, tiled=True)  4.79 us
    ppermute x1, waiting for transfers between devices, on_device(): other = lax.ppermute(mine, 'core', swap)  2.84 us
    convert_element_type x2, other arithmetic, second(): bwd = (parts[3].astype(F32) + right[half:].astype(F32)).astype(BF)  2.03 us
  transfers between devices with their start and end apart: 11, of which 6 were waited for; matrix products, arithmetic and copies ran while one was open for 8% of the time, Pallas kernels for 4%

profile of v9, /device:TPU:32, one launch (start us, length us, event | category | flops | bytes accessed | tf_op | source)
XLA Modules:
  0.0 100.9 jit_solution(8957669096857553956)
XLA Ops:
  0.6 3.0 %shard_map.102 = bf16[32,18,8,128]{3,2,1,0:T(8,128)(2,1)} custom-call(bf16[256,1024]{1,0:T(8,128)(2,1)} %x_ref.1, bf16[256,1024]{1,0:T(8,128)(2,1)} %g_ref.1, bf16[256]{0:T(256)(128)(2,1)} %gate_ref.3, s32[256]{0:T(256)} %expert_ref.3, s32[256]{0:T(256)} %slot_ref.3), custom_call_target="tpu_custom_call" | custom-call | tf_op jit(solution)/shard_map/pallas_call | solution.py:165
  3.6 43.6 %all_to_all.10.mine_ref = bf16[32,18,8,128]{3,2,1,0:T(8,128)(2,1)S(1)} all-to-all(bf16[32,18,8,128]{3,2,1,0:T(8,128)(2,1)} %shard_map.102), channel_id=1, replica_groups=mesh['chip'=32,'core'=2,'dp'=4] {'chip'}, dimensions={0} | all-to-all | bytes 2359296 | tf_op jit(solution)/shard_map/all_to_all | solution.py:226
  47.2 2.8 %collective-permute-done.other_ref = bf16[32,18,8,128]{3,2,1,0:T(8,128)(2,1)S(1)} collective-permute-done((bf16[32,18,8,128]{3,2,1,0:T(8,128)(2,1)S(1)}, bf16[32,18,8,128]{3,2,1,0:T(8,128)(2,1)S(1)}, u32[]{:S(2)}, u32[]{:S(2)}) %collective-permute-start) | collective-permute-done | bytes 1179680 | tf_op jit(solution)/shard_map/ppermute | solution.py:227
  50.1 7.8 %expert_input.1 = (bf16[576,1024]{1,0:T(8,128)(2,1)S(1)}, bf16[576,1024]{1,0:T(8,128)(2,1)S(1)}, bf16[32,10,8,128]{3,2,1,0:T(8,128)(2,1)S(1)}, bf16[32,10,8,128]...) custom-call(bf16[32,18,8,128]{3,2,1,0:T(8,128)(2,1)S(1)} %all_to_all, ...), custom_call_target="tpu_custom_call" | custom-call | tf_op jit(solution)/shard_map/expert_input/pallas_call | solution.py:165
  58.1 1.5 %collective-permute-start.7 = (bf16[256,1024]{1,0:T(8,128)(2,1)}, bf16[256,1024]{1,0:T(8,128)(2,1)}, u32[]{:S(2)}, u32[]{:S(2)}) collective-permute-start(bf16[256,1024]{1,0:T(8,128)(2,1)} %get-tuple-element.42), channel_id=1, source_target_pairs={{0,1},{1,2},{2,3},{3,0},{4,5},{5,6},{6,7},{7,4},{8,9},{9,10},{10,1... | collective-permute-start | bytes 1572872 | tf_op jit(solution)/shard_map/down_one/ppermute | solution.py:184
  59.6 1.8 %collective-permute-start.6 = (bf16[256,1024]{1,0:T(8,128)(2,1)S(1)}, bf16[256,1024]{1,0:T(8,128)(2,1)}, u32[]{:S(2)}, u32[]{:S(2)}) collective-permute-start(bf16[256,1024]{1,0:T(8,128)(2,1)S(1)} %get-tuple-element.41), channel_id=1, source_target_pairs={{0,3},{1,0},{2,1},{3,2},{4,7},{5,4},{6,5},{7,6},{8,11},{9,8},{10,9... | collective-permute-start | bytes 1572872 | tf_op jit(solution)/shard_map/down_one/ppermute | solution.py:184
  61.3 2.2 %up.1 = (bf16[256,1024]{1,0:T(8,128)(2,1)}, bf16[256,1024]{1,0:T(8,128)(2,1)}, bf16[128,1024]{1,0:T(8,128)(2,1)S(1)}, bf16[128,1024]{1,0:T(8,128)(2,1)S(1)}, bf16[256,1024]{1,0:T(8,128)(2,1)S(1)}) custom-call(bf16[576,1024]{1,0:T(8,128)(2,1)S(1)} %get-tuple-element.26.xs, bf16[576,1024]{1,0:T(8,128)(2,1)S(1)} %get-tuple-element.27.dh), custom_call_target="tpu_custom_call" | custom-call | tf_op jit(solution)/shard_map/up/pallas_call | solution.py:165
  63.5 1.6 %collective-permute-start.3 = (bf16[256,1024]{1,0:T(8,128)(2,1)}, bf16[256,1024]{1,0:T(8,128)(2,1)}, u32[]{:S(2)}, u32[]{:S(2)}) collective-permute-start(bf16[256,1024]{1,0:T(8,128)(2,1)} %get-tuple-element.31), channel_id=1, source_target_pairs={{0,3},{1,0},{2,1},{3,2},{4,7},{5,4},{6,5},{7,6},{8,11},{9,8},{10,9... | collective-permute-start | bytes 1572872 | tf_op jit(solution)/shard_map/up_one/ppermute | solution.py:184
  65.1 0.5 collective-permute-start.1
  65.6 1.0 %add_convert_fusion = bf16[32,10,8,128]{3,2,1,0:T(8,128)(2,1)} fusion(bf16[32,10,8,128]{3,2,1,0:T(8,128)(2,1)S(1)} %collective-permute-done.5, bf16[32,10,8,128]{3,2,1,0:T(8,128)(2,1)S(1)} %get-tuple-element.32), kind=kLoop, calls=%fused_computation | loop fusion | flops 1310720 | bytes 1966080 | tf_op jit(solution)/shard_map/convert_element_type | solution.py:264
  66.6 4.8 %all-to-all-start.1 = ((bf16[32,10,8,128]{3,2,1,0:T(8,128)(2,1)}), bf16[32,10,8,128]{3,2,1,0:T(8,128)(2,1)S(1)}, u32[]{:S(2)}, u32[]{:S(2)}) async-start(bf16[32,10,8,128]{3,2,1,0:T(8,128)(2,1)} %add_convert_fusion), calls=%async_computation.1 | async-start | bytes 1310720 | tf_op jit(solution)/shard_map/rows_back/all_to_all | solution.py:266
  71.4 3.0 %collective-permute-done.7 = bf16[256,1024]{1,0:T(8,128)(2,1)} collective-permute-done((bf16[256,1024]{1,0:T(8,128)(2,1)}, bf16[256,1024]{1,0:T(8,128)(2,1)}, u32[]{:S(2)}, u32[]{:S(2)}) %collective-permute-start.7) | collective-permute-done | bytes 524320 | tf_op jit(solution)/shard_map/down_one/ppermute | solution.py:184
  74.4 1.0 %add_convert_fusion.4 = bf16[128,1024]{1,0:T(8,128)(2,1)S(1)} fusion(bf16[128,1024]{1,0:T(8,128)(2,1)S(1)} %get-tuple-element.43, bf16[256,1024]{1,0:T(8,128)(2,1)} %collective-permute-done.7), kind=kLoop, calls=%fused_computation.7 | loop fusion | flops 524288 | bytes 786432 | tf_op jit(solution)/shard_map/convert_element_type | solution.py:189
  75.8 1.0 %add_convert_fusion.3 = bf16[128,1024]{1,0:T(8,128)(2,1)S(1)} fusion(bf16[128,1024]{1,0:T(8,128)(2,1)S(1)} %get-tuple-element.44, bf16[256,1024]{1,0:T(8,128)(2,1)} %collective-permute-done.6), kind=kLoop, calls=%fused_computation.6 | loop fusion | flops 524288 | bytes 786432 | tf_op jit(solution)/shard_map/convert_element_type | solution.py:190
  76.8 3.0 %collective-permute-start.9 = (bf16[128,1024]{1,0:T(8,128)(2,1)S(1)}, bf16[128,1024]{1,0:T(8,128)(2,1)S(1)}, u32[]{:S(2)}, u32[]{:S(2)}) collective-permute-start(bf16[128,1024]{1,0:T(8,128)(2,1)S(1)} %add_convert_fusion.3), channel_id=1, source_target_pairs={{0,3},{1,0},{2,1},{3,2},{4,7},{5,4},{6,5},{7,6},{8,11},{9,8},{10,9... | collective-permute-start | bytes 786440 | tf_op jit(solution)/shard_map/down_two/ppermute | solution.py:184
  79.8 5.9 %collective-permute-done.3 = bf16[256,1024]{1,0:T(8,128)(2,1)} collective-permute-done((bf16[256,1024]{1,0:T(8,128)(2,1)}, bf16[256,1024]{1,0:T(8,128)(2,1)}, u32[]{:S(2)}, u32[]{:S(2)}) %collective-permute-start.3) | collective-permute-done | bytes 524320 | tf_op jit(solution)/shard_map/up_one/ppermute | solution.py:184
  85.7 1.0 %add_convert_fusion.5 = bf16[128,1024]{1,0:T(8,128)(2,1)S(1)} fusion(bf16[128,1024]{1,0:T(8,128)(2,1)S(1)} %get-tuple-element.30, bf16[256,1024]{1,0:T(8,128)(2,1)} %collective-permute-done.3), kind=kLoop, calls=%fused_computation.8 | loop fusion | flops 524288 | bytes 786432 | tf_op jit(solution)/shard_map/convert_element_type | solution.py:190
  86.7 3.0 %collective-permute-start.4 = (bf16[128,1024]{1,0:T(8,128)(2,1)S(1)}, bf16[128,1024]{1,0:T(8,128)(2,1)S(1)}, u32[]{:S(2)}, u32[]{:S(2)}) collective-permute-start(bf16[128,1024]{1,0:T(8,128)(2,1)S(1)} %add_convert_fusion.5), channel_id=1, source_target_pairs={{0,3},{1,0},{2,1},{3,2},{4,7},{5,4},{6,5},{7,6},{8,11},{9,8},{10,9... | collective-permute-start | bytes 786440 | tf_op jit(solution)/shard_map/up_two/ppermute | solution.py:184
  89.8 1.0 %add_convert_fusion.6 = bf16[128,1024]{1,0:T(8,128)(2,1)S(1)} fusion(bf16[128,1024]{1,0:T(8,128)(2,1)S(1)} %get-tuple-element.28, bf16[256,1024]{1,0:T(8,128)(2,1)} %collective-permute-done.1), kind=kLoop, calls=%fused_computation.9 | loop fusion | flops 524288 | bytes 786432 | tf_op jit(solution)/shard_map/convert_element_type | solution.py:189
  91.2 2.5 %add_convert_fusion.2 = bf16[256,1024]{1,0:T(8,128)(2,1)} fusion(bf16[256,1024]{1,0:T(8,128)(2,1)S(1)} %get-tuple-element.40, bf16[256,1024]{1,0:T(8,128)(2,1)} %collective-permute-done.6, bf16[256,1024]{1,0:T(8,128)(2,1)} %collective-permute-done.7, pred[256]{0:T(512)(128)(4,1)S(1)} %broadcast_bitcast_fusion, ...), kind=kLoop, calls=%fused_computation.2 | loop fusion | flops 2097152 | bytes 2621696 | tf_op jit(solution)/shard_map/convert_element_type | solution.py:201
  93.8 1.3 %unpack.1 = (bf16[256,1024]{1,0:T(8,128)(2,1)}, bf16[256]{0:T(256)(128)(2,1)}) custom-call(bf16[32,10,8,128]{3,2,1,0:T(8,128)(2,1)S(1)} %all-to-all-done.1.back_ref, bf16[256]{0:T(256)(128)(2,1)S(1)} %copy-done.4, s32[256]{0:T(256)S(1)} %copy-done.2, s32[256]{0:T(256)S(1)} %copy-done.3), custom_call_target="tpu_custom_call" | custom-call | tf_op jit(solution)/shard_map/unpack/pallas_call | solution.py:165
  95.1 0.9 collective-permute-done.4
  96.0 2.5 %collective-permute-done.2 = bf16[128,1024]{1,0:T(8,128)(2,1)S(1)} collective-permute-done((bf16[128,1024]{1,0:T(8,128)(2,1)S(1)}, bf16[128,1024]{1,0:T(8,128)(2,1)S(1)}, u32[]{:S(2)}, u32[]{:S(2)}) %collective-permute-start.2) | collective-permute-done | bytes 262176 | tf_op jit(solution)/shard_map/up_two/ppermute | solution.py:184
  98.5 2.5 %fusion = bf16[1,256,1024]{2,1,0:T(8,128)(2,1)} fusion(bf16[256,1024]{1,0:T(8,128)(2,1)S(1)} %get-tuple-element.37, bf16[256,1024]{1,0:T(8,128)(2,1)} %collective-permute-done.3, bf16[256,1024]{1,0:T(8,128)(2,1)} %collective-permute-done.1, pred[256]{0:T(512)(128)(4,1)S(1)} %broadcast_bitcast_fusion, bf16[128,1024]{1,0:T(8,128)(2,1)S(1)} %collective-permute-done.4, ...), kind=kLoop, calls=%fused_computation.3 | loop fusion | flops 2097152 | bytes 2621696 | tf_op jit(solution)/shard_map/convert_element_type | solution.py:201
  (22 shorter events, 1.0 us)
Async XLA Ops:
  0.6 49.4 %copy-start.1 = (bf16[1,1024,1024]{2,1,0:T(8,128)(2,1)S(1)}, bf16[1,1024,1024]{2,1,0:T(8,128)(2,1)}, u32[]{:S(2)}) copy-start(bf16[1,1024,1024]{2,1,0:T(8,128)(2,1)} %down_ref.1) | copy-start | bytes 6291460
  3.6 46.5 %copy-start = (bf16[1,1024,1024]{2,1,0:T(8,128)(2,1)S(1)}, bf16[1,1024,1024]{2,1,0:T(8,128)(2,1)}, u32[]{:S(2)}) copy-start(bf16[1,1024,1024]{2,1,0:T(8,128)(2,1)} %up_ref.1) | copy-start | bytes 6291460
  47.2 2.8 %collective-permute-start = (bf16[32,18,8,128]{3,2,1,0:T(8,128)(2,1)S(1)}, bf16[32,18,8,128]{3,2,1,0:T(8,128)(2,1)S(1)}, u32[]{:S(2)}, u32[]{:S(2)}) collective-permute-start(bf16[32,18,8,128]{3,2,1,0:T(8,128)(2,1)S(1)} %all_to_all.10.mine_ref), channel_id=1, source_target_pairs={{0,4},{4,0},{1,5},{5,1},{2,6},{6,2},{3,7},{7,3},{8,12},{12,8},{9,1... | collective-permute-start | bytes 3538952 | tf_op jit(solution)/shard_map/ppermute | solution.py:227
  57.9 7.7 %collective-permute-start.5 = (bf16[32,10,8,128]{3,2,1,0:T(8,128)(2,1)S(1)}, bf16[32,10,8,128]{3,2,1,0:T(8,128)(2,1)S(1)}, u32[]{:S(2)}, u32[]{:S(2)}) collective-permute-start(bf16[32,10,8,128]{3,2,1,0:T(8,128)(2,1)S(1)} %get-tuple-element.33), channel_id=1, source_target_pairs={{0,4},{4,0},{1,5},{5,1},{2,6},{6,2},{3,7},{7,3},{8,12},{12,8},{9,1... | collective-permute-start | bytes 1966088 | tf_op jit(solution)/shard_map/swap_back/ppermute | solution.py:259
  58.1 16.3 %collective-permute-start.7 = (bf16[256,1024]{1,0:T(8,128)(2,1)}, bf16[256,1024]{1,0:T(8,128)(2,1)}, u32[]{:S(2)}, u32[]{:S(2)}) collective-permute-start(bf16[256,1024]{1,0:T(8,128)(2,1)} %get-tuple-element.42), channel_id=1, source_target_pairs={{0,1},{1,2},{2,3},{3,0},{4,5},{5,6},{6,7},{7,4},{8,9},{9,10},{10,1... | collective-permute-start | bytes 1572872 | tf_op jit(solution)/shard_map/down_one/ppermute | solution.py:184
  59.6 16.2 %collective-permute-start.6 = (bf16[256,1024]{1,0:T(8,128)(2,1)S(1)}, bf16[256,1024]{1,0:T(8,128)(2,1)}, u32[]{:S(2)}, u32[]{:S(2)}) collective-permute-start(bf16[256,1024]{1,0:T(8,128)(2,1)S(1)} %get-tuple-element.41), channel_id=1, source_target_pairs={{0,3},{1,0},{2,1},{3,2},{4,7},{5,4},{6,5},{7,6},{8,11},{9,8},{10,9... | collective-permute-start | bytes 1572872 | tf_op jit(solution)/shard_map/down_one/ppermute | solution.py:184
  63.5 22.2 %collective-permute-start.3 = (bf16[256,1024]{1,0:T(8,128)(2,1)}, bf16[256,1024]{1,0:T(8,128)(2,1)}, u32[]{:S(2)}, u32[]{:S(2)}) collective-permute-start(bf16[256,1024]{1,0:T(8,128)(2,1)} %get-tuple-element.31), channel_id=1, source_target_pairs={{0,3},{1,0},{2,1},{3,2},{4,7},{5,4},{6,5},{7,6},{8,11},{9,8},{10,9... | collective-permute-start | bytes 1572872 | tf_op jit(solution)/shard_map/up_one/ppermute | solution.py:184
  65.1 24.7 %collective-permute-start.1 = (bf16[256,1024]{1,0:T(8,128)(2,1)}, bf16[256,1024]{1,0:T(8,128)(2,1)}, u32[]{:S(2)}, u32[]{:S(2)}) collective-permute-start(bf16[256,1024]{1,0:T(8,128)(2,1)} %get-tuple-element.29), channel_id=1, source_target_pairs={{0,1},{1,2},{2,3},{3,0},{4,5},{5,6},{6,7},{7,4},{8,9},{9,10},{10,1... | collective-permute-start | bytes 1572872 | tf_op jit(solution)/shard_map/up_one/ppermute | solution.py:184
  66.6 27.2 %all-to-all-start.1 = ((bf16[32,10,8,128]{3,2,1,0:T(8,128)(2,1)}), bf16[32,10,8,128]{3,2,1,0:T(8,128)(2,1)S(1)}, u32[]{:S(2)}, u32[]{:S(2)}) async-start(bf16[32,10,8,128]{3,2,1,0:T(8,128)(2,1)} %add_convert_fusion), calls=%async_computation.1 | async-start | bytes 1310720 | tf_op jit(solution)/shard_map/rows_back/all_to_all | solution.py:266
  75.4 15.6 %collective-permute-start.8 = (bf16[128,1024]{1,0:T(8,128)(2,1)S(1)}, bf16[128,1024]{1,0:T(8,128)(2,1)S(1)}, u32[]{:S(2)}, u32[]{:S(2)}) collective-permute-start(bf16[128,1024]{1,0:T(8,128)(2,1)S(1)} %add_convert_fusion.4), channel_id=1, source_target_pairs={{0,1},{1,2},{2,3},{3,0},{4,5},{5,6},{6,7},{7,4},{8,9},{9,10},{10,1... | collective-permute-start | bytes 786440 | tf_op jit(solution)/shard_map/down_two/ppermute | solution.py:184
  76.8 14.5 %collective-permute-start.9 = (bf16[128,1024]{1,0:T(8,128)(2,1)S(1)}, bf16[128,1024]{1,0:T(8,128)(2,1)S(1)}, u32[]{:S(2)}, u32[]{:S(2)}) collective-permute-start(bf16[128,1024]{1,0:T(8,128)(2,1)S(1)} %add_convert_fusion.3), channel_id=1, source_target_pairs={{0,3},{1,0},{2,1},{3,2},{4,7},{5,4},{6,5},{7,6},{8,11},{9,8},{10,9... | collective-permute-start | bytes 786440 | tf_op jit(solution)/shard_map/down_two/ppermute | solution.py:184
  86.7 9.2 %collective-permute-start.4 = (bf16[128,1024]{1,0:T(8,128)(2,1)S(1)}, bf16[128,1024]{1,0:T(8,128)(2,1)S(1)}, u32[]{:S(2)}, u32[]{:S(2)}) collective-permute-start(bf16[128,1024]{1,0:T(8,128)(2,1)S(1)} %add_convert_fusion.5), channel_id=1, source_target_pairs={{0,3},{1,0},{2,1},{3,2},{4,7},{5,4},{6,5},{7,6},{8,11},{9,8},{10,9... | collective-permute-start | bytes 786440 | tf_op jit(solution)/shard_map/up_two/ppermute | solution.py:184
  90.8 7.7 %collective-permute-start.2 = (bf16[128,1024]{1,0:T(8,128)(2,1)S(1)}, bf16[128,1024]{1,0:T(8,128)(2,1)S(1)}, u32[]{:S(2)}, u32[]{:S(2)}) collective-permute-start(bf16[128,1024]{1,0:T(8,128)(2,1)S(1)} %add_convert_fusion.6), channel_id=1, source_target_pairs={{0,1},{1,2},{2,3},{3,0},{4,5},{5,6},{6,7},{7,4},{8,9},{9,10},{10,1... | collective-permute-start | bytes 786440 | tf_op jit(solution)/shard_map/up_two/ppermute | solution.py:184
  91.2 2.5 %copy-start.2 = (s32[256]{0:T(256)S(1)}, s32[256]{0:T(256)}, u32[]{:S(2)}) copy-start(s32[256]{0:T(256)} %expert_ref.3) | copy-start | bytes 3076
  91.2 2.5 %copy-start.3 = (s32[256]{0:T(256)S(1)}, s32[256]{0:T(256)}, u32[]{:S(2)}) copy-start(s32[256]{0:T(256)} %slot_ref.3) | copy-start | bytes 3076
  91.2 2.5 %copy-start.4 = (bf16[256]{0:T(256)(128)(2,1)S(1)}, bf16[256]{0:T(256)(128)(2,1)}, u32[]{:S(2)}) copy-start(bf16[256]{0:T(256)(128)(2,1)} %gate_ref.3) | copy-start | bytes 1540

commit v10 on v8

--- a/solution.py
+++ b/solution.py
@@ -193,7 +193,8 @@
 
 def early(own, left, right):
     low = lax.broadcasted_iota(jnp.int32, own.shape, 0) < own.shape[0] // 2
-    return lax.optimization_barrier(own.astype(F32) + jnp.where(low, right, left).astype(F32))
+    begun = own.astype(F32) + jnp.where(low, right, left).astype(F32)
+    return lax.optimization_barrier(begun.astype(BF))
 
 
 def total(begun, left2, right2):
@@ -201,7 +202,7 @@
     both = lambda a: jnp.broadcast_to(a[None], (2, half, columns))
     low = lax.broadcasted_iota(jnp.int32, (2, half, columns), 0) == 0
     then = jnp.where(low, both(left2), both(right2)).astype(F32)
-    return (begun.reshape(2, half, columns) + then).astype(BF).reshape(2 * half, columns)
+    return (begun.reshape(2, half, columns).astype(F32) + then).astype(BF).reshape(2 * half, columns)
 
 
 def after(value, earlier):
@@ -217,7 +218,7 @@
     swap = [(0, 1), (1, 0)]
     sent = call(
         pack_kernel,
-        10,
+        56,
         shape(groups, 18, 8, LANES),
         [pltpu.VMEM((rows, width), F32), turn],
         tokens_in,

time: 102 us -> 100 us (0.980)
  local copies, waits for them, and re-layouts: 4.19 us -> 0.1 us
  Pallas kernels: 11.9 us -> 14.3 us
    unnamed x20 -> x10, local copies, waits for them, and re-layouts: 4.12 us -> 0.03 us
    convert_element_type x2 -> x3, other arithmetic: 2.18 us -> 4.62 us  [the longest x1 2.34 us: early(): return lax.optimization_barrier(begun.astype(BF))]
    pallas_call x4, Pallas kernels: 11.9 us -> 14.3 us  [call(): pl.pallas_call(kernel, out_shape=out, in_specs=[whole] * len(args), out_s...]
    add x1 -> x0, other arithmetic: 2.32 us -> none  [early(): own.astype(F32) + jnp.where(low, right, left).astype(F32)]
  transfers between devices with their start and end apart: 11 -> 11, of which waited for: 4 -> 5; matrix products, arithmetic and copies ran while one was open for 9% -> 9% of each run, Pallas kernels for 3% -> 4%
where the time goes in v10:
time: 100 us; the launch traced here: 99.7 us
  blocking collectives  43.6 us (44%)
  starting transfers between devices  18 us (18%)
  Pallas kernels  14.3 us (14%)
  waiting for transfers between devices  13.2 us (13%)
  other arithmetic  9.72 us (10%)
    all_to_all x1, blocking collectives, on_device(): mine = lax.all_to_all(sent, 'chip', split_axis=0, concat_axis=0, tiled=True)  43.6 us
    pallas_call x4, Pallas kernels, call(): pl.pallas_call(kernel, out_shape=out, in_specs=[whole] * len(args), out_s...  14.3 us
    ppermute x8, starting transfers between devices, ring(): return (lax.ppermute(fwd, 'dp', AHEAD), lax.ppermute(bwd, 'dp', BEHIND))  13 us
    ppermute x8, waiting for transfers between devices, ring(): return (lax.ppermute(fwd, 'dp', AHEAD), lax.ppermute(bwd, 'dp', BEHIND))  10.3 us
    all_to_all x1, starting transfers between devices, on_device(): back = lax.all_to_all(both, 'chip', split_axis=0, concat_axis=0, tiled=True)  4.79 us
    ppermute x1, waiting for transfers between devices, on_device(): other = lax.ppermute(mine, 'core', swap)  2.84 us
    convert_element_type x1, other arithmetic, early(): return lax.optimization_barrier(begun.astype(BF))  2.34 us
    convert_element_type x2, other arithmetic, total(): (begun.reshape(2, half, columns).astype(F32) + then).astype(BF)  2.29 us
  transfers between devices with their start and end apart: 11, of which 5 were waited for; matrix products, arithmetic and copies ran while one was open for 9% of the time, Pallas kernels for 4%

profile of v10, /device:TPU:32, one launch (start us, length us, event | category | flops | bytes accessed | tf_op | source)
XLA Modules:
  0.0 99.7 jit_solution(16553368158549008782)
XLA Ops:
  0.6 3.0 %shard_map.102 = bf16[32,18,8,128]{3,2,1,0:T(8,128)(2,1)} custom-call(bf16[256,1024]{1,0:T(8,128)(2,1)} %x_ref.1, bf16[256,1024]{1,0:T(8,128)(2,1)} %g_ref.1, bf16[256]{0:T(256)(128)(2,1)} %gate_ref.3, s32[256]{0:T(256)} %expert_ref.3, s32[256]{0:T(256)} %slot_ref.3), custom_call_target="tpu_custom_call" | custom-call | tf_op jit(solution)/shard_map/pallas_call | solution.py:165
  3.6 43.6 %all_to_all.10.mine_ref = bf16[32,18,8,128]{3,2,1,0:T(8,128)(2,1)S(1)} all-to-all(bf16[32,18,8,128]{3,2,1,0:T(8,128)(2,1)} %shard_map.102), channel_id=1, replica_groups=mesh['chip'=32,'core'=2,'dp'=4] {'chip'}, dimensions={0} | all-to-all | bytes 2359296 | tf_op jit(solution)/shard_map/all_to_all | solution.py:230
  47.2 2.8 %collective-permute-done.other_ref = bf16[32,18,8,128]{3,2,1,0:T(8,128)(2,1)S(1)} collective-permute-done((bf16[32,18,8,128]{3,2,1,0:T(8,128)(2,1)S(1)}, bf16[32,18,8,128]{3,2,1,0:T(8,128)(2,1)S(1)}, u32[]{:S(2)}, u32[]{:S(2)}) %collective-permute-start) | collective-permute-done | bytes 1179680 | tf_op jit(solution)/shard_map/ppermute | solution.py:231
  50.1 7.8 %expert_input.1 = (bf16[576,1024]{1,0:T(8,128)(2,1)S(1)}, bf16[576,1024]{1,0:T(8,128)(2,1)S(1)}, bf16[32,10,8,128]{3,2,1,0:T(8,128)(2,1)S(1)}, bf16[32,10,8,128]...) custom-call(bf16[32,18,8,128]{3,2,1,0:T(8,128)(2,1)S(1)} %all_to_all, ...), custom_call_target="tpu_custom_call" | custom-call | tf_op jit(solution)/shard_map/expert_input/pallas_call | solution.py:165
  58.1 1.5 %collective-permute-start.7 = (bf16[256,1024]{1,0:T(8,128)(2,1)}, bf16[256,1024]{1,0:T(8,128)(2,1)}, u32[]{:S(2)}, u32[]{:S(2)}) collective-permute-start(bf16[256,1024]{1,0:T(8,128)(2,1)} %get-tuple-element.42), channel_id=1, source_target_pairs={{0,1},{1,2},{2,3},{3,0},{4,5},{5,6},{6,7},{7,4},{8,9},{9,10},{10,1... | collective-permute-start | bytes 1572872 | tf_op jit(solution)/shard_map/down_one/ppermute | solution.py:184
  59.7 1.8 %collective-permute-start.6 = (bf16[256,1024]{1,0:T(8,128)(2,1)S(1)}, bf16[256,1024]{1,0:T(8,128)(2,1)}, u32[]{:S(2)}, u32[]{:S(2)}) collective-permute-start(bf16[256,1024]{1,0:T(8,128)(2,1)S(1)} %get-tuple-element.41), channel_id=1, source_target_pairs={{0,3},{1,0},{2,1},{3,2},{4,7},{5,4},{6,5},{7,6},{8,11},{9,8},{10,9... | collective-permute-start | bytes 1572872 | tf_op jit(solution)/shard_map/down_one/ppermute | solution.py:184
  61.4 2.2 %up.1 = (bf16[256,1024]{1,0:T(8,128)(2,1)}, bf16[256,1024]{1,0:T(8,128)(2,1)}, bf16[128,1024]{1,0:T(8,128)(2,1)S(1)}, bf16[128,1024]{1,0:T(8,128)(2,1)S(1)}, bf16[256,1024]{1,0:T(8,128)(2,1)S(1)}) custom-call(bf16[576,1024]{1,0:T(8,128)(2,1)S(1)} %get-tuple-element.26.xs, bf16[576,1024]{1,0:T(8,128)(2,1)S(1)} %get-tuple-element.27.dh), custom_call_target="tpu_custom_call" | custom-call | tf_op jit(solution)/shard_map/up/pallas_call | solution.py:165
  63.9 3.0 %collective-permute-start.3 = (bf16[256,1024]{1,0:T(8,128)(2,1)}, bf16[256,1024]{1,0:T(8,128)(2,1)}, u32[]{:S(2)}, u32[]{:S(2)}) collective-permute-start(bf16[256,1024]{1,0:T(8,128)(2,1)} %get-tuple-element.31), channel_id=1, source_target_pairs={{0,3},{1,0},{2,1},{3,2},{4,7},{5,4},{6,5},{7,6},{8,11},{9,8},{10,9... | collective-permute-start | bytes 1572872 | tf_op jit(solution)/shard_map/up_one/ppermute | solution.py:184
  66.9 1.0 %add_convert_fusion = bf16[32,10,8,128]{3,2,1,0:T(8,128)(2,1)} fusion(bf16[32,10,8,128]{3,2,1,0:T(8,128)(2,1)S(1)} %collective-permute-done.5, bf16[32,10,8,128]{3,2,1,0:T(8,128)(2,1)S(1)} %get-tuple-element.32), kind=kLoop, calls=%fused_computation | loop fusion | flops 1310720 | bytes 1966080 | tf_op jit(solution)/shard_map/convert_element_type | solution.py:268
  67.9 4.8 %all-to-all-start.1 = ((bf16[32,10,8,128]{3,2,1,0:T(8,128)(2,1)}), bf16[32,10,8,128]{3,2,1,0:T(8,128)(2,1)S(1)}, u32[]{:S(2)}, u32[]{:S(2)}) async-start(bf16[32,10,8,128]{3,2,1,0:T(8,128)(2,1)} %add_convert_fusion), calls=%async_computation.1 | async-start | bytes 1310720 | tf_op jit(solution)/shard_map/rows_back/all_to_all | solution.py:270
  72.7 1.7 %collective-permute-done.7 = bf16[256,1024]{1,0:T(8,128)(2,1)} collective-permute-done((bf16[256,1024]{1,0:T(8,128)(2,1)}, bf16[256,1024]{1,0:T(8,128)(2,1)}, u32[]{:S(2)}, u32[]{:S(2)}) %collective-permute-start.7) | collective-permute-done | bytes 524320 | tf_op jit(solution)/shard_map/down_one/ppermute | solution.py:184
  74.4 1.0 %add_convert_fusion.6 = bf16[128,1024]{1,0:T(8,128)(2,1)S(1)} fusion(bf16[128,1024]{1,0:T(8,128)(2,1)S(1)} %get-tuple-element.43, bf16[256,1024]{1,0:T(8,128)(2,1)} %collective-permute-done.7), kind=kLoop, calls=%fused_computation.9 | loop fusion | flops 524288 | bytes 786432 | tf_op jit(solution)/shard_map/convert_element_type | solution.py:189
  75.4 0.4 collective-permute-start.8
  75.8 1.0 %add_convert_fusion.5 = bf16[128,1024]{1,0:T(8,128)(2,1)S(1)} fusion(bf16[128,1024]{1,0:T(8,128)(2,1)S(1)} %get-tuple-element.44, bf16[256,1024]{1,0:T(8,128)(2,1)} %collective-permute-done.6), kind=kLoop, calls=%fused_computation.8 | loop fusion | flops 524288 | bytes 786432 | tf_op jit(solution)/shard_map/convert_element_type | solution.py:190
  76.8 3.0 %collective-permute-start.9 = (bf16[128,1024]{1,0:T(8,128)(2,1)S(1)}, bf16[128,1024]{1,0:T(8,128)(2,1)S(1)}, u32[]{:S(2)}, u32[]{:S(2)}) collective-permute-start(bf16[128,1024]{1,0:T(8,128)(2,1)S(1)} %add_convert_fusion.5), channel_id=1, source_target_pairs={{0,3},{1,0},{2,1},{3,2},{4,7},{5,4},{6,5},{7,6},{8,11},{9,8},{10,9... | collective-permute-start | bytes 786440 | tf_op jit(solution)/shard_map/down_two/ppermute | solution.py:184
  79.8 6.0 %collective-permute-done.3 = bf16[256,1024]{1,0:T(8,128)(2,1)} collective-permute-done((bf16[256,1024]{1,0:T(8,128)(2,1)}, bf16[256,1024]{1,0:T(8,128)(2,1)}, u32[]{:S(2)}, u32[]{:S(2)}) %collective-permute-start.3) | collective-permute-done | bytes 524320 | tf_op jit(solution)/shard_map/up_one/ppermute | solution.py:184
  85.8 1.0 %add_convert_fusion.7 = bf16[128,1024]{1,0:T(8,128)(2,1)S(1)} fusion(bf16[128,1024]{1,0:T(8,128)(2,1)S(1)} %get-tuple-element.30, bf16[256,1024]{1,0:T(8,128)(2,1)} %collective-permute-done.3), kind=kLoop, calls=%fused_computation.10 | loop fusion | flops 524288 | bytes 786432 | tf_op jit(solution)/shard_map/convert_element_type | solution.py:190
  86.8 3.0 %collective-permute-start.4 = (bf16[128,1024]{1,0:T(8,128)(2,1)S(1)}, bf16[128,1024]{1,0:T(8,128)(2,1)S(1)}, u32[]{:S(2)}, u32[]{:S(2)}) collective-permute-start(bf16[128,1024]{1,0:T(8,128)(2,1)S(1)} %add_convert_fusion.7), channel_id=1, source_target_pairs={{0,3},{1,0},{2,1},{3,2},{4,7},{5,4},{6,5},{7,6},{8,11},{9,8},{10,9... | collective-permute-start | bytes 786440 | tf_op jit(solution)/shard_map/up_two/ppermute | solution.py:184
  89.9 1.0 %add_convert_fusion.8 = bf16[128,1024]{1,0:T(8,128)(2,1)S(1)} fusion(bf16[128,1024]{1,0:T(8,128)(2,1)S(1)} %get-tuple-element.28, bf16[256,1024]{1,0:T(8,128)(2,1)} %collective-permute-done.1), kind=kLoop, calls=%fused_computation.11 | loop fusion | flops 524288 | bytes 786432 | tf_op jit(solution)/shard_map/convert_element_type | solution.py:189
  91.0 2.3 %add_convert_fusion.3 = (bf16[256,1024]{1,0:T(8,128)(2,1)S(1)}, bf16[256,1024]{1,0:T(8,128)(2,1)S(1)}) fusion(bf16[256,1024]{1,0:T(8,128)(2,1)S(1)} %get-tuple-element.40, bf16[256,1024]{1,0:T(8,128)(2,1)} %collective-permute-done.6, bf16[256,1024]{1,0:T(8,128)(2,1)} %collective-permute-done.7, pred[256]{0:T(512)(128)(4,1)S(1)} %iota_compare_fusion, ...), kind=kLoop, calls=%fused_computation.3 | loop fusion | flops 2621440 | bytes 4194560 | tf_op jit(solution)/shard_map/convert_element_type | solution.py:197
  93.4 1.1 %add_convert_fusion.2 = bf16[256,1024]{1,0:T(8,128)(2,1)} fusion(bf16[256,1024]{1,0:T(8,128)(2,1)S(1)} %get-tuple-element.48, pred[256]{0:T(512)(128)(4,1)S(1)} %broadcast_bitcast_fusion, bf16[128,1024]{1,0:T(8,128)(2,1)S(1)} %collective-permute-done.9, bf16[128,1024]{1,0:T(8,128)(2,1)S(1)} %collective-permute-done.8), kind=kLoop, calls=%fused_computation.2 | loop fusion | flops 1310720 | bytes 1573120 | tf_op jit(solution)/shard_map/convert_element_type | solution.py:205
  94.5 1.3 %unpack.1 = (bf16[256,1024]{1,0:T(8,128)(2,1)}, bf16[256]{0:T(256)(128)(2,1)}) custom-call(bf16[32,10,8,128]{3,2,1,0:T(8,128)(2,1)S(1)} %all-to-all-done.1.back_ref, bf16[256]{0:T(256)(128)(2,1)S(1)} %copy-done.4, s32[256]{0:T(256)S(1)} %copy-done.2, s32[256]{0:T(256)S(1)} %copy-done.3), custom_call_target="tpu_custom_call" | custom-call | tf_op jit(solution)/shard_map/unpack/pallas_call | solution.py:165
  96.0 2.5 %collective-permute-done.2 = bf16[128,1024]{1,0:T(8,128)(2,1)S(1)} collective-permute-done((bf16[128,1024]{1,0:T(8,128)(2,1)S(1)}, bf16[128,1024]{1,0:T(8,128)(2,1)S(1)}, u32[]{:S(2)}, u32[]{:S(2)}) %collective-permute-start.2) | collective-permute-done | bytes 262176 | tf_op jit(solution)/shard_map/up_two/ppermute | solution.py:184
  98.5 1.1 %fusion = bf16[1,256,1024]{2,1,0:T(8,128)(2,1)} fusion(bf16[256,1024]{1,0:T(8,128)(2,1)S(1)} %get-tuple-element.49, pred[256]{0:T(512)(128)(4,1)S(1)} %broadcast_bitcast_fusion, bf16[128,1024]{1,0:T(8,128)(2,1)S(1)} %collective-permute-done.4, bf16[128,1024]{1,0:T(8,128)(2,1)S(1)} %collective-permute-done.2), kind=kLoop, calls=%fused_computation.5 | loop fusion | flops 1310720 | bytes 1573120 | tf_op jit(solution)/shard_map/convert_element_type | solution.py:205
  (24 shorter events, 0.9 us)
Async XLA Ops:
  0.6 49.4 %copy-start.1 = (bf16[1,1024,1024]{2,1,0:T(8,128)(2,1)S(1)}, bf16[1,1024,1024]{2,1,0:T(8,128)(2,1)}, u32[]{:S(2)}) copy-start(bf16[1,1024,1024]{2,1,0:T(8,128)(2,1)} %down_ref.1) | copy-start | bytes 6291460
  3.6 46.5 %copy-start = (bf16[1,1024,1024]{2,1,0:T(8,128)(2,1)S(1)}, bf16[1,1024,1024]{2,1,0:T(8,128)(2,1)}, u32[]{:S(2)}) copy-start(bf16[1,1024,1024]{2,1,0:T(8,128)(2,1)} %up_ref.1) | copy-start | bytes 6291460
  47.2 2.8 %collective-permute-start = (bf16[32,18,8,128]{3,2,1,0:T(8,128)(2,1)S(1)}, bf16[32,18,8,128]{3,2,1,0:T(8,128)(2,1)S(1)}, u32[]{:S(2)}, u32[]{:S(2)}) collective-permute-start(bf16[32,18,8,128]{3,2,1,0:T(8,128)(2,1)S(1)} %all_to_all.10.mine_ref), channel_id=1, source_target_pairs={{0,4},{4,0},{1,5},{5,1},{2,6},{6,2},{3,7},{7,3},{8,12},{12,8},{9,1... | collective-permute-start | bytes 3538952 | tf_op jit(solution)/shard_map/ppermute | solution.py:231
  57.9 9.0 %collective-permute-start.5 = (bf16[32,10,8,128]{3,2,1,0:T(8,128)(2,1)S(1)}, bf16[32,10,8,128]{3,2,1,0:T(8,128)(2,1)S(1)}, u32[]{:S(2)}, u32[]{:S(2)}) collective-permute-start(bf16[32,10,8,128]{3,2,1,0:T(8,128)(2,1)S(1)} %get-tuple-element.33), channel_id=1, source_target_pairs={{0,4},{4,0},{1,5},{5,1},{2,6},{6,2},{3,7},{7,3},{8,12},{12,8},{9,1... | collective-permute-start | bytes 1966088 | tf_op jit(solution)/shard_map/swap_back/ppermute | solution.py:263
  58.1 16.3 %collective-permute-start.7 = (bf16[256,1024]{1,0:T(8,128)(2,1)}, bf16[256,1024]{1,0:T(8,128)(2,1)}, u32[]{:S(2)}, u32[]{:S(2)}) collective-permute-start(bf16[256,1024]{1,0:T(8,128)(2,1)} %get-tuple-element.42), channel_id=1, source_target_pairs={{0,1},{1,2},{2,3},{3,0},{4,5},{5,6},{6,7},{7,4},{8,9},{9,10},{10,1... | collective-permute-start | bytes 1572872 | tf_op jit(solution)/shard_map/down_one/ppermute | solution.py:184
  59.7 16.1 %collective-permute-start.6 = (bf16[256,1024]{1,0:T(8,128)(2,1)S(1)}, bf16[256,1024]{1,0:T(8,128)(2,1)}, u32[]{:S(2)}, u32[]{:S(2)}) collective-permute-start(bf16[256,1024]{1,0:T(8,128)(2,1)S(1)} %get-tuple-element.41), channel_id=1, source_target_pairs={{0,3},{1,0},{2,1},{3,2},{4,7},{5,4},{6,5},{7,6},{8,11},{9,8},{10,9... | collective-permute-start | bytes 1572872 | tf_op jit(solution)/shard_map/down_one/ppermute | solution.py:184
  63.6 26.2 %collective-permute-start.1 = (bf16[256,1024]{1,0:T(8,128)(2,1)}, bf16[256,1024]{1,0:T(8,128)(2,1)}, u32[]{:S(2)}, u32[]{:S(2)}) collective-permute-start(bf16[256,1024]{1,0:T(8,128)(2,1)} %get-tuple-element.29), channel_id=1, source_target_pairs={{0,1},{1,2},{2,3},{3,0},{4,5},{5,6},{6,7},{7,4},{8,9},{9,10},{10,1... | collective-permute-start | bytes 1572872 | tf_op jit(solution)/shard_map/up_one/ppermute | solution.py:184
  63.9 21.9 %collective-permute-start.3 = (bf16[256,1024]{1,0:T(8,128)(2,1)}, bf16[256,1024]{1,0:T(8,128)(2,1)}, u32[]{:S(2)}, u32[]{:S(2)}) collective-permute-start(bf16[256,1024]{1,0:T(8,128)(2,1)} %get-tuple-element.31), channel_id=1, source_target_pairs={{0,3},{1,0},{2,1},{3,2},{4,7},{5,4},{6,5},{7,6},{8,11},{9,8},{10,9... | collective-permute-start | bytes 1572872 | tf_op jit(solution)/shard_map/up_one/ppermute | solution.py:184
  67.9 26.6 %all-to-all-start.1 = ((bf16[32,10,8,128]{3,2,1,0:T(8,128)(2,1)}), bf16[32,10,8,128]{3,2,1,0:T(8,128)(2,1)S(1)}, u32[]{:S(2)}, u32[]{:S(2)}) async-start(bf16[32,10,8,128]{3,2,1,0:T(8,128)(2,1)} %add_convert_fusion), calls=%async_computation.1 | async-start | bytes 1310720 | tf_op jit(solution)/shard_map/rows_back/all_to_all | solution.py:270
  75.4 17.9 %collective-permute-start.8 = (bf16[128,1024]{1,0:T(8,128)(2,1)S(1)}, bf16[128,1024]{1,0:T(8,128)(2,1)S(1)}, u32[]{:S(2)}, u32[]{:S(2)}) collective-permute-start(bf16[128,1024]{1,0:T(8,128)(2,1)S(1)} %add_convert_fusion.6), channel_id=1, source_target_pairs={{0,1},{1,2},{2,3},{3,0},{4,5},{5,6},{6,7},{7,4},{8,9},{9,10},{10,1... | collective-permute-start | bytes 786440 | tf_op jit(solution)/shard_map/down_two/ppermute | solution.py:184
  76.8 16.6 %collective-permute-start.9 = (bf16[128,1024]{1,0:T(8,128)(2,1)S(1)}, bf16[128,1024]{1,0:T(8,128)(2,1)S(1)}, u32[]{:S(2)}, u32[]{:S(2)}) collective-permute-start(bf16[128,1024]{1,0:T(8,128)(2,1)S(1)} %add_convert_fusion.5), channel_id=1, source_target_pairs={{0,3},{1,0},{2,1},{3,2},{4,7},{5,4},{6,5},{7,6},{8,11},{9,8},{10,9... | collective-permute-start | bytes 786440 | tf_op jit(solution)/shard_map/down_two/ppermute | solution.py:184
  86.8 9.2 %collective-permute-start.4 = (bf16[128,1024]{1,0:T(8,128)(2,1)S(1)}, bf16[128,1024]{1,0:T(8,128)(2,1)S(1)}, u32[]{:S(2)}, u32[]{:S(2)}) collective-permute-start(bf16[128,1024]{1,0:T(8,128)(2,1)S(1)} %add_convert_fusion.7), channel_id=1, source_target_pairs={{0,3},{1,0},{2,1},{3,2},{4,7},{5,4},{6,5},{7,6},{8,11},{9,8},{10,9... | collective-permute-start | bytes 786440 | tf_op jit(solution)/shard_map/up_two/ppermute | solution.py:184
  90.9 7.7 %collective-permute-start.2 = (bf16[128,1024]{1,0:T(8,128)(2,1)S(1)}, bf16[128,1024]{1,0:T(8,128)(2,1)S(1)}, u32[]{:S(2)}, u32[]{:S(2)}) collective-permute-start(bf16[128,1024]{1,0:T(8,128)(2,1)S(1)} %add_convert_fusion.8), channel_id=1, source_target_pairs={{0,1},{1,2},{2,3},{3,0},{4,5},{5,6},{6,7},{7,4},{8,9},{9,10},{10,1... | collective-permute-start | bytes 786440 | tf_op jit(solution)/shard_map/up_two/ppermute | solution.py:184
  93.3 1.2 %copy-start.2 = (s32[256]{0:T(256)S(1)}, s32[256]{0:T(256)}, u32[]{:S(2)}) copy-start(s32[256]{0:T(256)} %expert_ref.3) | copy-start | bytes 3076
  93.3 1.2 %copy-start.3 = (s32[256]{0:T(256)S(1)}, s32[256]{0:T(256)}, u32[]{:S(2)}) copy-start(s32[256]{0:T(256)} %slot_ref.3) | copy-start | bytes 3076
  93.3 1.2 %copy-start.4 = (bf16[256]{0:T(256)(128)(2,1)S(1)}, bf16[256]{0:T(256)(128)(2,1)}, u32[]{:S(2)}) copy-start(bf16[256]{0:T(256)(128)(2,1)} %gate_ref.3) | copy-start | bytes 1540

commit v11 on v7

--- a/solution.py
+++ b/solution.py
@@ -9,7 +9,7 @@
 
 BF = jnp.bfloat16
 F32 = jnp.float32
-VMEM = 56 * 1024 * 1024
+MIB = 1024 * 1024
 LANES = 128
 
 
@@ -157,7 +157,7 @@
     gate_out_ref[...] = (total / gate).astype(BF).reshape(count)
 
 
-def call(kernel, out, scratch, *args):
+def call(kernel, room, out, scratch, *args):
     whole = pl.BlockSpec(memory_space=pltpu.VMEM)
     return pl.pallas_call(
         kernel,
@@ -165,7 +165,7 @@
         in_specs=[whole] * len(args),
         out_specs=jax.tree.map(lambda _: whole, out),
         scratch_shapes=scratch,
-        compiler_params=pltpu.CompilerParams(vmem_limit_bytes=VMEM),
+        compiler_params=pltpu.CompilerParams(vmem_limit_bytes=room * MIB),
     )(*args)
 
 
@@ -215,6 +215,7 @@
     swap = [(0, 1), (1, 0)]
     sent = call(
         pack_kernel,
+        56,
         shape(groups, 18, 8, LANES),
         [pltpu.VMEM((rows, width), F32), turn],
         tokens_in,
@@ -239,6 +240,7 @@
     with jax.named_scope("all"):
       keep, give, *both_parts = call(
         expert_kernel,
+        28,
         (shape(groups, 10, 8, LANES), shape(groups, 10, 8, LANES)) + parts(hidden, width) + parts(width, hidden),
         [pltpu.VMEM((2 * rows, width), BF), pltpu.VMEM((2 * rows, hidden), BF), pltpu.VMEM((2 * rows, LANES), F32), pltpu.VMEM((2 * rows, width), BF),
             pltpu.VMEM((2 * rows, hidden), BF),
@@ -271,6 +273,7 @@
     with jax.named_scope("unpack"):
       in_grad, gate_grad = call(
           unpack_kernel,
+          8,
           (shape(count, width), shape(count)),
           [pltpu.VMEM((rows, width), BF), turn],
           back,

time: 107 us -> 103 us (0.963)
  Pallas kernels: 18.7 us -> 14 us
  other arithmetic: 7.3 us -> 10.7 us
  local copies, waits for them, and re-layouts: 1.99 us -> 0.1 us
    pallas_call x3, Pallas kernels: 18.7 us -> 14 us  [call(): pl.pallas_call(kernel, out_shape=out, in_specs=[whole] * len(args), out_s...]
    convert_element_type x2, other arithmetic: 0.13 us -> 2.03 us  [second(): bwd = (parts[3].astype(F32) + right[half:].astype(F32)).astype(BF)]
    unnamed x18 -> x10, local copies, waits for them, and re-layouts: 1.91 us -> 0.03 us
    convert_element_type x1, other arithmetic: 0.84 us -> 2.34 us  [early(): return lax.optimization_barrier(begun.astype(BF))]
    convert_element_type x2, other arithmetic: 0.84 us -> 2.03 us  [second(): fwd = (parts[2].astype(F32) + left[:half].astype(F32)).astype(BF)]
    convert_element_type x1, other arithmetic: 2.17 us -> 1.02 us  [on_device(): both = (keep.astype(F32) + got.astype(F32)).astype(BF)]
  transfers between devices with their start and end apart: 11 -> 11, of which waited for: 6 -> 5; matrix products, arithmetic and copies ran while one was open for 5% -> 8% of each run, Pallas kernels for 2% -> 1%
where the time goes in v11:
time: 103 us
  blocking collectives  43.6 us (42%)
  starting transfers between devices  17.9 us (17%)
  waiting for transfers between devices  15.7 us (15%)
  Pallas kernels  14 us (14%)
  other arithmetic  10.7 us (10%)
    all_to_all x1, blocking collectives, on_device(): mine = lax.all_to_all(sent, 'chip', split_axis=0, concat_axis=0, tiled=True)  43.6 us
    pallas_call x3, Pallas kernels, call(): pl.pallas_call(kernel, out_shape=out, in_specs=[whole] * len(args), out_s...  14 us
    ppermute x8, starting transfers between devices, ring(): return (lax.ppermute(fwd, 'dp', AHEAD), lax.ppermute(bwd, 'dp', BEHIND))  13 us
    ppermute x8, waiting for transfers between devices, ring(): return (lax.ppermute(fwd, 'dp', AHEAD), lax.ppermute(bwd, 'dp', BEHIND))  12.9 us
    all_to_all x1, starting transfers between devices, on_device(): back = lax.all_to_all(both, 'chip', split_axis=0, concat_axis=0, tiled=True)  4.79 us
    convert_element_type x2, other arithmetic, total(): (begun.reshape(2, half, columns).astype(F32) + then).astype(BF)  3.23 us
    ppermute x1, waiting for transfers between devices, on_device(): other = lax.ppermute(mine, 'core', swap)  2.84 us
    convert_element_type x1, other arithmetic, early(): return lax.optimization_barrier(begun.astype(BF))  2.34 us
  transfers between devices with their start and end apart: 11, of which 5 were waited for; matrix products, arithmetic and copies ran while one was open for 8% of the time, Pallas kernels for 1%

profile of v11, /device:TPU:32, one launch (start us, length us, event | category | flops | bytes accessed | tf_op | source)
XLA Modules:
  0.0 102.7 jit_solution(18146956840685912123)
XLA Ops:
  0.6 3.0 %shard_map.102 = bf16[32,18,8,128]{3,2,1,0:T(8,128)(2,1)} custom-call(bf16[256,1024]{1,0:T(8,128)(2,1)} %x_ref.1, bf16[256,1024]{1,0:T(8,128)(2,1)} %g_ref.1, bf16[256]{0:T(256)(128)(2,1)} %gate_ref.3, s32[256]{0:T(256)} %expert_ref.3, s32[256]{0:T(256)} %slot_ref.3), custom_call_target="tpu_custom_call" | custom-call | tf_op jit(solution)/shard_map/pallas_call | solution.py:162
  3.6 43.6 %all_to_all.10.mine_ref = bf16[32,18,8,128]{3,2,1,0:T(8,128)(2,1)S(1)} all-to-all(bf16[32,18,8,128]{3,2,1,0:T(8,128)(2,1)} %shard_map.102), channel_id=1, replica_groups=mesh['chip'=32,'core'=2,'dp'=4] {'chip'}, dimensions={0} | all-to-all | bytes 2359296 | tf_op jit(solution)/shard_map/all_to_all | solution.py:227
  47.2 2.8 %collective-permute-done.other_ref = bf16[32,18,8,128]{3,2,1,0:T(8,128)(2,1)S(1)} collective-permute-done((bf16[32,18,8,128]{3,2,1,0:T(8,128)(2,1)S(1)}, bf16[32,18,8,128]{3,2,1,0:T(8,128)(2,1)S(1)}, u32[]{:S(2)}, u32[]{:S(2)}) %collective-permute-start) | collective-permute-done | bytes 1179680 | tf_op jit(solution)/shard_map/ppermute | solution.py:228
  50.1 9.7 %all.1 = (bf16[32,10,8,128]{3,2,1,0:T(8,128)(2,1)S(1)}, bf16[32,10,8,128]{3,2,1,0:T(8,128)(2,1)S(1)}, bf16[256,1024]{1,0:T(8,128)(2,1)}, bf16[256,1024]{1,0:T(8,...) custom-call(bf16[32,18,8,128]{3,2,1,0:T(8,128)(2,1)S(1)} %all_to_all, ...), custom_call_target="tpu_custom_call" | custom-call | tf_op jit(solution)/shard_map/all/pallas_call | solution.py:162
  59.9 1.5 %collective-permute-start.7 = (bf16[256,1024]{1,0:T(8,128)(2,1)}, bf16[256,1024]{1,0:T(8,128)(2,1)}, u32[]{:S(2)}, u32[]{:S(2)}) collective-permute-start(bf16[256,1024]{1,0:T(8,128)(2,1)} %get-tuple-element.38), channel_id=1, source_target_pairs={{0,1},{1,2},{2,3},{3,0},{4,5},{5,6},{6,7},{7,4},{8,9},{9,10},{10,1... | collective-permute-start | bytes 1572872 | tf_op jit(solution)/shard_map/down_one/ppermute | solution.py:181
  61.5 1.7 %collective-permute-start.6 = (bf16[256,1024]{1,0:T(8,128)(2,1)}, bf16[256,1024]{1,0:T(8,128)(2,1)}, u32[]{:S(2)}, u32[]{:S(2)}) collective-permute-start(bf16[256,1024]{1,0:T(8,128)(2,1)} %get-tuple-element.37), channel_id=1, source_target_pairs={{0,3},{1,0},{2,1},{3,2},{4,7},{5,4},{6,5},{7,6},{8,11},{9,8},{10,9... | collective-permute-start | bytes 1572872 | tf_op jit(solution)/shard_map/down_one/ppermute | solution.py:181
  63.2 0.3 collective-permute-start.1
  63.5 3.0 %collective-permute-start.3 = (bf16[256,1024]{1,0:T(8,128)(2,1)}, bf16[256,1024]{1,0:T(8,128)(2,1)}, u32[]{:S(2)}, u32[]{:S(2)}) collective-permute-start(bf16[256,1024]{1,0:T(8,128)(2,1)} %get-tuple-element.27), channel_id=1, source_target_pairs={{0,3},{1,0},{2,1},{3,2},{4,7},{5,4},{6,5},{7,6},{8,11},{9,8},{10,9... | collective-permute-start | bytes 1572872 | tf_op jit(solution)/shard_map/up_one/ppermute | solution.py:181
  66.5 1.0 add_convert_fusion
  67.5 4.8 %all-to-all-start.1 = ((bf16[32,10,8,128]{3,2,1,0:T(8,128)(2,1)}), bf16[32,10,8,128]{3,2,1,0:T(8,128)(2,1)S(1)}, u32[]{:S(2)}, u32[]{:S(2)}) async-start(bf16[32,10,8,128]{3,2,1,0:T(8,128)(2,1)} %add_convert_fusion), calls=%async_computation.1 | async-start | bytes 1310720 | tf_op jit(solution)/shard_map/rows_back/all_to_all | solution.py:265
  72.3 3.9 %collective-permute-done.7 = bf16[256,1024]{1,0:T(8,128)(2,1)} collective-permute-done((bf16[256,1024]{1,0:T(8,128)(2,1)}, bf16[256,1024]{1,0:T(8,128)(2,1)}, u32[]{:S(2)}, u32[]{:S(2)}) %collective-permute-start.7) | collective-permute-done | bytes 524320 | tf_op jit(solution)/shard_map/down_one/ppermute | solution.py:181
  76.2 1.0 add_convert_fusion.6
  77.2 0.4 collective-permute-start.8
  77.6 1.0 add_convert_fusion.5
  78.6 3.0 %collective-permute-start.9 = (bf16[128,1024]{1,0:T(8,128)(2,1)S(1)}, bf16[128,1024]{1,0:T(8,128)(2,1)S(1)}, u32[]{:S(2)}, u32[]{:S(2)}) collective-permute-start(bf16[128,1024]{1,0:T(8,128)(2,1)S(1)} %add_convert_fusion.5), channel_id=1, source_target_pairs={{0,3},{1,0},{2,1},{3,2},{4,7},{5,4},{6,5},{7,6},{8,11},{9,8},{10,9... | collective-permute-start | bytes 786440 | tf_op jit(solution)/shard_map/down_two/ppermute | solution.py:181
  81.6 6.2 %collective-permute-done.3 = bf16[256,1024]{1,0:T(8,128)(2,1)} collective-permute-done((bf16[256,1024]{1,0:T(8,128)(2,1)}, bf16[256,1024]{1,0:T(8,128)(2,1)}, u32[]{:S(2)}, u32[]{:S(2)}) %collective-permute-start.3) | collective-permute-done | bytes 524320 | tf_op jit(solution)/shard_map/up_one/ppermute | solution.py:181
  87.8 1.0 add_convert_fusion.7
  88.8 3.0 %collective-permute-start.4 = (bf16[128,1024]{1,0:T(8,128)(2,1)S(1)}, bf16[128,1024]{1,0:T(8,128)(2,1)S(1)}, u32[]{:S(2)}, u32[]{:S(2)}) collective-permute-start(bf16[128,1024]{1,0:T(8,128)(2,1)S(1)} %add_convert_fusion.7), channel_id=1, source_target_pairs={{0,3},{1,0},{2,1},{3,2},{4,7},{5,4},{6,5},{7,6},{8,11},{9,8},{10,9... | collective-permute-start | bytes 786440 | tf_op jit(solution)/shard_map/up_two/ppermute | solution.py:181
  91.9 1.0 add_convert_fusion.8
  93.0 2.3 %add_convert_fusion.3 = (bf16[256,1024]{1,0:T(8,128)(2,1)S(1)}, bf16[256,1024]{1,0:T(8,128)(2,1)S(1)}) fusion(bf16[256,1024]{1,0:T(8,128)(2,1)S(1)} %get-tuple-element.36, bf16[256,1024]{1,0:T(8,128)(2,1)} %collective-permute-done.6, bf16[256,1024]{1,0:T(8,128)(2,1)} %collective-permute-done.7, pred[256]{0:T(512)(128)(4,1)S(1)} %iota_compare_fusion, ...), kind=kLoop, calls=%fused_computation.3 | loop fusion | flops 2621440 | bytes 4194560 | tf_op jit(solution)/shard_map/convert_element_type | solution.py:194
  95.4 1.1 %add_convert_fusion.2 = bf16[256,1024]{1,0:T(8,128)(2,1)} fusion(bf16[256,1024]{1,0:T(8,128)(2,1)S(1)} %get-tuple-element.44, pred[256]{0:T(512)(128)(4,1)S(1)} %broadcast_bitcast_fusion, bf16[128,1024]{1,0:T(8,128)(2,1)S(1)} %collective-permute-done.9, bf16[128,1024]{1,0:T(8,128)(2,1)S(1)} %collective-permute-done.8), kind=kLoop, calls=%fused_computation.2 | loop fusion | flops 1310720 | bytes 1573120 | tf_op jit(solution)/shard_map/convert_element_type | solution.py:202
  96.5 1.3 %unpack.1 = (bf16[256,1024]{1,0:T(8,128)(2,1)}, bf16[256]{0:T(256)(128)(2,1)}) custom-call(bf16[32,10,8,128]{3,2,1,0:T(8,128)(2,1)S(1)} %all-to-all-done.1.back_ref, bf16[256]{0:T(256)(128)(2,1)S(1)} %copy-done.4, s32[256]{0:T(256)S(1)} %copy-done.2, s32[256]{0:T(256)S(1)} %copy-done.3), custom_call_target="tpu_custom_call" | custom-call | tf_op jit(solution)/shard_map/unpack/pallas_call | solution.py:162
  98.1 2.6 %collective-permute-done.2 = bf16[128,1024]{1,0:T(8,128)(2,1)} collective-permute-done((bf16[128,1024]{1,0:T(8,128)(2,1)S(1)}, bf16[128,1024]{1,0:T(8,128)(2,1)}, u32[]{:S(2)}, u32[]{:S(2)}) %collective-permute-start.2) | collective-permute-done | bytes 262176 | tf_op jit(solution)/shard_map/up_two/ppermute | solution.py:181
  100.7 2.1 %fusion = bf16[1,256,1024]{2,1,0:T(8,128)(2,1)} fusion(bf16[256,1024]{1,0:T(8,128)(2,1)S(1)} %get-tuple-element.45, pred[256]{0:T(512)(128)(4,1)S(1)} %broadcast_bitcast_fusion, bf16[128,1024]{1,0:T(8,128)(2,1)S(1)} %collective-permute-done.4, bf16[128,1024]{1,0:T(8,128)(2,1)} %collective-permute-done.2), kind=kLoop, calls=%fused_computation.5 | loop fusion | flops 1310720 | bytes 1573120 | tf_op jit(solution)/shard_map/convert_element_type | solution.py:202
  (23 shorter events, 0.5 us)
Async XLA Ops:
  0.6 49.4 %copy-start.1 = (bf16[1,1024,1024]{2,1,0:T(8,128)(2,1)S(1)}, bf16[1,1024,1024]{2,1,0:T(8,128)(2,1)}, u32[]{:S(2)}) copy-start(bf16[1,1024,1024]{2,1,0:T(8,128)(2,1)} %down_ref.1) | copy-start | bytes 6291460
  3.6 46.5 %copy-start = (bf16[1,1024,1024]{2,1,0:T(8,128)(2,1)S(1)}, bf16[1,1024,1024]{2,1,0:T(8,128)(2,1)}, u32[]{:S(2)}) copy-start(bf16[1,1024,1024]{2,1,0:T(8,128)(2,1)} %up_ref.1) | copy-start | bytes 6291460
  47.2 2.8 %collective-permute-start = (bf16[32,18,8,128]{3,2,1,0:T(8,128)(2,1)S(1)}, bf16[32,18,8,128]{3,2,1,0:T(8,128)(2,1)S(1)}, u32[]{:S(2)}, u32[]{:S(2)}) collective-permute-start(bf16[32,18,8,128]{3,2,1,0:T(8,128)(2,1)S(1)} %all_to_all.10.mine_ref), channel_id=1, source_target_pairs={{0,4},{4,0},{1,5},{5,1},{2,6},{6,2},{3,7},{7,3},{8,12},{12,8},{9,1... | collective-permute-start | bytes 3538952 | tf_op jit(solution)/shard_map/ppermute | solution.py:228
  59.8 6.7 %collective-permute-start.5 = (bf16[32,10,8,128]{3,2,1,0:T(8,128)(2,1)S(1)}, bf16[32,10,8,128]{3,2,1,0:T(8,128)(2,1)S(1)}, u32[]{:S(2)}, u32[]{:S(2)}) collective-permute-start(bf16[32,10,8,128]{3,2,1,0:T(8,128)(2,1)S(1)} %get-tuple-element.29), channel_id=1, source_target_pairs={{0,4},{4,0},{1,5},{5,1},{2,6},{6,2},{3,7},{7,3},{8,12},{12,8},{9,1... | collective-permute-start | bytes 1966088 | tf_op jit(solution)/shard_map/swap_back/ppermute | solution.py:260
  59.9 16.3 %collective-permute-start.7 = (bf16[256,1024]{1,0:T(8,128)(2,1)}, bf16[256,1024]{1,0:T(8,128)(2,1)}, u32[]{:S(2)}, u32[]{:S(2)}) collective-permute-start(bf16[256,1024]{1,0:T(8,128)(2,1)} %get-tuple-element.38), channel_id=1, source_target_pairs={{0,1},{1,2},{2,3},{3,0},{4,5},{5,6},{6,7},{7,4},{8,9},{9,10},{10,1... | collective-permute-start | bytes 1572872 | tf_op jit(solution)/shard_map/down_one/ppermute | solution.py:181
  61.5 16.1 %collective-permute-start.6 = (bf16[256,1024]{1,0:T(8,128)(2,1)}, bf16[256,1024]{1,0:T(8,128)(2,1)}, u32[]{:S(2)}, u32[]{:S(2)}) collective-permute-start(bf16[256,1024]{1,0:T(8,128)(2,1)} %get-tuple-element.37), channel_id=1, source_target_pairs={{0,3},{1,0},{2,1},{3,2},{4,7},{5,4},{6,5},{7,6},{8,11},{9,8},{10,9... | collective-permute-start | bytes 1572872 | tf_op jit(solution)/shard_map/down_one/ppermute | solution.py:181
  63.2 28.6 %collective-permute-start.1 = (bf16[256,1024]{1,0:T(8,128)(2,1)S(1)}, bf16[256,1024]{1,0:T(8,128)(2,1)}, u32[]{:S(2)}, u32[]{:S(2)}) collective-permute-start(bf16[256,1024]{1,0:T(8,128)(2,1)S(1)} %get-tuple-element.25), channel_id=1, source_target_pairs={{0,1},{1,2},{2,3},{3,0},{4,5},{5,6},{6,7},{7,4},{8,9},{9,10},{10,1... | collective-permute-start | bytes 1572872 | tf_op jit(solution)/shard_map/up_one/ppermute | solution.py:181
  63.5 24.3 %collective-permute-start.3 = (bf16[256,1024]{1,0:T(8,128)(2,1)}, bf16[256,1024]{1,0:T(8,128)(2,1)}, u32[]{:S(2)}, u32[]{:S(2)}) collective-permute-start(bf16[256,1024]{1,0:T(8,128)(2,1)} %get-tuple-element.27), channel_id=1, source_target_pairs={{0,3},{1,0},{2,1},{3,2},{4,7},{5,4},{6,5},{7,6},{8,11},{9,8},{10,9... | collective-permute-start | bytes 1572872 | tf_op jit(solution)/shard_map/up_one/ppermute | solution.py:181
  67.5 29.0 %all-to-all-start.1 = ((bf16[32,10,8,128]{3,2,1,0:T(8,128)(2,1)}), bf16[32,10,8,128]{3,2,1,0:T(8,128)(2,1)S(1)}, u32[]{:S(2)}, u32[]{:S(2)}) async-start(bf16[32,10,8,128]{3,2,1,0:T(8,128)(2,1)} %add_convert_fusion), calls=%async_computation.1 | async-start | bytes 1310720 | tf_op jit(solution)/shard_map/rows_back/all_to_all | solution.py:265
  77.2 18.2 %collective-permute-start.8 = (bf16[128,1024]{1,0:T(8,128)(2,1)S(1)}, bf16[128,1024]{1,0:T(8,128)(2,1)S(1)}, u32[]{:S(2)}, u32[]{:S(2)}) collective-permute-start(bf16[128,1024]{1,0:T(8,128)(2,1)S(1)} %add_convert_fusion.6), channel_id=1, source_target_pairs={{0,1},{1,2},{2,3},{3,0},{4,5},{5,6},{6,7},{7,4},{8,9},{9,10},{10,1... | collective-permute-start | bytes 786440 | tf_op jit(solution)/shard_map/down_two/ppermute | solution.py:181
  78.6 16.8 %collective-permute-start.9 = (bf16[128,1024]{1,0:T(8,128)(2,1)S(1)}, bf16[128,1024]{1,0:T(8,128)(2,1)S(1)}, u32[]{:S(2)}, u32[]{:S(2)}) collective-permute-start(bf16[128,1024]{1,0:T(8,128)(2,1)S(1)} %add_convert_fusion.5), channel_id=1, source_target_pairs={{0,3},{1,0},{2,1},{3,2},{4,7},{5,4},{6,5},{7,6},{8,11},{9,8},{10,9... | collective-permute-start | bytes 786440 | tf_op jit(solution)/shard_map/down_two/ppermute | solution.py:181
  88.8 9.2 %collective-permute-start.4 = (bf16[128,1024]{1,0:T(8,128)(2,1)S(1)}, bf16[128,1024]{1,0:T(8,128)(2,1)S(1)}, u32[]{:S(2)}, u32[]{:S(2)}) collective-permute-start(bf16[128,1024]{1,0:T(8,128)(2,1)S(1)} %add_convert_fusion.7), channel_id=1, source_target_pairs={{0,3},{1,0},{2,1},{3,2},{4,7},{5,4},{6,5},{7,6},{8,11},{9,8},{10,9... | collective-permute-start | bytes 786440 | tf_op jit(solution)/shard_map/up_two/ppermute | solution.py:181
  92.9 7.8 %collective-permute-start.2 = (bf16[128,1024]{1,0:T(8,128)(2,1)S(1)}, bf16[128,1024]{1,0:T(8,128)(2,1)}, u32[]{:S(2)}, u32[]{:S(2)}) collective-permute-start(bf16[128,1024]{1,0:T(8,128)(2,1)S(1)} %add_convert_fusion.8), channel_id=1, source_target_pairs={{0,1},{1,2},{2,3},{3,0},{4,5},{5,6},{6,7},{7,4},{8,9},{9,10},{10,1... | collective-permute-start | bytes 786440 | tf_op jit(solution)/shard_map/up_two/ppermute | solution.py:181
  95.3 1.2 %copy-start.2 = (s32[256]{0:T(256)S(1)}, s32[256]{0:T(256)}, u32[]{:S(2)}) copy-start(s32[256]{0:T(256)} %expert_ref.3) | copy-start | bytes 3076
  95.3 1.2 %copy-start.3 = (s32[256]{0:T(256)S(1)}, s32[256]{0:T(256)}, u32[]{:S(2)}) copy-start(s32[256]{0:T(256)} %slot_ref.3) | copy-start | bytes 3076
  95.4 1.2 %copy-start.4 = (bf16[256]{0:T(256)(128)(2,1)S(1)}, bf16[256]{0:T(256)(128)(2,1)}, u32[]{:S(2)}) copy-start(bf16[256]{0:T(256)(128)(2,1)} %gate_ref.3) | copy-start | bytes 1540
